TPU v7x, 32 devices: a whole 2x2x4 slice. The times are simulated.
32 devices in a mesh: fsdp: 8 (over y, x, core), seq: 4 (over z).
Axes of the slice: x: 2, y: 2, z: 4, core: 2. Of those that a mesh axis runs over, the one named last changes fastest.
Arguments:
- tokens: bfloat16 [16, 2048, 768], P('fsdp', 'seq'), may hold values from -6 to 6
- teacher: bfloat16 [16, 2048, 768], P('fsdp', 'seq'), may hold values from -6 to 6
- segment_ids: int32 [16, 2048], P('fsdp', 'seq'), may hold values from 0 to 3, as said below
- latent_flags: int32 [16, 2048], P('fsdp', 'seq'), may hold values from 0 to 1, as said below
- valid_mask: int32 [16, 2048], P('fsdp', 'seq'), may hold values from 0 to 1, as said below
- attngain: bfloat16 [768], P('fsdp'), may hold values from 0.5 to 1.5
- attnshift: bfloat16 [768], P('fsdp'), may hold values from -4 to 4
- qkvweight: bfloat16 [768, 2304], P('fsdp'), may hold values from -0.3125 to 0.3125
- qvbias: bfloat16 [1536], P('fsdp'), may hold values from -4 to 4
- outweight: bfloat16 [768, 768], P('fsdp'), may hold values from -0.875 to 0.875
- outbias: bfloat16 [768], P('fsdp'), may hold values from -4 to 4
- mlpgain: bfloat16 [768], P('fsdp'), may hold values from 0.5 to 1.5
- mlpshift: bfloat16 [768], P('fsdp'), may hold values from -4 to 4
- fcweight: bfloat16 [768, 3072], P('fsdp'), may hold values from -0.21875 to 0.21875
- fcbias: bfloat16 [3072], P('fsdp'), may hold values from -6 to 6
- projweight: bfloat16 [3072, 768], P('fsdp'), may hold values from -0.109375 to 0.109375
- projbias: bfloat16 [768], P('fsdp'), may hold values from -4 to 4
Outputs:
- distill_loss: float32 [], replicated
- layer_out: bfloat16 [16, 2048, 768], P('fsdp', 'seq')
- grad_tokens: bfloat16 [16, 2048, 768], P('fsdp', 'seq')
- grad_attngain: float32 [768], P('fsdp')
- grad_attnshift: float32 [768], P('fsdp')
- grad_qkvweight: float32 [768, 2304], P('fsdp')
- grad_qvbias: float32 [1536], P('fsdp')
- grad_outweight: float32 [768, 768], P('fsdp')
- grad_outbias: float32 [768], P('fsdp')
- grad_mlpgain: float32 [768], P('fsdp')
- grad_mlpshift: float32 [768], P('fsdp')
- grad_fcweight: float32 [768, 3072], P('fsdp')
- grad_fcbias: float32 [3072], P('fsdp')
- grad_projweight: float32 [3072, 768], P('fsdp')
- grad_projbias: float32 [768], P('fsdp')
Inputs may be any that keep to these rules, and one draw needn't show every extreme that they name: `segment_ids`: ids never fall along a sequence, start at 0, and every sequence holds four documents. `latent_flags`: the first token of every sequence is not latent. `valid_mask`: the first token of every sequence is valid.
All inputs are finite; a program needn't handle non-finite values.
Results may differ from a plain program's by a relative error of at most 0.012.
The roundings to bfloat16 on the way count: a program that leaves them out, or rounds other values in their place, can miss the bound.
Values may be sent and summed in bfloat16 or wider, within the bound.
No kernel may reach another device: no remote copies, remote signals or barrier semaphores. Data moves between devices by JAX's collectives and lax.ppermute only.
A program may use at most 256 MiB of HBM per device.

v0:
```python
import math

import jax
import jax.numpy as jnp
from jax import lax
from jax.sharding import PartitionSpec as P

H = 12
HD = 64


EPSILON = 1e-05


def for_sending(x):

    def short(part):
        return part.astype(jnp.bfloat16) if part.dtype == jnp.float32 else part

    return jax.tree.map(short, x)


def layer_norm(values, gain, shift):
    center = values - jnp.mean(values, -1, keepdims=True)
    spread = jnp.mean(center * center, -1, keepdims=True)
    return center * lax.rsqrt(spread + EPSILON) * gain + shift


def gelu_tanh(values):
    inner = 0.7978845608028654 * (values + 0.044715 * values * values * values)
    return 0.5 * values * (1.0 + jnp.tanh(inner))


def split_heads(joint_item):
    length = joint_item.shape[0]
    heads_local = joint_item.shape[-1] // HD
    query = joint_item[:, 0, 0].reshape(length, heads_local, HD)
    keys = joint_item[:, 1, 0].reshape(length, heads_local, HD)
    values = joint_item[:, 2, 0].reshape(length, heads_local, HD)
    return (query, keys, values)


def block_scores(query_block, keys, segments, start):
    block = query_block.shape[0]
    length = keys.shape[0]
    scale = 1.0 / math.sqrt(HD)
    scores = (
        jnp.einsum("qhd,khd->hqk", query_block, keys, preferred_element_type=jnp.float32) * scale
    )
    place = jnp.arange(length, dtype=jnp.int32)
    rows_here = place[start : start + block]
    allowed = (place[None, :] <= rows_here[:, None]) & (
        segments[start : start + block, None] == segments[None, :]
    )
    return jnp.where(allowed[None], scores, -1e30)


def attend_sequence(item):
    joint_item, segments = item
    query, keys, values = split_heads(joint_item)
    length = query.shape[0]
    block = min(512, length)
    mixed_blocks = []
    total_blocks = []
    for start in range(0, length, block):
        masked = block_scores(query[start : start + block], keys, segments, start)
        highest = jnp.max(masked, -1, keepdims=True)
        powers = jnp.exp(masked - highest)
        total = jnp.sum(powers, -1, keepdims=True)
        probs = powers / total
        mixed = jnp.einsum(
            "hqk,khd->qhd", probs.astype(jnp.bfloat16), values, preferred_element_type=jnp.float32
        )
        mixed_blocks.append(mixed.reshape(block, -1).astype(jnp.bfloat16))
        total_blocks.append((highest + jnp.log(total))[:, :, 0])
    return (jnp.concatenate(mixed_blocks, 0), jnp.concatenate(total_blocks, 1))


def attend_items(pieces):
    joint_piece, segment_piece = pieces
    segments = segment_piece[:, :, 0, 0, 0]
    mixed, log_total = lax.map(attend_sequence, (joint_piece, segments))
    return (mixed, log_total, joint_piece, segments)


def back_sequence(item):
    joint_item, segments, log_total, grad_mixed = item
    query, keys, values = split_heads(joint_item)
    length, heads_local, _ = query.shape
    grad_out = grad_mixed[:, 0].reshape(length, heads_local, HD)
    block = min(512, length)
    scale = 1.0 / math.sqrt(HD)
    grad_keys = jnp.zeros((length, heads_local, HD), jnp.float32)
    grad_values = jnp.zeros((length, heads_local, HD), jnp.float32)
    query_grads = []
    for start in range(0, length, block):
        query_block = query[start : start + block]
        grad_block = grad_out[start : start + block]
        masked = block_scores(query_block, keys, segments, start)
        probs = jnp.exp(masked - log_total[:, start : start + block, None])
        probs_low = probs.astype(jnp.bfloat16)
        grad_values = grad_values + jnp.einsum(
            "hqk,qhd->khd", probs_low, grad_block, preferred_element_type=jnp.float32
        )
        grad_probs = jnp.einsum(
            "qhd,khd->hqk", grad_block, values, preferred_element_type=jnp.float32
        )
        center = jnp.sum(probs * grad_probs, -1, keepdims=True)
        grad_scores = (probs * (grad_probs - center)).astype(jnp.bfloat16)
        query_grads.append(
            jnp.einsum("hqk,khd->qhd", grad_scores, keys, preferred_element_type=jnp.float32)
            * scale
        )
        grad_keys = (
            grad_keys
            + jnp.einsum(
                "hqk,qhd->khd", grad_scores, query_block, preferred_element_type=jnp.float32
            )
            * scale
        )
    grad_query = jnp.concatenate(query_grads, 0)
    stacked = jnp.stack([grad_query, grad_keys, grad_values], 1).astype(jnp.bfloat16)
    return stacked.reshape(length, 3, 1, heads_local * HD)


def local(
    tokens,
    teacher,
    segment_ids,
    latent_flags,
    valid_mask,
    attngain,
    attnshift,
    qkvweight,
    qvbias,
    outweight,
    outbias,
    mlpgain,
    mlpshift,
    fcweight,
    fcbias,
    projweight,
    projbias,
):
    seqs_local, block_len, width = tokens.shape
    groups = lax.axis_size("seq")
    heads_local = H // groups
    rows = seqs_local * block_len
    weight = (valid_mask * (1 - latent_flags)).astype(jnp.float32).reshape(rows)
    local_count = jnp.sum(weight)
    gathered = (
        lax.all_gather(attngain, "fsdp", axis=0, tiled=True),
        lax.all_gather(attnshift, "fsdp", axis=0, tiled=True),
        lax.all_gather(qkvweight, "fsdp", axis=0, tiled=True),
        lax.all_gather(qvbias, "fsdp", axis=0, tiled=True),
        lax.all_gather(outweight, "fsdp", axis=0, tiled=True),
        lax.all_gather(outbias, "fsdp", axis=0, tiled=True),
        lax.all_gather(mlpgain, "fsdp", axis=0, tiled=True),
        lax.all_gather(mlpshift, "fsdp", axis=0, tiled=True),
        lax.all_gather(fcweight, "fsdp", axis=0, tiled=True),
        lax.all_gather(fcbias, "fsdp", axis=0, tiled=True),
        lax.all_gather(projweight, "fsdp", axis=0, tiled=True),
        lax.all_gather(projbias, "fsdp", axis=0, tiled=True),
    )
    first_gain = gathered[0].astype(jnp.float32)
    first_shift = gathered[1].astype(jnp.float32)
    joint_weight = gathered[2]
    joint_bias = gathered[3].astype(jnp.float32)
    merge_weight = gathered[4]
    merge_bias = gathered[5].astype(jnp.float32)
    second_gain = gathered[6].astype(jnp.float32)
    second_shift = gathered[7].astype(jnp.float32)
    up_weight = gathered[8]
    up_bias = gathered[9].astype(jnp.float32)
    down_weight = gathered[10]
    down_bias = gathered[11].astype(jnp.float32)
    inputs = tokens.astype(jnp.float32).reshape(rows, width)
    normed, first_back = jax.vjp(layer_norm, inputs, first_gain, first_shift)
    normed_low = normed.astype(jnp.bfloat16)
    bias_full = jnp.concatenate(
        [joint_bias[:width], jnp.zeros((width,), jnp.float32), joint_bias[width:]]
    )
    joint = jnp.dot(normed_low, joint_weight, preferred_element_type=jnp.float32) + bias_full
    joint_low = joint.astype(jnp.bfloat16).reshape(
        seqs_local, block_len, 3, groups, heads_local * HD
    )
    segment_low = jnp.broadcast_to(
        segment_ids.astype(jnp.bfloat16)[:, :, None, None, None],
        (seqs_local, block_len, 1, groups, 1),
    )
    mixed, log_total, kept_joint, kept_segment = attend_items(
        (
            lax.all_to_all(joint_low, "seq", split_axis=3, concat_axis=1, tiled=True),
            lax.all_to_all(segment_low, "seq", split_axis=3, concat_axis=1, tiled=True),
        )
    )
    length = mixed.shape[1]
    mixed_back = lax.all_to_all(
        for_sending(mixed.reshape(seqs_local, length, 1, heads_local * HD)),
        "seq",
        split_axis=1,
        concat_axis=2,
        tiled=True,
    )
    attended = mixed_back.reshape(rows, width)
    branch = jnp.dot(attended, merge_weight, preferred_element_type=jnp.float32) + merge_bias
    resid = inputs + branch
    normed_two, second_back = jax.vjp(layer_norm, resid, second_gain, second_shift)
    normed_two_low = normed_two.astype(jnp.bfloat16)
    hidden = jnp.dot(normed_two_low, up_weight, preferred_element_type=jnp.float32) + up_bias
    active, gelu_back = jax.vjp(gelu_tanh, hidden)
    active_low = active.astype(jnp.bfloat16)
    result = (
        resid + jnp.dot(active_low, down_weight, preferred_element_type=jnp.float32) + down_bias
    )
    layer_out = result.astype(jnp.bfloat16).reshape(tokens.shape)
    error = result - teacher.astype(jnp.float32).reshape(rows, width)
    local_sum = jnp.sum(weight * jnp.sum(error * error, -1))
    total_sum, total_count = lax.psum((local_sum, local_count), ("fsdp", "seq"))
    distill_loss = total_sum / (width * total_count)
    token_total = rows * lax.axis_size("fsdp") * groups
    factor = token_total / total_count
    grad_result = error * (weight * factor)[:, None]
    back_params = (
        lax.all_gather(attngain, "fsdp", axis=0, tiled=True),
        lax.all_gather(attnshift, "fsdp", axis=0, tiled=True),
        lax.all_gather(qkvweight, "fsdp", axis=0, tiled=True),
        lax.all_gather(qvbias, "fsdp", axis=0, tiled=True),
        lax.all_gather(outweight, "fsdp", axis=0, tiled=True),
        lax.all_gather(outbias, "fsdp", axis=0, tiled=True),
        lax.all_gather(mlpgain, "fsdp", axis=0, tiled=True),
        lax.all_gather(mlpshift, "fsdp", axis=0, tiled=True),
        lax.all_gather(fcweight, "fsdp", axis=0, tiled=True),
        lax.all_gather(fcbias, "fsdp", axis=0, tiled=True),
        lax.all_gather(projweight, "fsdp", axis=0, tiled=True),
        lax.all_gather(projbias, "fsdp", axis=0, tiled=True),
    )
    joint_weight = back_params[2]
    merge_weight = back_params[4]
    up_weight = back_params[8]
    down_weight = back_params[10]
    grad_mlp = grad_result.astype(jnp.bfloat16)
    grad_downbias = jnp.sum(grad_mlp, 0, dtype=jnp.float32)
    grad_downweight = jnp.einsum(
        "rf,rd->fd", active_low, grad_mlp, preferred_element_type=jnp.float32
    )
    grad_active = jnp.einsum("rd,fd->rf", grad_mlp, down_weight, preferred_element_type=jnp.float32)
    grad_hidden = gelu_back(grad_active)[0].astype(jnp.bfloat16)
    grad_upbias = jnp.sum(grad_hidden, 0, dtype=jnp.float32)
    grad_upweight = jnp.einsum(
        "rd,rf->df", normed_two_low, grad_hidden, preferred_element_type=jnp.float32
    )
    grad_normed_two = jnp.einsum(
        "rf,df->rd", grad_hidden, up_weight, preferred_element_type=jnp.float32
    )
    resid_part, grad_secondgain, grad_secondshift = second_back(grad_normed_two)
    grad_resid = grad_result + resid_part
    grad_branch = grad_resid.astype(jnp.bfloat16)
    grad_mergebias = jnp.sum(grad_branch, 0, dtype=jnp.float32)
    grad_mergeweight = jnp.einsum(
        "rd,re->de", attended, grad_branch, preferred_element_type=jnp.float32
    )
    grad_attended = jnp.einsum(
        "re,de->rd", grad_branch, merge_weight, preferred_element_type=jnp.float32
    ).astype(jnp.bfloat16)
    grad_heads = lax.all_to_all(
        grad_attended.reshape(seqs_local, block_len, groups, heads_local * HD),
        "seq",
        split_axis=2,
        concat_axis=1,
        tiled=True,
    )
    grad_joint_heads = lax.map(back_sequence, (kept_joint, kept_segment, log_total, grad_heads))
    grad_joint = lax.all_to_all(
        grad_joint_heads, "seq", split_axis=1, concat_axis=3, tiled=True
    ).reshape(rows, 3 * width)
    grad_jointweight = jnp.einsum(
        "rd,re->de", normed_low, grad_joint, preferred_element_type=jnp.float32
    )
    column_sums = jnp.sum(grad_joint, 0, dtype=jnp.float32)
    grad_jointbias = jnp.concatenate([column_sums[:width], column_sums[2 * width :]])
    grad_normed = jnp.einsum(
        "re,de->rd", grad_joint, joint_weight, preferred_element_type=jnp.float32
    )
    input_part, grad_firstgain, grad_firstshift = first_back(grad_normed)
    grad_tokens = (grad_resid + input_part).astype(jnp.bfloat16).reshape(tokens.shape)
    shards = (
        lax.psum_scatter(grad_firstgain, "fsdp", scatter_dimension=0, tiled=True),
        lax.psum_scatter(grad_firstshift, "fsdp", scatter_dimension=0, tiled=True),
        lax.psum_scatter(grad_jointweight, "fsdp", scatter_dimension=0, tiled=True),
        lax.psum_scatter(grad_jointbias, "fsdp", scatter_dimension=0, tiled=True),
        lax.psum_scatter(grad_mergeweight, "fsdp", scatter_dimension=0, tiled=True),
        lax.psum_scatter(grad_mergebias, "fsdp", scatter_dimension=0, tiled=True),
        lax.psum_scatter(grad_secondgain, "fsdp", scatter_dimension=0, tiled=True),
        lax.psum_scatter(grad_secondshift, "fsdp", scatter_dimension=0, tiled=True),
        lax.psum_scatter(grad_upweight, "fsdp", scatter_dimension=0, tiled=True),
        lax.psum_scatter(grad_upbias, "fsdp", scatter_dimension=0, tiled=True),
        lax.psum_scatter(grad_downweight, "fsdp", scatter_dimension=0, tiled=True),
        lax.psum_scatter(grad_downbias, "fsdp", scatter_dimension=0, tiled=True),
    )
    summed = (
        lax.psum(shards[0].astype(jnp.bfloat16), "seq").astype(jnp.float32),
        lax.psum(shards[1].astype(jnp.bfloat16), "seq").astype(jnp.float32),
        lax.psum(shards[2].astype(jnp.bfloat16), "seq").astype(jnp.float32),
        lax.psum(shards[3].astype(jnp.bfloat16), "seq").astype(jnp.float32),
        lax.psum(shards[4].astype(jnp.bfloat16), "seq").astype(jnp.float32),
        lax.psum(shards[5].astype(jnp.bfloat16), "seq").astype(jnp.float32),
        lax.psum(shards[6].astype(jnp.bfloat16), "seq").astype(jnp.float32),
        lax.psum(shards[7].astype(jnp.bfloat16), "seq").astype(jnp.float32),
        lax.psum(shards[8].astype(jnp.bfloat16), "seq").astype(jnp.float32),
        lax.psum(shards[9].astype(jnp.bfloat16), "seq").astype(jnp.float32),
        lax.psum(shards[10].astype(jnp.bfloat16), "seq").astype(jnp.float32),
        lax.psum(shards[11].astype(jnp.bfloat16), "seq").astype(jnp.float32),
    )
    return (
        distill_loss,
        layer_out,
        grad_tokens,
        summed[0],
        summed[1],
        summed[2],
        summed[3],
        summed[4],
        summed[5],
        summed[6],
        summed[7],
        summed[8],
        summed[9],
        summed[10],
        summed[11],
    )


def solution(mesh):
    placed = (
        P("fsdp", "seq", None),
        P("fsdp", "seq", None),
        P("fsdp", "seq"),
        P("fsdp", "seq"),
        P("fsdp", "seq"),
        P("fsdp"),
        P("fsdp"),
        P("fsdp", None),
        P("fsdp"),
        P("fsdp", None),
        P("fsdp"),
        P("fsdp"),
        P("fsdp"),
        P("fsdp", None),
        P("fsdp"),
        P("fsdp", None),
        P("fsdp"),
    )
    return jax.shard_map(
        local,
        mesh=mesh,
        in_specs=placed,
        out_specs=(
            P(),
            P("fsdp", "seq", None),
            P("fsdp", "seq", None),
            P("fsdp"),
            P("fsdp"),
            P("fsdp", None),
            P("fsdp"),
            P("fsdp", None),
            P("fsdp"),
            P("fsdp"),
            P("fsdp"),
            P("fsdp", None),
            P("fsdp"),
            P("fsdp", None),
            P("fsdp"),
        ),
        check_vma=False,
    )
```

profile of v0, /device:TPU:0, one launch (start us, length us, event | category | flops | bytes accessed | tf_op | source)
XLA Modules:
  0.0 1246.0 jit_solution(2136501249223661194)
XLA Ops:
  19.6 26.6 %all-reduce.17 = (bf16[768]{0:T(1024)(128)(2,1)S(1)}, bf16[768]{0:T(1024)(128)(2,1)S(1)}, bf16[1536]{0:T(1024)(128)(2,1)S(1)}, bf16[768]{0:T(1024)(128)(2,1)}, b...) all-reduce(bf16[768]{0:T(1024)(128)(2,1)S(1)} %dynamic-update-slice, ...), channel_id=1, replica_groups=mesh['fsdp'=8,'seq'=4] {'fsdp'}, use_global_device_ids=true, to_apply=%add.1 | all-reduce | flops 6144 | bytes 24576
  57.7 12.8 %reshape.747 = bf16[2,512,3,4,192]{4,3,2,1,0:T(4,128)(2,1)} reshape(bf16[1024,2304]{1,0:T(8,128)(2,1)} %add_convert_fusion) | data formatting | bytes 9437184 | tf_op jit(solution)/shard_map/reshape | solution.py:184
  70.5 17.3 %copy.86 = bf16[2,512,3,4,192]{1,0,4,2,3:T(2,128)(2,1)} copy(bf16[2,512,3,4,192]{4,3,2,1,0:T(4,128)(2,1)} %reshape.747) | data formatting | bytes 9437184 | tf_op jit(solution)/shard_map/reshape | solution.py:184
  92.9 101.8 %all-to-all-done = bf16[2,512,3,4,192]{1,0,4,2,3:T(2,128)(2,1)} async-done(((bf16[2,512,3,4,192]{1,0,4,2,3:T(2,128)(2,1)}), bf16[2,512,3,4,192]{1,0,4,2,3:T(2,128)(2,1)}, u32[]{:S(2)}, u32[]{:S(2)}) %all-to-all-start) | async-done | bytes 4718624 | tf_op jit(solution)/shard_map/all_to_all | solution.py:193
  216.1 113.0 %while.22 = (s32[]{:T(128)}, bf16[2,2048,192]{1,2,0:T(8,128)(2,1)}, f32[2,3,2048]{2,1,0:T(4,128)S(1)}, bf16[2,2048,3,1,192]{1,4,2,3,0:T(8,128)(2,1)}, bf16[2,204...) while((s32[]{:T(128)}, bf16[2,2048,192]{1,2,0:T(8,128)(2,1)}, ...), condition=%wide.region_11.12_spmd, body=%wide.region_2.11_spmd.sunk | while | flops 3393599488 | bytes 199532768 | solution.py:82
  349.5 38.3 %all-to-all-done.2 = bf16[2,2048,1,192]{3,0,2,1:T(2,128)(2,1)} async-done(((bf16[2,2048,1,192]{3,0,2,1:T(2,128)(2,1)}), bf16[2,2048,1,192]{3,0,2,1:T(2,128)(2,1)}, u32[]{:S(2)}, u32[]{:S(2)}) %all-to-all-start.2) | async-done | bytes 1572896 | tf_op jit(solution)/shard_map/all_to_all | solution.py:198
  404.2 11.2 fusion.113
  415.5 13.7 %multiply_reduce_fusion.6 = (f32[1024]{0:T(1024)S(1)}, f32[1024,768]{1,0:T(8,128)}) fusion(bf16[2,512,768]{2,1,0:T(8,128)(2,1)} %param.22, f32[768]{0:T(1024)S(1)} %convert_element_type.248, f32[1024,768]{1,0:T(8,128)S(1)} %copy-done.15, bf16[3072,768]{1,0:T(8,128)(2,1)} %all-gather.12.cloned.1.call-done, f32[1024,3072]{1,0:T(8,128)} %fusion.113, ...), kind=kOutput, calls=%fused_computation.184 | convolution fusion | flops 4868013056 | bytes 25185280 | tf_op jit(solution)/shard_map/dot_general | solution.py:214
  429.8 39.5 %all-reduce.15 = (f32[]{:T(128)}, f32[]{:T(128)}) all-reduce(f32[]{:T(128)} %get-tuple-element.149, f32[]{:T(128)} %get-tuple-element.148), channel_id=1, replica_groups=mesh['fsdp'=8,'seq'=4] {'fsdp','seq'}, use_global_device_ids=true, to_apply=%region_16.17 | all-reduce | flops 2 | bytes 16 | tf_op jit(solution)/shard_map/psum | solution.py:219
  473.6 18.5 %convert_reduce_fusion = (f32[3072]{0:T(1024)}, bf16[1024,3072]{1,0:T(8,128)(2,1)S(1)}) fusion(f32[1024,3072]{1,0:T(8,128)} %fusion.113, f32[3072]{0:T(1024)S(1)} %bitcast.448, bf16[1024,768]{1,0:T(8,128)(2,1)S(1)} %get-tuple-element.202, bf16[3072,768]{1,0:T(8,128)(2,1)} %all-gather.12.cloned.1.call-done), kind=kOutput, calls=%fused_computation.151 | convolution fusion | flops 4916769792 | bytes 25190400 | tf_op jit(solution)/shard_map/rd,fd->rf/dot_general | solution.py:247
  532.8 13.0 %fusion.114 = f32[3072,768]{1,0:T(8,128)} fusion(bf16[1024,768]{1,0:T(8,128)(2,1)S(1)} %copy-done.36, f32[1024,3072]{1,0:T(8,128)} %fusion.113, f32[3072]{0:T(1024)S(1)} %bitcast.449), kind=kOutput, calls=%fused_computation.222 | convolution fusion | flops 4863295488 | bytes 23605248 | tf_op jit(solution)/shard_map/rf,rd->fd/dot_general | solution.py:244
  545.8 23.3 %all-to-all-done.3 = bf16[2,512,4,192]{1,0,3,2:T(2,128)(2,1)S(1)} async-done(((bf16[2,512,4,192]{1,0,3,2:T(2,128)(2,1)}), bf16[2,512,4,192]{1,0,3,2:T(2,128)(2,1)S(1)}, u32[]{:S(2)}, u32[]{:S(2)}) %all-to-all-start.3) | async-done | bytes 1572896 | tf_op jit(solution)/shard_map/all_to_all | solution.py:266
  571.6 315.2 %while.23 = (s32[]{:T(128)}, bf16[2,2048,3,1,192]{1,4,3,2,0:T(8,128)(2,1)}, bf16[2,2048,3,1,192]{1,4,2,3,0:T(8,128)(2,1)}, bf16[2,2048]{1,0:T(2,128)(2,1)S(1)}, ...) while((s32[]{:T(128)}, ...), condition=%wide.region_26.27_spmd, body=%wide.region_21.26_spmd.sunk | while | flops 8274178048 | bytes 657154752 | solution.py:273
  633.1 26.1 %multiply_convert_fusion.8 = (bf16[3,512,2048]{2,1,0:T(8,128)(2,1)}, bf16[3,512,2048]{2,1,0:T(8,128)(2,1)}) fusion(f32[3,512,2048]{2,1,0:T(8,128)} %get-tuple-element.454, f32[3,512,2048]{2,1,0:T(8,128)} %copy-done, f32[3,512]{1,0:T(4,128)S(1)} %get-tuple-element.455, f32[3,512]{1,0:T(4,128)S(1)} %get-tuple-element.443, ...), kind=kLoop, calls=%fused_computation.68.clone.1 | loop fusion | flops 37748736 | bytes 65036288 | tf_op jit(solution)/shard_map/while/body/eval_jaxpr/convert_element_type | solution.py:109
  696.7 18.2 %multiply_convert_fusion.9 = (bf16[3,512,2048]{2,1,0:T(8,128)(2,1)}, bf16[3,512,2048]{2,1,0:T(8,128)(2,1)}) fusion(f32[3,512,2048]{2,1,0:T(8,128)} %get-tuple-element.460, f32[3,512,2048]{2,1,0:T(8,128)} %fusion.362, f32[3,512]{1,0:T(4,128)} %get-tuple-element.461, f32[3,512]{1,0:T(4,128)S(1)} %get-tuple-element.451, ...), kind=kLoop, calls=%fused_computation.62.clone.1 | loop fusion | flops 37748736 | bytes 65036288 | tf_op jit(solution)/shard_map/while/body/eval_jaxpr/convert_element_type | solution.py:109
  789.1 22.8 %multiply_convert_fusion.8 = (bf16[3,512,2048]{2,1,0:T(8,128)(2,1)}, bf16[3,512,2048]{2,1,0:T(8,128)(2,1)}) fusion(f32[3,512,2048]{2,1,0:T(8,128)} %get-tuple-element.454, f32[3,512,2048]{2,1,0:T(8,128)} %copy-done, f32[3,512]{1,0:T(4,128)S(1)} %get-tuple-element.455, f32[3,512]{1,0:T(4,128)S(1)} %get-tuple-element.443, ...), kind=kLoop, calls=%fused_computation.68.clone.1 | loop fusion | flops 37748736 | bytes 65036288 | tf_op jit(solution)/shard_map/while/body/eval_jaxpr/convert_element_type | solution.py:109
  847.8 18.1 %multiply_convert_fusion.9 = (bf16[3,512,2048]{2,1,0:T(8,128)(2,1)}, bf16[3,512,2048]{2,1,0:T(8,128)(2,1)}) fusion(f32[3,512,2048]{2,1,0:T(8,128)} %get-tuple-element.460, f32[3,512,2048]{2,1,0:T(8,128)} %fusion.362, f32[3,512]{1,0:T(4,128)} %get-tuple-element.461, f32[3,512]{1,0:T(4,128)S(1)} %get-tuple-element.451, ...), kind=kLoop, calls=%fused_computation.62.clone.1 | loop fusion | flops 37748736 | bytes 65036288 | tf_op jit(solution)/shard_map/while/body/eval_jaxpr/convert_element_type | solution.py:109
  886.8 16.2 %copy.95 = bf16[2,2048,3,1,192]{4,0,3,2,1:T(2,128)(2,1)} copy(bf16[2,2048,3,1,192]{1,4,3,2,0:T(8,128)(2,1)} %get-tuple-element.77) | data formatting | bytes 9437184 | tf_op jit(solution)/shard_map/while | solution.py:273
  909.1 137.3 %all-to-all-done.4 = bf16[2,2048,3,1,192]{4,0,3,2,1:T(2,128)(2,1)} async-done(((bf16[2,2048,3,1,192]{4,0,3,2,1:T(2,128)(2,1)}), bf16[2,2048,3,1,192]{4,0,3,2,1:T(2,128)(2,1)}, u32[]{:S(2)}, u32[]{:S(2)}) %all-to-all-start.4) | async-done | bytes 4718624 | tf_op jit(solution)/shard_map/all_to_all | solution.py:274
  1046.4 16.9 %copy.102 = bf16[2,4,512,3,1,192]{2,1,5,3,0,4:T(4,128)(2,1)} copy(bf16[2,4,512,3,1,192]{5,0,3,2,1,4:T(2,128)(2,1)} %bitcast.59) | data formatting | bytes 9437184 | tf_op jit(solution)/shard_map/all_to_all | solution.py:274
  1104.7 44.6 %reduce-scatter.5.cloned.1.call-done = f32[96,2304]{1,0:T(8,128)} async-done(((f32[768,2304]{1,0:T(8,128)}), f32[96,2304]{1,0:T(8,128)}) %reduce-scatter.5.cloned.1.call-update) | async-done | bytes 884752 | tf_op jit(solution)/shard_map/reduce_scatter | solution.py:290
  1159.2 25.1 %all-reduce.16 = (bf16[768]{0:T(1024)(128)(2,1)S(1)}, bf16[768]{0:T(1024)(128)(2,1)S(1)}, bf16[1536]{0:T(1024)(128)(2,1)S(1)}, bf16[768]{0:T(1024)(128)(2,1)S(1)...) all-reduce(f32[768]{0:T(1024)S(1)} %get-tuple-element.143, ...), channel_id=2, replica_groups=mesh['fsdp'=8,'seq'=4] {'fsdp'}, use_global_device_ids=true, to_apply=%region_30.31.clone | all-reduce | flops 9216 | bytes 55296
  1184.9 11.8 all-reduce.18
  1205.3 24.9 %all-reduce.22.cloned.1.call-done = (bf16[96,2304]{1,0:T(8,128)(2,1)}, bf16[96,768]{1,0:T(8,128)(2,1)}, bf16[96,3072]{1,0:T(8,128)(2,1)}, bf16[384,768]{1,0:T(8,128)(2,1)}) async-done(((bf16[96,2304]{1,0:T(8,128)(2,1)}, bf16[96,768]{1,0:T(8,128)(2,1)}, bf16[96,3072]{1,0:T(8,128)(2,1)}, bf16[384,768]{1,0:T(8,128)(2,1)}), (bf16[96,2304]{1,0:T(8,128)(2,1)}, bf16[96,768]{1,0:T(8,128)(2,1)}, ...) | async-done | bytes 1769488 | tf_op jit(solution)/shard_map/psum | solution.py:304
  (469 shorter events, 521.9 us)
Async XLA Ops:
  7.2 42.3 %copy-start.5 = (bf16[2,512,768]{2,1,0:T(8,128)(2,1)S(1)}, bf16[2,512,768]{2,1,0:T(8,128)(2,1)}, u32[]{:S(2)}) copy-start(bf16[2,512,768]{2,1,0:T(8,128)(2,1)} %param.21) | copy-start | bytes 4718596
  7.2 42.9 %all-gather.6.cloned.1.call-start = ((), (), s32[]{:S(2)}) async-start(), calls=%async_computation.9 | async-start | bytes 3981312 | tf_op jit(solution)/shard_map/all_gather | solution.py:154
  7.9 390.7 %all-gather.8.cloned.1.call-start = ((), (), s32[]{:S(2)}) async-start(), calls=%async_computation.10 | async-start | bytes 1327104 | tf_op jit(solution)/shard_map/all_gather | solution.py:156
  8.7 395.6 %all-gather.10.cloned.1.call-start = ((), (), s32[]{:S(2)}) async-start(), calls=%async_computation.11 | async-start | bytes 5308416 | tf_op jit(solution)/shard_map/all_gather | solution.py:160
  87.8 106.9 %all-to-all-start = ((bf16[2,512,3,4,192]{1,0,4,2,3:T(2,128)(2,1)}), bf16[2,512,3,4,192]{1,0,4,2,3:T(2,128)(2,1)}, u32[]{:S(2)}, u32[]{:S(2)}) async-start(bf16[2,512,3,4,192]{1,0,4,2,3:T(2,128)(2,1)} %copy.86), calls=%async_computation | async-start | bytes 9437184 | tf_op jit(solution)/shard_map/all_to_all | solution.py:193
  195.3 20.8 %all-to-all-start.1 = ((bf16[2,512,1,4,1]{1,0,4,2,3:T(2,128)(2,1)}), bf16[2,512,1,4,1]{1,0,4,2,3:T(2,128)(2,1)S(1)}, u32[]{:S(2)}, u32[]{:S(2)}) async-start(bf16[2,512,1,4,1]{1,0,4,2,3:T(2,128)(2,1)} %broadcast_in_dim.114), calls=%async_computation.1 | async-start | bytes 16384 | tf_op jit(solution)/shard_map/all_to_all | solution.py:194
  198.5 216.9 %all-gather.12.cloned.1.call-start = ((), (), s32[]{:S(2)}) async-start(), calls=%async_computation.12 | async-start | bytes 5308416 | tf_op jit(solution)/shard_map/all_gather | solution.py:162
  335.3 63.3 %copy-start.6 = (bf16[2,512,768]{2,1,0:T(8,128)(2,1)S(1)}, bf16[2,512,768]{2,1,0:T(8,128)(2,1)}, u32[]{:S(2)}) copy-start(bf16[2,512,768]{2,1,0:T(8,128)(2,1)} %param.21) | copy-start | bytes 4718596
  335.3 52.5 %all-to-all-start.2 = ((bf16[2,2048,1,192]{3,0,2,1:T(2,128)(2,1)}), bf16[2,2048,1,192]{3,0,2,1:T(2,128)(2,1)}, u32[]{:S(2)}, u32[]{:S(2)}) async-start(bf16[2,2048,1,192]{3,0,2,1:T(2,128)(2,1)} %bitcast.418), calls=%async_computation.2 | async-start | bytes 4194304 | tf_op jit(solution)/shard_map/all_to_all | solution.py:198
  340.5 747.7 %reduce-scatter.7.cloned.1.call-start = ((), (), s32[]{:S(2)}) async-start(), calls=%async_computation.14 | async-start | bytes 2654208 | tf_op jit(solution)/shard_map/reduce_scatter | solution.py:292
  470.0 22.1 %slice-start.4 = ((s8[4718592]{0:T(1024)(128)(4,1)}), s8[4194304]{0:T(1024)(128)(4,1)S(1)}, s32[]{:S(2)}) async-start(s8[4718592]{0:T(1024)(128)(4,1)} %bitcast.450), calls=%async_computation.22 | async-start | bytes 8388608
  507.7 592.7 %reduce-scatter.9.cloned.1.call-start = ((), (), s32[]{:S(2)}) async-start(), calls=%async_computation.15 | async-start | bytes 10616832 | tf_op jit(solution)/shard_map/reduce_scatter | solution.py:296
  528.6 40.6 %all-to-all-start.3 = ((bf16[2,512,4,192]{1,0,3,2:T(2,128)(2,1)}), bf16[2,512,4,192]{1,0,3,2:T(2,128)(2,1)S(1)}, u32[]{:S(2)}, u32[]{:S(2)}) async-start(bf16[2,512,4,192]{1,0,3,2:T(2,128)(2,1)} %reshape.704), calls=%async_computation.3 | async-start | bytes 3145728 | tf_op jit(solution)/shard_map/all_to_all | solution.py:266
  532.8 569.8 %reduce-scatter.11.cloned.1.call-start = ((), (), s32[]{:S(2)}) async-start(), calls=%async_computation.16 | async-start | bytes 10616832 | tf_op jit(solution)/shard_map/reduce_scatter | solution.py:298
  572.6 27.3 %copy-start.26 = (f32[3,512]{1,0:T(4,128)}, f32[3,512]{1,0:T(4,128)S(1)}, u32[]{:S(2)}) copy-start(f32[3,512]{1,0:T(4,128)S(1)} %get-tuple-element.435) | copy-start | bytes 18436 | tf_op jit(solution)/shard_map/while
  580.3 42.4 %copy-start.4 = (pred[512,2048]{1,0:T(8,128)(4,1)}, pred[512,2048]{1,0:T(8,128)(4,1)S(1)}, u32[]{:S(2)}) copy-start(pred[512,2048]{1,0:T(8,128)(4,1)S(1)} %get-tuple-element.448) | copy-start | bytes 3145732 | tf_op jit(solution)/shard_map/while
  729.0 27.3 %copy-start.26 = (f32[3,512]{1,0:T(4,128)}, f32[3,512]{1,0:T(4,128)S(1)}, u32[]{:S(2)}) copy-start(f32[3,512]{1,0:T(4,128)S(1)} %get-tuple-element.435) | copy-start | bytes 18436 | tf_op jit(solution)/shard_map/while
  732.4 18.5 %copy-start.10 = (bf16[512,1,1,192]{0,3,2,1:T(8,128)(2,1)}, bf16[512,1,1,192]{0,3,2,1:T(8,128)(2,1)S(1)}, u32[]{:S(2)}) copy-start(bf16[512,1,1,192]{0,3,2,1:T(8,128)(2,1)S(1)} %get-tuple-element.433) | copy-start | bytes 589828 | tf_op jit(solution)/shard_map/while
  736.7 41.9 %copy-start.4 = (pred[512,2048]{1,0:T(8,128)(4,1)}, pred[512,2048]{1,0:T(8,128)(4,1)S(1)}, u32[]{:S(2)}) copy-start(pred[512,2048]{1,0:T(8,128)(4,1)S(1)} %get-tuple-element.448) | copy-start | bytes 3145732 | tf_op jit(solution)/shard_map/while
  902.9 143.4 %all-to-all-start.4 = ((bf16[2,2048,3,1,192]{4,0,3,2,1:T(2,128)(2,1)}), bf16[2,2048,3,1,192]{4,0,3,2,1:T(2,128)(2,1)}, u32[]{:S(2)}, u32[]{:S(2)}) async-start(bf16[2,2048,3,1,192]{4,0,3,2,1:T(2,128)(2,1)} %copy.95), calls=%async_computation.4 | async-start | bytes 12582912 | tf_op jit(solution)/shard_map/all_to_all | solution.py:274
  908.3 241.0 %reduce-scatter.5.cloned.1.call-start = ((), (), s32[]{:S(2)}) async-start(), calls=%async_computation.13 | async-start | bytes 7962624 | tf_op jit(solution)/shard_map/reduce_scatter | solution.py:290
  1084.7 145.5 %all-reduce.22.cloned.1.call-start = ((), (), s32[]{:S(2)}) async-start(), calls=%async_computation.17 | async-start | bytes 3538944 | tf_op jit(solution)/shard_map/psum | solution.py:304
  1104.7 51.4 %copy-start.50 = (f32[1,4,2,128]{3,1,2,0:T(4,128)S(1)}, f32[1,4,2,128]{3,1,2,0:T(4,128)}, u32[]{:S(2)}) copy-start(f32[1,4,2,128]{3,1,2,0:T(4,128)} %copy-done.49) | copy-start | bytes 12292
  1104.7 51.4 %copy-start.44 = (f32[1024]{0:T(1024)S(1)}, f32[1024]{0:T(1024)}, u32[]{:S(2)}) copy-start(f32[1024]{0:T(1024)} %copy-done.43) | copy-start | bytes 12292
  (92 other events, 480.8 us)
Sparse Core Ops, SparseCore 0:
  9.9 36.8 all-gather.5
  48.7 24.0 all-gather.7
  74.7 38.9 all-gather.9
  201.0 40.8 all-gather.11
  507.8 43.0 reduce-scatter.6
  554.7 76.4 reduce-scatter.8
  635.1 76.4 reduce-scatter.10
  1084.8 64.5 reduce-scatter.4
  1153.1 76.9 all-reduce.21
where the time goes:
time: 1260 us; the launch traced here: 1250 us
  waiting for transfers between devices  373 us (30%)
  matrix products  356 us (28%)
  other arithmetic  177 us (14%)
  local copies, waits for them, and re-layouts  159 us (13%)
  blocking collectives  112 us (9%)
  loops' own time  24.8 us (2%)
  starting transfers between devices  23.5 us (2%)
  between operations  21.1 us (2%)
    all_to_all x1, waiting for transfers between devices, local(): lax.all_to_all(grad_joint_heads, 'seq', split_axis=1, concat_axis=3, tile...  137 us
    all_to_all x1, waiting for transfers between devices, local(): lax.all_to_all(joint_low, 'seq', split_axis=3, concat_axis=1, tiled=True)  102 us
    convert_element_type x4, other arithmetic, back_sequence(): grad_scores = (probs * (grad_probs - center)).astype(jnp.bfloat16)  85.3 us
    dot_general x8, matrix products, back_sequence(): jnp.einsum('qhd,khd->hqk', grad_block, values, preferred_element_type=jnp...  73.9 us
    dot_general x16, matrix products, block_scores(): jnp.einsum('qhd,khd->hqk', query_block, keys, preferred_element_type=jnp....  54.2 us
    unnamed x2, blocking collectives  51.7 us
    dot_general x8, matrix products, back_sequence(): jnp.einsum('hqk,qhd->khd', probs_low, grad_block, preferred_element_type=...  46.4 us
    reduce_scatter x1, waiting for transfers between devices, local(): lax.psum_scatter(grad_jointweight, 'fsdp', scatter_dimension=0, tiled=True)  44.6 us
  transfers between devices with their start and end apart: 14, of which 6 were waited for; matrix products, arithmetic and copies ran while one was open for 48% of the time, Pallas kernels for 0%

commit v1 on v0

v1 whole, which is shorter than its diff:
```python
import functools

import jax
import jax.numpy as jnp
from jax import lax
from jax.experimental import pallas as pl
from jax.experimental.pallas import tpu as pltpu
from jax.sharding import PartitionSpec as P

H = 12
HD = 64
PAIR = 2 * HD
EPSILON = 1e-05
KEY_TILE = 128
QUERY_TILE = 256
ROW_TILE = 256
HALO_CHUNK = 128
VMEM_LIMIT = 62 * 1024 * 1024

NT = (((1,), (1,)), ((), ()))
NN = (((1,), (0,)), ((), ()))
TN = (((0,), (0,)), ((), ()))
F32 = jnp.float32
BF16 = jnp.bfloat16


def dot(left, right, dims=NN):
    return lax.dot_general(left, right, dims, preferred_element_type=F32)


def norm_parts(values):
    center = values - jnp.mean(values, -1, keepdims=True)
    spread = jnp.mean(center * center, -1, keepdims=True)
    scale = lax.rsqrt(spread + EPSILON)
    return center * scale, scale


def norm_back(grad, gain, unit, scale):
    weighted = grad * gain
    first = jnp.mean(weighted, -1, keepdims=True)
    second = jnp.mean(weighted * unit, -1, keepdims=True)
    return scale * (weighted - first - unit * second)


def piece_copies(order_ref, pieces, whole_ref, sems):
    copies = []
    for place, piece in enumerate(pieces):
        rows = piece.shape[0]
        if len(pieces) == 1:
            target = whole_ref
        else:
            target = whole_ref.at[pl.ds(pl.multiple_of(order_ref[place] * rows, 16), rows), :]
        copies.append(pltpu.make_async_copy(piece, target, sems.at[place]))
    return copies


def project_kernel(
    halo_tiles, count, low_ref, order_ref, halo_ref, own_ref, gain_ref, shift_ref, bias_ref, *rest
):
    pieces = rest[:count]
    normed_ref, query_ref, key_ref, value_ref, weight_ref, sems = rest[count:]
    seq, tile = pl.program_id(0), pl.program_id(1)
    width = own_ref.shape[-1]

    @pl.when((seq == 0) & (tile == 0))
    def _():
        copies = piece_copies(order_ref, pieces, weight_ref, sems)
        for copy in copies:
            copy.start()
        for copy in copies:
            copy.wait()

    def keys_values(rows):
        unit, _ = norm_parts(rows.astype(F32))
        normed = (unit * gain_ref[...] + shift_ref[...]).astype(BF16)
        normed_ref[0] = normed
        key_ref[0] = dot(normed, weight_ref[:, width : 2 * width]).astype(BF16)
        value_ref[0] = (
            dot(normed, weight_ref[:, 2 * width :]) + bias_ref[:, width:]
        ).astype(BF16)

    @pl.when((tile >= low_ref[seq]) & (tile < halo_tiles))
    def _():
        keys_values(halo_ref[0])

    @pl.when(tile >= halo_tiles)
    def _():
        keys_values(own_ref[0])
        query_ref[0] = (
            dot(normed_ref[0], weight_ref[:, :width]) + bias_ref[:, :width]
        ).astype(BF16)


def project(low, order, halo, own, gain, shift, bias, pieces):
    seqs, block, width = own.shape
    halo_tiles = halo.shape[1] // ROW_TILE
    own_tiles = block // ROW_TILE
    length = halo.shape[1] + block
    spot = lambda s, t, low, order: (s, jnp.maximum(t, low[s]), 0)
    in_halo = lambda s, t, low, order: (
        s,
        jnp.minimum(jnp.maximum(t, low[s]), halo_tiles - 1),
        0,
    )
    in_own = lambda s, t, low, order: (s, jnp.maximum(t - halo_tiles, 0), 0)
    fixed = lambda s, t, low, order: (0, 0)
    tile = (1, ROW_TILE, width)
    return pl.pallas_call(
        functools.partial(project_kernel, halo_tiles, len(pieces)),
        grid_spec=pltpu.PrefetchScalarGridSpec(
            num_scalar_prefetch=2,
            grid=(seqs, halo_tiles + own_tiles),
            in_specs=[
                pl.BlockSpec(tile, in_halo),
                pl.BlockSpec(tile, in_own),
                pl.BlockSpec((1, width), fixed),
                pl.BlockSpec((1, width), fixed),
                pl.BlockSpec((1, 2 * width), fixed),
            ]
            + [pl.BlockSpec(memory_space=pl.ANY)] * len(pieces),
            out_specs=[
                pl.BlockSpec(tile, spot),
                pl.BlockSpec(tile, in_own),
                pl.BlockSpec(tile, spot),
                pl.BlockSpec(tile, spot),
            ],
            scratch_shapes=[
                pltpu.VMEM((width, 3 * width), BF16),
                pltpu.SemaphoreType.DMA((len(pieces),)),
            ],
        ),
        out_shape=[
            jax.ShapeDtypeStruct((seqs, length, width), BF16),
            jax.ShapeDtypeStruct((seqs, block, width), BF16),
            jax.ShapeDtypeStruct((seqs, length, width), BF16),
            jax.ShapeDtypeStruct((seqs, length, width), BF16),
        ],
        compiler_params=pltpu.CompilerParams(vmem_limit_bytes=VMEM_LIMIT),
        cost_estimate=pl.CostEstimate(
            flops=10 * seqs * block * width * width, bytes_accessed=24 << 20, transcendentals=0
        ),
        name="project",
    )(low, order, halo, own, gain, shift, bias, *pieces)


def two_heads(tile):
    left = lax.broadcasted_iota(jnp.int32, tile.shape, 1) < HD
    zero = jnp.zeros_like(tile)
    return jnp.concatenate([jnp.where(left, tile, zero), jnp.where(left, zero, tile)], 0)


def visible(first_key, starts, first_query):
    shape = (KEY_TILE, starts.shape[1])
    keys = first_key + lax.broadcasted_iota(jnp.int32, shape, 0)
    queries = first_query + lax.broadcasted_iota(jnp.int32, shape, 1)
    return (keys >= starts) & (keys <= queries)


def attend_kernel(halo, low_ref, query_ref, key_ref, value_ref, start_ref, out_ref, log_ref):
    seq = pl.program_id(0)
    block = query_ref.shape[1]
    tiles = block // QUERY_TILE
    for tile in range(tiles):
        here = slice(tile * QUERY_TILE, (tile + 1) * QUERY_TILE)
        query = query_ref[0, here, :] * 0.125
        starts = start_ref[0, :, here]

        def step(j, carry):
            high0, high1, total0, total1, mixed = carry
            place = pl.ds(pl.multiple_of(j * KEY_TILE, KEY_TILE), KEY_TILE)
            scores = dot(two_heads(key_ref[0, place, :]), query, NT)
            ok = visible(j * KEY_TILE, starts, halo + tile * QUERY_TILE)
            scores0 = jnp.where(ok, scores[:KEY_TILE], -1e30)
            scores1 = jnp.where(ok, scores[KEY_TILE:], -1e30)
            next0 = jnp.maximum(high0, jnp.max(scores0, 0, keepdims=True))
            next1 = jnp.maximum(high1, jnp.max(scores1, 0, keepdims=True))
            powers0 = jnp.exp(scores0 - next0)
            powers1 = jnp.exp(scores1 - next1)
            fade0 = jnp.exp(high0 - next0)
            fade1 = jnp.exp(high1 - next1)
            total0 = total0 * fade0 + jnp.sum(powers0, 0, keepdims=True)
            total1 = total1 * fade1 + jnp.sum(powers1, 0, keepdims=True)
            powers = jnp.concatenate([powers0.astype(BF16), powers1.astype(BF16)], 0)
            added = dot(two_heads(value_ref[0, place, :]), powers, TN)
            fade = jnp.concatenate(
                [
                    jnp.broadcast_to(fade0, (HD, QUERY_TILE)),
                    jnp.broadcast_to(fade1, (HD, QUERY_TILE)),
                ],
                0,
            )
            return next0, next1, total0, total1, mixed * fade + added

        row = jnp.zeros((1, QUERY_TILE), F32)
        high0, high1, total0, total1, mixed = lax.fori_loop(
            low_ref[seq * tiles + tile],
            (halo + (tile + 1) * QUERY_TILE) // KEY_TILE,
            step,
            (row - 1e30, row - 1e30, row, row, jnp.zeros((PAIR, QUERY_TILE), F32)),
        )
        total = jnp.concatenate(
            [
                jnp.broadcast_to(total0, (HD, QUERY_TILE)),
                jnp.broadcast_to(total1, (HD, QUERY_TILE)),
            ],
            0,
        )
        out_ref[0, here, :] = jnp.transpose(mixed / total).astype(BF16)
        log_ref[0, 0, 0:1, here] = high0 + jnp.log(total0)
        log_ref[0, 0, 1:2, here] = high1 + jnp.log(total1)


def attend(low, query, keys, values, starts):
    seqs, block, width = query.shape
    length = keys.shape[1]
    pairs = width // PAIR
    rows = pl.BlockSpec((1, block, PAIR), lambda s, p, low: (s, 0, p))
    full = pl.BlockSpec((1, length, PAIR), lambda s, p, low: (s, 0, p))
    return pl.pallas_call(
        functools.partial(attend_kernel, length - block),
        grid_spec=pltpu.PrefetchScalarGridSpec(
            num_scalar_prefetch=1,
            grid=(seqs, pairs),
            in_specs=[rows, full, full, pl.BlockSpec((1, 1, block), lambda s, p, low: (s, 0, 0))],
            out_specs=[rows, pl.BlockSpec((1, 1, 2, block), lambda s, p, low: (s, p, 0, 0))],
        ),
        out_shape=[
            jax.ShapeDtypeStruct((seqs, block, width), BF16),
            jax.ShapeDtypeStruct((seqs, pairs, 2, block), F32),
        ],
        compiler_params=pltpu.CompilerParams(vmem_limit_bytes=VMEM_LIMIT),
        cost_estimate=pl.CostEstimate(
            flops=16 << 30, bytes_accessed=16 << 20, transcendentals=8 << 20
        ),
        name="attend",
    )(low, query, keys, values, starts)


def attend_back_kernel(
    halo,
    low_ref,
    first_ref,
    query_ref,
    key_ref,
    value_ref,
    start_ref,
    out_ref,
    grad_ref,
    log_ref,
    gquery_ref,
    gkey_ref,
    gvalue_ref,
    turned_ref,
    center_ref,
    sumk_ref,
    sumv_ref,
):
    seq = pl.program_id(0)
    block = query_ref.shape[1]
    tiles = block // QUERY_TILE
    turned_ref[...] = jnp.zeros_like(turned_ref)
    products = jnp.transpose(grad_ref[0].astype(F32) * out_ref[0].astype(F32))
    center_ref[0:1, :] = jnp.sum(products[:HD], 0, keepdims=True)
    center_ref[1:2, :] = jnp.sum(products[HD:], 0, keepdims=True)
    left = lax.broadcasted_iota(jnp.int32, (KEY_TILE, PAIR), 1) < HD

    def step(j, nothing):
        place = pl.ds(pl.multiple_of(j * KEY_TILE, KEY_TILE), KEY_TILE)
        keys = two_heads(key_ref[0, place, :])
        values = two_heads(value_ref[0, place, :])
        sumk_ref[...] = jnp.zeros_like(sumk_ref)
        sumv_ref[...] = jnp.zeros_like(sumv_ref)
        for tile in range(tiles):
            here = slice(tile * QUERY_TILE, (tile + 1) * QUERY_TILE)
            last = (halo + (tile + 1) * QUERY_TILE) // KEY_TILE

            @pl.when((j >= low_ref[seq * tiles + tile]) & (j < last))
            def _():
                query = query_ref[0, here, :] * 0.125
                grad = grad_ref[0, here, :]
                scores = dot(keys, query, NT)
                gprobs = dot(values, grad, NT)
                ok = visible(j * KEY_TILE, start_ref[0, :, here], halo + tile * QUERY_TILE)
                probs, gscores = [], []
                for head in range(2):
                    part = slice(head * KEY_TILE, (head + 1) * KEY_TILE)
                    masked = jnp.where(ok, scores[part] - log_ref[0, 0, head : head + 1, here], -1e30)
                    prob = jnp.exp(masked)
                    gscore = prob * (gprobs[part] - center_ref[head : head + 1, here])
                    probs.append(prob.astype(BF16))
                    gscores.append(gscore.astype(BF16))
                probs = jnp.concatenate(probs, 0)
                gscores = jnp.concatenate(gscores, 0)
                sumv_ref[...] += dot(probs, grad)
                sumk_ref[...] += dot(gscores, query)
                turned_ref[:, here] += dot(keys, gscores, TN)

        gkey_ref[0, place, :] = jnp.where(left, sumk_ref[:KEY_TILE], sumk_ref[KEY_TILE:]).astype(BF16)
        gvalue_ref[0, place, :] = jnp.where(left, sumv_ref[:KEY_TILE], sumv_ref[KEY_TILE:]).astype(BF16)
        return nothing

    lax.fori_loop(first_ref[seq], (halo + block) // KEY_TILE, step, 0)
    gquery_ref[0] = (jnp.transpose(turned_ref[...]) * 0.125).astype(BF16)


def attend_back(low, first, query, keys, values, starts, mixed, grad, logs):
    seqs, block, width = query.shape
    length = keys.shape[1]
    pairs = width // PAIR
    rows = pl.BlockSpec((1, block, PAIR), lambda s, p, low, first: (s, 0, p))
    full = pl.BlockSpec((1, length, PAIR), lambda s, p, low, first: (s, 0, p))
    return pl.pallas_call(
        functools.partial(attend_back_kernel, length - block),
        grid_spec=pltpu.PrefetchScalarGridSpec(
            num_scalar_prefetch=2,
            grid=(seqs, pairs),
            in_specs=[
                rows,
                full,
                full,
                pl.BlockSpec((1, 1, block), lambda s, p, low, first: (s, 0, 0)),
                rows,
                rows,
                pl.BlockSpec((1, 1, 2, block), lambda s, p, low, first: (s, p, 0, 0)),
            ],
            out_specs=[rows, full, full],
            scratch_shapes=[
                pltpu.VMEM((PAIR, block), F32),
                pltpu.VMEM((8, block), F32),
                pltpu.VMEM((2 * KEY_TILE, PAIR), F32),
                pltpu.VMEM((2 * KEY_TILE, PAIR), F32),
            ],
        ),
        out_shape=[
            jax.ShapeDtypeStruct((seqs, block, width), BF16),
            jax.ShapeDtypeStruct((seqs, length, width), BF16),
            jax.ShapeDtypeStruct((seqs, length, width), BF16),
        ],
        compiler_params=pltpu.CompilerParams(vmem_limit_bytes=VMEM_LIMIT),
        cost_estimate=pl.CostEstimate(
            flops=40 << 30, bytes_accessed=28 << 20, transcendentals=8 << 20
        ),
        name="attend_back",
    )(low, first, query, keys, values, starts, mixed, grad, logs)


def mlp_kernel(
    counts,
    order_ref,
    factor_ref,
    mixed_ref,
    token_ref,
    teacher_ref,
    weight_ref,
    outbias_ref,
    gain_ref,
    shift_ref,
    upbias_ref,
    downbias_ref,
    *rest,
):
    out_pieces = rest[: counts[0]]
    up_pieces = rest[counts[0] : counts[0] + counts[1]]
    down_pieces = rest[counts[0] + counts[1] : sum(counts)]
    (
        layer_ref,
        gresid_ref,
        gmixed_ref,
        normed_ref,
        active_ref,
        ghidden_ref,
        gmlp_ref,
        gbranch_ref,
        sums_ref,
        upsums_ref,
        merge_ref,
        up_ref,
        down_ref,
        slope_ref,
        resid_ref,
        total_ref,
        sems,
    ) = rest[sum(counts) :]
    width = token_ref.shape[-1]
    chunks = active_ref.shape[-1] // width
    step = pl.program_id(0)
    copies = [
        piece_copies(order_ref, pieces, whole, sems.at[k])
        for k, (pieces, whole) in enumerate(
            ((out_pieces, merge_ref), (up_pieces, up_ref), (down_pieces, down_ref))
        )
    ]

    def arrive(k):
        @pl.when(step == 0)
        def _():
            for copy in copies[k]:
                copy.wait()

    @pl.when(step == 0)
    def _():
        for group in copies:
            for copy in group:
                copy.start()
        sums_ref[...] = jnp.zeros_like(sums_ref)
        upsums_ref[...] = jnp.zeros_like(upsums_ref)

    arrive(0)
    resid = (
        token_ref[...].astype(F32) + dot(mixed_ref[...], merge_ref[...]) + outbias_ref[...]
    )
    unit, scale = norm_parts(resid)
    normed_ref[...] = (unit * gain_ref[...] + shift_ref[...]).astype(BF16)
    resid_ref[...] = resid
    arrive(1)
    arrive(2)
    total_ref[...] = resid + downbias_ref[...]

    def forward(c, nothing):
        cols = pl.ds(pl.multiple_of(c * width, 128), width)
        hidden = dot(normed_ref[...], up_ref[:, cols]) + upbias_ref[:, cols]
        square = hidden * hidden
        curve = jnp.tanh(0.7978845608028654 * (hidden + 0.044715 * square * hidden))
        half = 0.5 * (1.0 + curve)
        active = (half * hidden).astype(BF16)
        active_ref[:, cols] = active
        slope_ref[:, cols] = half + 0.5 * hidden * (1.0 - curve * curve) * (
            0.7978845608028654 * (1.0 + 3.0 * 0.044715 * square)
        )
        total_ref[...] += dot(active, down_ref[cols, :])
        return nothing

    lax.fori_loop(0, chunks, forward, 0)
    result = total_ref[...]
    layer_ref[...] = result.astype(BF16)
    error = result - teacher_ref[...].astype(F32)
    weight = weight_ref[...]
    sums_ref[4:5, :] += jnp.sum(weight * (error * error), 0, keepdims=True)
    gresult = error * (weight * factor_ref[0])
    gmlp = gresult.astype(BF16)
    gmlp_ref[...] = gmlp
    gresid_ref[...] = gresult
    sums_ref[3:4, :] += jnp.sum(gmlp.astype(F32), 0, keepdims=True)
    total_ref[...] = jnp.zeros_like(total_ref)

    def backward(c, nothing):
        cols = pl.ds(pl.multiple_of(c * width, 128), width)
        gactive = dot(gmlp_ref[...], down_ref[cols, :], NT)
        ghidden = (gactive * slope_ref[:, cols]).astype(BF16)
        ghidden_ref[:, cols] = ghidden
        upsums_ref[0:1, cols] += jnp.sum(ghidden.astype(F32), 0, keepdims=True)
        total_ref[...] += dot(ghidden, up_ref[:, cols], NT)
        return nothing

    lax.fori_loop(0, chunks, backward, 0)
    gnormed = total_ref[...]
    unit, scale = norm_parts(resid_ref[...])
    sums_ref[1:2, :] += jnp.sum(gnormed * unit, 0, keepdims=True)
    sums_ref[2:3, :] += jnp.sum(gnormed, 0, keepdims=True)
    gresid = gresid_ref[...] + norm_back(gnormed, gain_ref[...], unit, scale)
    gresid_ref[...] = gresid
    gbranch = gresid.astype(BF16)
    gbranch_ref[...] = gbranch
    sums_ref[0:1, :] += jnp.sum(gbranch.astype(F32), 0, keepdims=True)
    gmixed_ref[...] = dot(gbranch, merge_ref[...], NT).astype(BF16)


def mlp(order, factor, mixed, tokens, teacher, weight, vectors, out_pieces, up_pieces, down_pieces):
    rows, width = tokens.shape
    outbias, gain, shift, upbias, downbias = vectors
    hidden = upbias.shape[1]
    tile = lambda n: pl.BlockSpec((ROW_TILE, n), lambda i, order: (i, 0))
    fixed = lambda m, n: pl.BlockSpec((m, n), lambda i, order: (0, 0))
    pieces = [*out_pieces, *up_pieces, *down_pieces]
    counts = (len(out_pieces), len(up_pieces), len(down_pieces))
    shape = jax.ShapeDtypeStruct
    return pl.pallas_call(
        functools.partial(mlp_kernel, counts),
        grid_spec=pltpu.PrefetchScalarGridSpec(
            num_scalar_prefetch=1,
            grid=(rows // ROW_TILE,),
            in_specs=[
                pl.BlockSpec(memory_space=pltpu.SMEM),
                tile(width),
                tile(width),
                tile(width),
                tile(1),
                fixed(1, width),
                fixed(1, width),
                fixed(1, width),
                fixed(1, hidden),
                fixed(1, width),
            ]
            + [pl.BlockSpec(memory_space=pl.ANY)] * len(pieces),
            out_specs=[
                tile(width),
                tile(width),
                tile(width),
                tile(width),
                tile(hidden),
                tile(hidden),
                tile(width),
                tile(width),
                fixed(8, width),
                fixed(8, hidden),
            ],
            scratch_shapes=[
                pltpu.VMEM((width, width), BF16),
                pltpu.VMEM((width, hidden), BF16),
                pltpu.VMEM((hidden, width), BF16),
                pltpu.VMEM((ROW_TILE, hidden), F32),
                pltpu.VMEM((ROW_TILE, width), F32),
                pltpu.VMEM((ROW_TILE, width), F32),
                pltpu.SemaphoreType.DMA((3, max(counts))),
            ],
        ),
        out_shape=[
            shape((rows, width), BF16),
            shape((rows, width), F32),
            shape((rows, width), BF16),
            shape((rows, width), BF16),
            shape((rows, hidden), BF16),
            shape((rows, hidden), BF16),
            shape((rows, width), BF16),
            shape((rows, width), BF16),
            shape((8, width), F32),
            shape((8, hidden), F32),
        ],
        compiler_params=pltpu.CompilerParams(vmem_limit_bytes=VMEM_LIMIT),
        cost_estimate=pl.CostEstimate(
            flops=4 * rows * width * (width + 2 * hidden),
            bytes_accessed=40 << 20,
            transcendentals=rows * hidden,
        ),
        name="mlp",
    )(
        order,
        factor,
        mixed,
        tokens,
        teacher,
        weight,
        outbias,
        gain,
        shift,
        upbias,
        downbias,
        *pieces,
    )


def halo_back_kernel(
    count, low_ref, order_ref, halo_ref, gkey_ref, gvalue_ref, *rest
):
    pieces = rest[:count]
    out_ref, sums_ref, weight_ref, sems = rest[count:]
    seq, tile = pl.program_id(0), pl.program_id(1)
    width = halo_ref.shape[-1]

    @pl.when((seq == 0) & (tile == 0))
    def _():
        copies = piece_copies(order_ref, pieces, weight_ref, sems)
        for copy in copies:
            copy.start()
        for copy in copies:
            copy.wait()
        sums_ref[...] = jnp.zeros_like(sums_ref)

    @pl.when(tile < low_ref[seq])
    def _():
        out_ref[...] = jnp.zeros_like(out_ref)

    @pl.when(tile >= low_ref[seq])
    def _():
        grad = dot(gkey_ref[0], weight_ref[:, width : 2 * width], NT)
        grad += dot(gvalue_ref[0], weight_ref[:, 2 * width :], NT)
        unit, _ = norm_parts(halo_ref[0].astype(F32))
        out_ref[0] = grad.astype(BF16)
        sums_ref[0:1, :] += jnp.sum(grad * unit, 0, keepdims=True)
        sums_ref[1:2, :] += jnp.sum(grad, 0, keepdims=True)


def halo_back(low, order, halo, gkeys, gvalues, pieces):
    seqs, rows, width = halo.shape
    halo_tiles = rows // ROW_TILE
    tile = (1, ROW_TILE, width)
    spot = lambda s, t, low, order: (s, jnp.minimum(jnp.maximum(t, low[s]), halo_tiles - 1), 0)
    plain = lambda s, t, low, order: (s, t, 0)
    return pl.pallas_call(
        functools.partial(halo_back_kernel, len(pieces)),
        grid_spec=pltpu.PrefetchScalarGridSpec(
            num_scalar_prefetch=2,
            grid=(seqs, halo_tiles),
            in_specs=[pl.BlockSpec(tile, spot)] * 3
            + [pl.BlockSpec(memory_space=pl.ANY)] * len(pieces),
            out_specs=[
                pl.BlockSpec(tile, plain),
                pl.BlockSpec((8, width), lambda s, t, low, order: (0, 0)),
            ],
            scratch_shapes=[
                pltpu.VMEM((width, 3 * width), BF16),
                pltpu.SemaphoreType.DMA((len(pieces),)),
            ],
        ),
        out_shape=[
            jax.ShapeDtypeStruct((seqs, rows, width), BF16),
            jax.ShapeDtypeStruct((8, width), F32),
        ],
        compiler_params=pltpu.CompilerParams(vmem_limit_bytes=VMEM_LIMIT),
        cost_estimate=pl.CostEstimate(
            flops=4 << 30, bytes_accessed=16 << 20, transcendentals=0
        ),
        name="halo_back",
    )(low, order, halo, gkeys, gvalues, *pieces)


def own_back_kernel(
    halo_tiles,
    count,
    low_ref,
    order_ref,
    own_ref,
    normed_ref,
    gquery_ref,
    gkey_ref,
    gvalue_ref,
    *rest,
):
    pieces = rest[:count]
    gnormed_ref, gweight_ref, sums_ref, weight_ref, total_ref, sems = rest[count:]
    seq, tile = pl.program_id(0), pl.program_id(1)
    width = own_ref.shape[-1]
    own = tile >= halo_tiles
    copies = piece_copies(order_ref, pieces, weight_ref, sems)

    @pl.when((seq == 0) & (tile == 0))
    def _():
        for copy in copies:
            copy.start()
        sums_ref[...] = jnp.zeros_like(sums_ref)
        total_ref[...] = jnp.zeros_like(total_ref)
        for copy in copies:
            copy.wait()

    def gather(index, grad_ref):
        cols = slice(index * width, (index + 1) * width)
        total_ref[:, cols] += dot(normed_ref[0], grad_ref[0], TN)

    @pl.when(tile >= low_ref[seq])
    def _():
        gather(1, gkey_ref)
        gather(2, gvalue_ref)
        sums_ref[3:4, :] += jnp.sum(gvalue_ref[0].astype(F32), 0, keepdims=True)

    @pl.when(own)
    def _():
        gather(0, gquery_ref)
        sums_ref[2:3, :] += jnp.sum(gquery_ref[0].astype(F32), 0, keepdims=True)
        grad = dot(gquery_ref[0], weight_ref[:, :width], NT)
        grad += dot(gkey_ref[0], weight_ref[:, width : 2 * width], NT)
        grad += dot(gvalue_ref[0], weight_ref[:, 2 * width :], NT)
        gnormed_ref[0] = grad
        unit, _ = norm_parts(own_ref[0].astype(F32))
        sums_ref[0:1, :] += jnp.sum(grad * unit, 0, keepdims=True)
        sums_ref[1:2, :] += jnp.sum(grad, 0, keepdims=True)

    @pl.when((seq == pl.num_programs(0) - 1) & (tile == pl.num_programs(1) - 1))
    def _():
        gweight_ref[...] = total_ref[...].astype(BF16)


def own_back(low, order, own, normed, gquery, gkeys, gvalues, pieces):
    seqs, block, width = own.shape
    length = normed.shape[1]
    halo_tiles = (length - block) // ROW_TILE
    own_tiles = block // ROW_TILE
    tile = (1, ROW_TILE, width)
    spot = lambda s, t, low, order: (s, jnp.maximum(t, low[s]), 0)
    in_own = lambda s, t, low, order: (s, jnp.maximum(t - halo_tiles, 0), 0)
    fixed = lambda s, t, low, order: (0, 0)
    return pl.pallas_call(
        functools.partial(own_back_kernel, halo_tiles, len(pieces)),
        grid_spec=pltpu.PrefetchScalarGridSpec(
            num_scalar_prefetch=2,
            grid=(seqs, halo_tiles + own_tiles),
            in_specs=[
                pl.BlockSpec(tile, in_own),
                pl.BlockSpec(tile, spot),
                pl.BlockSpec(tile, in_own),
                pl.BlockSpec(tile, spot),
                pl.BlockSpec(tile, spot),
            ]
            + [pl.BlockSpec(memory_space=pl.ANY)] * len(pieces),
            out_specs=[
                pl.BlockSpec(tile, in_own),
                pl.BlockSpec((width, 3 * width), fixed),
                pl.BlockSpec((8, width), fixed),
            ],
            scratch_shapes=[
                pltpu.VMEM((width, 3 * width), BF16),
                pltpu.VMEM((width, 3 * width), F32),
                pltpu.SemaphoreType.DMA((len(pieces),)),
            ],
        ),
        out_shape=[
            jax.ShapeDtypeStruct((seqs, block, width), F32),
            jax.ShapeDtypeStruct((width, 3 * width), BF16),
            jax.ShapeDtypeStruct((8, width), F32),
        ],
        compiler_params=pltpu.CompilerParams(vmem_limit_bytes=VMEM_LIMIT),
        cost_estimate=pl.CostEstimate(
            flops=16 << 30, bytes_accessed=24 << 20, transcendentals=0
        ),
        name="own_back",
    )(low, order, own, normed, gquery, gkeys, gvalues, *pieces)


def finish_kernel(own_ref, gnormed_ref, more_ref, gresid_ref, gain_ref, out_ref):
    unit, scale = norm_parts(own_ref[...].astype(F32))
    grad = gnormed_ref[...] + more_ref[...].astype(F32)
    out_ref[...] = (gresid_ref[...] + norm_back(grad, gain_ref[...], unit, scale)).astype(BF16)


def finish(own, gnormed, more, gresid, gain):
    rows, width = own.shape
    tile = pl.BlockSpec((ROW_TILE, width), lambda i: (i, 0))
    return pl.pallas_call(
        finish_kernel,
        grid=(rows // ROW_TILE,),
        in_specs=[tile, tile, tile, tile, pl.BlockSpec((1, width), lambda i: (0, 0))],
        out_specs=tile,
        out_shape=jax.ShapeDtypeStruct((rows, width), BF16),
        cost_estimate=pl.CostEstimate(
            flops=20 * rows * width, bytes_accessed=14 * rows * width, transcendentals=0
        ),
        name="finish",
    )(own, gnormed, more, gresid, gain)


def swap(x, axis, bit):
    size = lax.axis_size(axis)
    return lax.ppermute(x, axis, [(i, i ^ bit) for i in range(size)])


def shift(x, axis, step):
    size = lax.axis_size(axis)
    return lax.ppermute(
        x, axis, [(i, i + step) for i in range(size) if 0 <= i + step < size]
    )


def sum_over(x, axis):
    bit = 1
    while bit < lax.axis_size(axis):
        x = x + swap(x, axis, bit)
        bit *= 2
    return x


def max_over(x, axis):
    bit = 1
    while bit < lax.axis_size(axis):
        x = jnp.maximum(x, swap(x, axis, bit))
        bit *= 2
    return x


def gather_pieces(shard):
    size = lax.axis_size("fsdp")
    if size != 8:
        return [lax.all_gather(shard, "fsdp", axis=0, tiled=True)]
    near = [shard] + [swap(shard, "fsdp", 2 * d) for d in range(1, size // 2)]
    return near + [swap(piece, "fsdp", 1) for piece in near]


def piece_order():
    size = lax.axis_size("fsdp")
    me = lax.axis_index("fsdp").astype(jnp.int32)
    if size != 8:
        return jnp.zeros((1,), jnp.int32)
    return jnp.stack(
        [me ^ (2 * d) for d in range(size // 2)] + [me ^ (2 * d) ^ 1 for d in range(size // 2)]
    )


def reduce_rows(parts):
    size = lax.axis_size("fsdp")
    me = lax.axis_index("fsdp")
    rows, columns = parts.shape[1:]
    if size != 8:
        total = lax.psum_scatter(parts, "fsdp", scatter_dimension=0, tiled=False)
        return lax.psum(total, "seq").astype(F32)
    pairs = parts.reshape(size // 2, 2, rows, columns)
    core = me % 2
    chip = me // 2
    pick = lambda a, k, ax: lax.dynamic_index_in_dim(a, k, ax, keepdims=False)
    other = swap(pick(pairs, 1 - core, 1), "fsdp", 1)
    mine = (pick(pairs, core, 1).astype(F32) + other.astype(F32)).astype(BF16)
    arrived = [
        swap(pick(mine, chip ^ d, 0), "fsdp", 2 * d) for d in range(1, size // 2)
    ]
    total = pick(mine, chip, 0).astype(F32)
    for part in arrived:
        total = total + part.astype(F32)
    total = total.astype(BF16)
    groups = lax.axis_size("seq")
    place = lax.axis_index("seq")
    if groups == 4:
        halves = total.reshape(2, rows // 2, columns)
        odd = place % 2
        half = pick(halves, odd, 0).astype(F32) + swap(pick(halves, 1 - odd, 0), "seq", 1).astype(F32)
        half = half.astype(BF16)
        half = (half.astype(F32) + swap(half, "seq", 2).astype(F32)).astype(BF16)
        back = swap(half, "seq", 1)
        return jnp.where(
            odd == 0,
            jnp.concatenate([half, back], 0),
            jnp.concatenate([back, half], 0),
        ).astype(F32)
    return lax.psum(total, "seq").astype(F32)


def local(
    tokens,
    teacher,
    segment_ids,
    latent_flags,
    valid_mask,
    attngain,
    attnshift,
    qkvweight,
    qvbias,
    outweight,
    outbias,
    mlpgain,
    mlpshift,
    fcweight,
    fcbias,
    projweight,
    projbias,
):
    seqs, block, width = tokens.shape
    groups = lax.axis_size("seq")
    owners = lax.axis_size("fsdp")
    rows = seqs * block
    halo_rows = (groups - 1) * block
    far_rows = halo_rows - block
    me = lax.axis_index("fsdp")
    place = lax.axis_index("seq").astype(jnp.int32)
    hidden = fcweight.shape[1]

    near = shift(tokens, "seq", 1)

    shards = [attngain, attnshift, qvbias, outbias, mlpgain, mlpshift, fcbias, projbias]
    packed = jnp.concatenate(shards)
    table = jnp.where(
        lax.broadcasted_iota(jnp.int32, (owners, packed.shape[0]), 0) == me,
        packed[None],
        jnp.zeros((), BF16),
    )
    if owners == 8:
        table = sum_over(table, "fsdp")
    else:
        table = lax.psum(table, "fsdp")
    vectors = []
    at = 0
    for shard in shards:
        size = shard.shape[0]
        vectors.append(table[:, at : at + size].reshape(1, size * owners).astype(F32))
        at += size
    gain1, shift1, bias1, outbias_v, gain2, shift2, upbias, downbias = vectors

    order = piece_order()
    qkv_pieces = gather_pieces(qkvweight)
    out_pieces = gather_pieces(outweight)
    up_pieces = gather_pieces(fcweight)
    down_pieces = gather_pieces(projweight)

    weight = (valid_mask * (1 - latent_flags)).astype(F32)
    below = jnp.sum(
        (segment_ids[:, :, None] < jnp.arange(1, 4, dtype=jnp.int32)).astype(jnp.int32), 1
    )
    facts = jnp.concatenate([below.reshape(-1), jnp.sum(weight).astype(jnp.int32)[None]])
    facts = sum_over(facts, "seq")
    bounds = facts[:-1].reshape(seqs, 3)

    def start_of(positions):
        found = jnp.zeros((seqs,) + positions.shape, jnp.int32)
        for d in range(3):
            bound = bounds[:, d].reshape((seqs,) + (1,) * positions.ndim)
            found = jnp.maximum(found, jnp.where(bound <= positions[None], bound, 0))
        return found

    firsts = jnp.arange(groups, dtype=jnp.int32) * block
    reach = jnp.max(firsts[None] - start_of(firsts)) - block
    chunks = jnp.maximum(reach + HALO_CHUNK - 1, 0) // HALO_CHUNK
    chunks = max_over(chunks[None], "fsdp")[0]
    count = sum_over(facts[-1:], "fsdp")[0].astype(F32)
    base = (place - (groups - 1)) * block
    starts = start_of(place * block + jnp.arange(block, dtype=jnp.int32)) - base
    low_rows = starts[:, ::QUERY_TILE]
    low = (low_rows // KEY_TILE).reshape(-1)
    low_tile = starts[:, 0] // ROW_TILE
    first = low_tile * (ROW_TILE // KEY_TILE)
    starts = starts[:, None, :]

    halo = jnp.concatenate([jnp.zeros((seqs, far_rows, width), BF16), near], 1)

    def fetch(state):
        j, halo = state
        sent = lax.dynamic_slice_in_dim(halo, halo_rows - HALO_CHUNK * (j + 1), HALO_CHUNK, 1)
        came = shift(sent, "seq", 1)
        return j + 1, lax.dynamic_update_slice_in_dim(
            halo, came, far_rows - HALO_CHUNK * (j + 1), 1
        )

    if far_rows > 0:
        _, halo = lax.while_loop(lambda state: state[0] < chunks, fetch, (jnp.int32(0), halo))

    normed, query, keys, values = project(
        low_tile, order, halo, tokens, gain1, shift1, bias1, qkv_pieces
    )
    mixed, logs = attend(low, query, keys, values, starts)

    factor = (rows * owners * groups) / count
    (
        layer_out,
        gresid,
        gmixed,
        normed2,
        active,
        ghidden,
        gmlp,
        gbranch,
        sums,
        upsums,
    ) = mlp(
        order,
        factor.reshape(1),
        mixed.reshape(rows, width),
        tokens.reshape(rows, width),
        teacher.reshape(rows, width),
        weight.reshape(rows, 1),
        (outbias_v, gain2, shift2, upbias, downbias),
        out_pieces,
        up_pieces,
        down_pieces,
    )

    def outer(left, right):
        return lax.dot_general(left, right, TN, preferred_element_type=F32).astype(BF16)

    grad_down = reduce_rows(outer(active, gmlp).reshape(owners, hidden // owners, width))
    grad_up = reduce_rows(outer(normed2, ghidden).reshape(owners, width // owners, hidden))
    grad_merge = reduce_rows(
        outer(mixed.reshape(rows, width), gbranch).reshape(owners, width // owners, width)
    )
    small = jnp.concatenate([sums[:4].reshape(-1), upsums[0], jnp.sum(sums[4:5], 1)])
    small = sum_over(sum_over(small, "seq"), "fsdp")

    gquery, gkeys, gvalues = attend_back(
        low, first, query, keys, values, starts, mixed, gmixed.reshape(seqs, block, width), logs
    )
    ghalo, halo_sums = halo_back(low_tile, order, halo, gkeys, gvalues, qkv_pieces)

    def give(state):
        j, ghalo = state
        j = j - 1
        sent = lax.dynamic_slice_in_dim(ghalo, far_rows - HALO_CHUNK * (j + 1), HALO_CHUNK, 1)
        came = shift(sent, "seq", -1)
        spot = halo_rows - HALO_CHUNK * (j + 1)
        held = lax.dynamic_slice_in_dim(ghalo, spot, HALO_CHUNK, 1)
        total = (held.astype(F32) + came.astype(F32)).astype(BF16)
        return j, lax.dynamic_update_slice_in_dim(ghalo, total, spot, 1)

    if far_rows > 0:
        _, ghalo = lax.while_loop(lambda state: state[0] > 0, give, (chunks, ghalo))
    more = shift(ghalo[:, far_rows:], "seq", -1)

    gnormed, gweight, own_sums = own_back(
        low_tile, order, tokens, normed, gquery, gkeys, gvalues, qkv_pieces
    )
    late = jnp.concatenate([(own_sums[:2] + halo_sums[:2]).reshape(-1), own_sums[2:4].reshape(-1)])
    late = sum_over(sum_over(late, "seq"), "fsdp")
    grad_joint = reduce_rows(gweight.reshape(owners, width // owners, 3 * width))

    grad_tokens = finish(
        tokens.reshape(rows, width),
        gnormed.reshape(rows, width),
        more.reshape(rows, width),
        gresid,
        gain1,
    ).reshape(tokens.shape)

    def own_part(vector, at, size):
        share = size // owners
        return lax.dynamic_slice_in_dim(vector, at + me * share, share)

    loss = small[-1] / (width * count)
    return (
        loss,
        layer_out.reshape(tokens.shape),
        grad_tokens,
        own_part(late, 0, width),
        own_part(late, width, width),
        grad_joint,
        own_part(late, 2 * width, 2 * width),
        grad_merge,
        own_part(small, 0, width),
        own_part(small, width, width),
        own_part(small, 2 * width, width),
        grad_up,
        own_part(small, 4 * width, hidden),
        grad_down,
        own_part(small, 3 * width, width),
    )


def solution(mesh):
    placed = (
        P("fsdp", "seq", None),
        P("fsdp", "seq", None),
        P("fsdp", "seq"),
        P("fsdp", "seq"),
        P("fsdp", "seq"),
        P("fsdp"),
        P("fsdp"),
        P("fsdp", None),
        P("fsdp"),
        P("fsdp", None),
        P("fsdp"),
        P("fsdp"),
        P("fsdp"),
        P("fsdp", None),
        P("fsdp"),
        P("fsdp", None),
        P("fsdp"),
    )
    return jax.shard_map(
        local,
        mesh=mesh,
        in_specs=placed,
        out_specs=(
            P(),
            P("fsdp", "seq", None),
            P("fsdp", "seq", None),
            P("fsdp"),
            P("fsdp"),
            P("fsdp", None),
            P("fsdp"),
            P("fsdp", None),
            P("fsdp"),
            P("fsdp"),
            P("fsdp"),
            P("fsdp", None),
            P("fsdp"),
            P("fsdp", None),
            P("fsdp"),
        ),
        check_vma=False,
    )
```

time: 1260 us -> 602 us (0.48); the launches traced: 1250 us -> 605 us
  matrix products: 356 us -> 20.7 us
  waiting for transfers between devices: 373 us -> 187 us
  Pallas kernels: 0 us -> 173 us
  other arithmetic: 177 us -> 26.9 us
  starting transfers between devices: 23.5 us -> 151 us
  local copies, waits for them, and re-layouts: 159 us -> 37.6 us
  blocking collectives: 112 us -> 0 us
  loops' own time: 24.8 us -> 0.04 us
    dot_general x68 -> x3, matrix products: 356 us -> 20.7 us  [outer(): lax.dot_general(left, right, TN, preferred_element_type=F32).astype(BF16)]
    all_to_all x5 -> x0, waiting for transfers between devices: 301 us -> none  [the longest x1 137 us: local(): lax.all_to_all(grad_joint_heads, 'seq', split_axis=1, concat_axis=3, tile...]
    ppermute x0 -> x81, waiting for transfers between devices: none -> 187 us  [the longest x77 166 us: swap(): return lax.ppermute(x, axis, [(i, i ^ bit) for i in range(size)])]
    pallas_call x0 -> x7, Pallas kernels: none -> 173 us  [the longest x1 51.1 us: mlp(): pl.pallas_call(functools.partial(mlp_kernel, counts), grid_spec=pltpu.Pre...]
    ppermute x0 -> x81, starting transfers between devices: none -> 151 us  [the longest x77 141 us: swap(): return lax.ppermute(x, axis, [(i, i ^ bit) for i in range(size)])]
    convert_element_type x31 -> x22, other arithmetic: 111 us -> 13.8 us  [the longest x4 7.3 us: reduce_rows(): mine = (pick(pairs, core, 1).astype(F32) + other.astype(F32)).astype(BF16)]
    all_to_all x7 -> x0, local copies, waits for them, and re-layouts: 54.9 us -> none  [the longest x2 26.3 us: local(): lax.all_to_all(grad_joint_heads, 'seq', split_axis=1, concat_axis=3, tile...]
    unnamed x2 -> x0, blocking collectives: 51.7 us -> none
  transfers between devices with their start and end apart: 14 -> 81, of which waited for: 6 -> 31; matrix products, arithmetic and copies ran while one was open for 48% -> 12% of each run, Pallas kernels for 0% -> 20%
where the time goes in v1:
time: 602 us; the launch traced here: 605 us
  waiting for transfers between devices  187 us (31%)
  Pallas kernels  173 us (29%)
  starting transfers between devices  151 us (25%)
  local copies, waits for them, and re-layouts  37.6 us (6%)
  other arithmetic  26.9 us (4%)
  matrix products  20.7 us (3%)
  between operations  9.12 us (2%)
    ppermute x77, waiting for transfers between devices, swap(): return lax.ppermute(x, axis, [(i, i ^ bit) for i in range(size)])  166 us
    ppermute x77, starting transfers between devices, swap(): return lax.ppermute(x, axis, [(i, i ^ bit) for i in range(size)])  141 us
    pallas_call x1, Pallas kernels, mlp(): pl.pallas_call(functools.partial(mlp_kernel, counts), grid_spec=pltpu.Pre...  51.1 us
    pallas_call x1, Pallas kernels, attend_back(): pl.pallas_call(functools.partial(attend_back_kernel, length - block), gri...  40.5 us
    pallas_call x1, Pallas kernels, attend(): pl.pallas_call(functools.partial(attend_kernel, length - block), grid_spe...  35.8 us
    ppermute x4, waiting for transfers between devices, shift(): lax.ppermute(x, axis, [(i, i + step) for i in range(size) if 0 <= i + ste...  20.8 us
    dot_general x3, matrix products, outer(): lax.dot_general(left, right, TN, preferred_element_type=F32).astype(BF16)  20.7 us
    pallas_call x1, Pallas kernels, own_back(): pl.pallas_call(functools.partial(own_back_kernel, halo_tiles, len(pieces)...  17.5 us
  transfers between devices with their start and end apart: 81, of which 31 were waited for; matrix products, arithmetic and copies ran while one was open for 12% of the time, Pallas kernels for 20%

profile of v1, /device:TPU:0, one launch (start us, length us, event | category | flops | bytes accessed | tf_op | source)
XLA Modules:
  0.0 605.2 jit_solution(9770189942616347478)
XLA Ops:
  63.1 8.7 %collective-permute-done.16.rest_3_ = bf16[96,2304]{1,0:T(8,128)(2,1)S(1)} collective-permute-done((bf16[96,2304]{1,0:T(8,128)(2,1)}, bf16[96,2304]{1,0:T(8,128)(2,1)S(1)}, u32[]{:S(2)}, u32[]{:S(2)}) %collective-permute-start.16) | collective-permute-done | bytes 442400 | tf_op jit(solution)/shard_map/ppermute | solution.py:742
  87.6 9.6 %collective-permute-done.30.rest_11_ = bf16[96,3072]{1,0:T(8,128)(2,1)S(1)} collective-permute-done((bf16[96,3072]{1,0:T(8,128)(2,1)}, bf16[96,3072]{1,0:T(8,128)(2,1)S(1)}, u32[]{:S(2)}, u32[]{:S(2)}) %collective-permute-start.30) | collective-permute-done | bytes 589856 | tf_op jit(solution)/shard_map/ppermute | solution.py:742
  97.2 10.6 %collective-permute-done.35.rest_17_ = bf16[384,768]{1,0:T(8,128)(2,1)S(1)} collective-permute-done((bf16[384,768]{1,0:T(8,128)(2,1)}, bf16[384,768]{1,0:T(8,128)(2,1)S(1)}, u32[]{:S(2)}, u32[]{:S(2)}) %collective-permute-start.35) | collective-permute-done | bytes 589856 | tf_op jit(solution)/shard_map/ppermute | solution.py:742
  112.0 14.7 %while.22 = (s32[]{:T(128)}, bf16[2,1536,768]{2,1,0:T(8,128)(2,1)}, s32[]{:T(128)}, s32[]{:T(128)}, s32[]{:T(128)}, /*index=5*/s32[]{:T(128)}, s32[]{:T(128)}, s32[]{:T(128)}, s32[]{:T(128)}, s32[]{:T(128)}) while((s32[]{:T(128)}, bf16[2,1536,768]{2,1,0:T(8,128)(2,1)}, s32[]{:T(128)}, s32[]{:T(128)}, s32[]{:T(128)}, /*index=5*/s32[]{:T(128)}, ...), condition=%wide.region_4.5_spmd, body=%wide.region_3.4_spmd.sunk | while | flops 11 | bytes 3145981 | solution.py:918
  117.6 8.4 %collective-permute-done = bf16[2,128,768]{2,1,0:T(8,128)(2,1)S(1)} collective-permute-done((bf16[2,128,768]{2,1,0:T(8,128)(2,1)S(1)}, bf16[2,128,768]{2,1,0:T(8,128)(2,1)S(1)}, u32[]{:S(2)}, u32[]{:S(2)}) %collective-permute-start) | collective-permute-done | bytes 393248 | tf_op jit(solution)/shard_map/while/body/ppermute | solution.py:747
  132.1 11.8 %project.1 = (bf16[2,2048,768]{2,1,0:T(8,128)(2,1)}, bf16[2,512,768]{2,1,0:T(8,128)(2,1)}, bf16[2,2048,768]{2,1,0:T(8,128)(2,1)}, bf16[2,2048,768]{2,1,0:T(8,128)(2,1)}) custom-call(s32[2]{0:T(128)} %get-tuple-element.136.low_ref, s32[8]{0:T(128)} %stack.35.order_ref, bf16[2,1536,768]{2,1,0:T(8,128)(2,1)} %get-tuple-element.96.halo_ref, ...), custom_call_target="tpu_custom_call" | custom-call | flops 6039797760 | bytes 25165824 | tf_op jit(solution)/shard_map/project/pallas_call | solution.py:108
  145.6 35.8 %attend.1 = (bf16[2,512,768]{2,1,0:T(8,128)(2,1)}, f32[2,6,2,512]{3,2,1,0:T(2,128)}) custom-call(s32[4]{0:T(128)} %reshape.486.low_ref, bf16[2,512,768]{2,1,0:T(8,128)(2,1)} %get-tuple-element.97.query_ref, bf16[2,2048,768]{2,1,0:T(8,128)(2,1)} %get-tuple-element.98.key_ref, bf16[2,2048,768]{2,1,0:T(8,128)(2,1)} %get-tuple-element.99.value_ref, ...), custom_call_target="tpu_custom_call" | custom-call | flops 17179869184 | bytes 16777216 | tf_op jit(solution)/shard_map/attend/pallas_call | solution.py:219
  181.4 51.1 %mlp.1 = (bf16[1024,768]{1,0:T(8,128)(2,1)}, f32[1024,768]{1,0:T(8,128)}, bf16[1024,768]{1,0:T(8,128)(2,1)}, bf16[1024,768]{1,0:T(8,128)(2,1)}, bf16[1024,3072]{...) custom-call(s32[8]{0:T(128)} %stack.35.order_ref, ...), custom_call_target="tpu_custom_call" | custom-call | flops 21743271936 | bytes 41943040 | tf_op jit(solution)/shard_map/mlp/pallas_call | solution.py:477
  238.1 40.5 %attend_back.1 = (bf16[2,512,768]{2,1,0:T(8,128)(2,1)}, bf16[2,2048,768]{2,1,0:T(8,128)(2,1)}, bf16[2,2048,768]{2,1,0:T(8,128)(2,1)}) custom-call(s32[4]{0:T(128)} %reshape.486.low_ref, s32[2]{0:T(128)} %get-tuple-element.135.first_ref, bf16[2,512,768]{2,1,0:T(8,128)(2,1)} %get-tuple-element.97.query_ref, bf16[2,2048,768]{2,1,0:T(8,128)(2,1)} %get-tuple-element.98.key_ref, ...), custom_call_target="tpu_custom_call" | custom-call | flops 42949672960 | bytes 29360128 | tf_op jit(solution)/shard_map/attend_back/pallas_call | solution.py:312
  278.6 9.7 %halo_back.1 = (bf16[2,1536,768]{2,1,0:T(8,128)(2,1)}, f32[8,768]{1,0:T(8,128)}) custom-call(s32[2]{0:T(128)} %get-tuple-element.136.low_ref, s32[8]{0:T(128)} %stack.35.order_ref, bf16[2,1536,768]{2,1,0:T(8,128)(2,1)} %get-tuple-element.96.halo_ref, bf16[2,2048,768]{2,1,0:T(8,128)(2,1)} %get-tuple-element.108.gkey_ref, ...), custom_call_target="tpu_custom_call" | custom-call | flops 4294967296 | bytes 16777216 | tf_op jit(solution)/shard_map/halo_back/pallas_call | solution.py:589
  288.4 17.5 %own_back.1 = (f32[2,512,768]{2,1,0:T(8,128)}, bf16[768,2304]{1,0:T(8,128)(2,1)}, f32[8,768]{1,0:T(8,128)}) custom-call(s32[2]{0:T(128)} %get-tuple-element.136.low_ref, s32[8]{0:T(128)} %stack.35.order_ref, bf16[2,512,768]{2,1,0:T(8,128)(2,1)} %own_ref.3, bf16[2,2048,768]{2,1,0:T(8,128)(2,1)} %get-tuple-element.104.normed_ref, ...), custom_call_target="tpu_custom_call" | custom-call | flops 17179869184 | bytes 25165824 | tf_op jit(solution)/shard_map/own_back/pallas_call | solution.py:681
  306.7 29.6 %collective-permute-start.48 = (f32[3072]{0:T(1024)S(1)}, f32[3072]{0:T(1024)S(1)}, u32[]{:S(2)}, u32[]{:S(2)}) collective-permute-start(f32[3072]{0:T(1024)S(1)} %constant_dynamic-update-slice_fusion.1), channel_id=1, source_target_pairs={{0,1},{1,0},{2,3},{3,2},{4,5},{5,4},{6,7},{7,6},{8,9},{9,8},{10,11... | collective-permute-start | bytes 36872 | tf_op jit(solution)/shard_map/ppermute | solution.py:742
  338.0 9.3 %convolution_convert_fusion = bf16[3072,768]{1,0:T(8,128)(2,1)} fusion(bf16[1024,3072]{1,0:T(8,128)(2,1)} %get-tuple-element.120, bf16[1024,768]{1,0:T(8,128)(2,1)} %get-tuple-element.121), kind=kOutput, calls=%fused_computation.5 | convolution fusion | flops 4834197504 | bytes 12582912 | tf_op jit(solution)/shard_map/dot_general | solution.py:951
  347.2 8.1 %convolution_convert_fusion.1 = bf16[768,3072]{1,0:T(8,128)(2,1)S(1)} fusion(bf16[1024,768]{1,0:T(8,128)(2,1)S(1)} %copy-done.26, bf16[1024,3072]{1,0:T(8,128)(2,1)} %get-tuple-element.119), kind=kOutput, calls=%fused_computation.6 | convolution fusion | flops 4834197504 | bytes 12582912 | tf_op jit(solution)/shard_map/dot_general | solution.py:951
  358.9 34.3 %collective-permute-start.49 = (f32[3072]{0:T(1024)S(1)}, f32[3072]{0:T(1024)S(1)}, u32[]{:S(2)}, u32[]{:S(2)}) collective-permute-start(f32[3072]{0:T(1024)S(1)} %add.338), channel_id=1, source_target_pairs={{0,2},{1,3},{2,0},{3,1},{4,6},{5,7},{6,4},{7,5},{8,10},{9,11},{10,... | collective-permute-start | bytes 36872 | tf_op jit(solution)/shard_map/ppermute | solution.py:742
  402.3 8.8 %collective-permute-start.53 = (bf16[4,96,2304]{2,1,0:T(8,128)(2,1)}, bf16[4,96,2304]{2,1,0:T(8,128)(2,1)S(1)}, u32[]{:S(2)}, u32[]{:S(2)}) collective-permute-start(bf16[4,96,2304]{2,1,0:T(8,128)(2,1)} %dynamic-slice_bitcast_fusion.2), channel_id=1, source_target_pairs={{0,4},{4,0},{8,12},{12,8},{16,20},{20,16},{24,28},{28,24},{1,5},{5... | collective-permute-start | bytes 5308424 | tf_op jit(solution)/shard_map/ppermute | solution.py:742
  412.2 16.6 %while.23 = (s32[]{:T(128)}, bf16[2,1536,768]{2,1,0:T(8,128)(2,1)}, s32[]{:T(128)}, s32[]{:T(128)}, s32[]{:T(128)}, /*index=5*/s32[]{:T(128)}, s32[]{:T(128)}, s32[]{:T(128)}, s32[]{:T(128)}) while((s32[]{:T(128)}, bf16[2,1536,768]{2,1,0:T(8,128)(2,1)}, s32[]{:T(128)}, s32[]{:T(128)}, s32[]{:T(128)}, /*index=5*/s32[]{:T(128)}, s32[]{:T(128)}, ...), condition=%wide.region_7.8_spmd, body=%wide.region_6.7_spmd.sunk | while | flops 786443 | bytes 3539189 | solution.py:977
  414.6 12.4 %collective-permute-done.1 = bf16[2,128,768]{2,1,0:T(8,128)(2,1)S(1)} collective-permute-done((bf16[2,128,768]{2,1,0:T(8,128)(2,1)S(1)}, bf16[2,128,768]{2,1,0:T(8,128)(2,1)S(1)}, u32[]{:S(2)}, u32[]{:S(2)}) %collective-permute-start.1) | collective-permute-done | bytes 393248 | tf_op jit(solution)/shard_map/while/body/ppermute | solution.py:747
  441.9 30.9 %collective-permute-done.65 = bf16[48,768]{1,0:T(8,128)(2,1)S(1)} collective-permute-done((bf16[48,768]{1,0:T(8,128)(2,1)S(1)}, bf16[48,768]{1,0:T(8,128)(2,1)S(1)}, u32[]{:S(2)}, u32[]{:S(2)}) %collective-permute-start.65) | collective-permute-done | bytes 73760 | tf_op jit(solution)/shard_map/ppermute | solution.py:742
  511.5 7.9 %collective-permute-done.75 = bf16[384,768]{1,0:T(8,128)(2,1)S(1)} collective-permute-done((bf16[384,768]{1,0:T(8,128)(2,1)S(1)}, bf16[384,768]{1,0:T(8,128)(2,1)S(1)}, u32[]{:S(2)}, u32[]{:S(2)}) %collective-permute-start.75) | collective-permute-done | bytes 589856 | tf_op jit(solution)/shard_map/ppermute | solution.py:742
  521.0 12.9 %collective-permute-done.76 = bf16[384,768]{1,0:T(8,128)(2,1)S(1)} collective-permute-done((bf16[384,768]{1,0:T(8,128)(2,1)S(1)}, bf16[384,768]{1,0:T(8,128)(2,1)S(1)}, u32[]{:S(2)}, u32[]{:S(2)}) %collective-permute-start.76) | collective-permute-done | bytes 589856 | tf_op jit(solution)/shard_map/ppermute | solution.py:742
  536.3 8.4 %collective-permute-done.68 = bf16[96,3072]{1,0:T(8,128)(2,1)S(1)} collective-permute-done((bf16[96,3072]{1,0:T(8,128)(2,1)S(1)}, bf16[96,3072]{1,0:T(8,128)(2,1)S(1)}, u32[]{:S(2)}, u32[]{:S(2)}) %collective-permute-start.68) | collective-permute-done | bytes 589856 | tf_op jit(solution)/shard_map/ppermute | solution.py:742
  544.7 8.6 %collective-permute-done.69 = bf16[96,3072]{1,0:T(8,128)(2,1)S(1)} collective-permute-done((bf16[96,3072]{1,0:T(8,128)(2,1)S(1)}, bf16[96,3072]{1,0:T(8,128)(2,1)S(1)}, u32[]{:S(2)}, u32[]{:S(2)}) %collective-permute-start.69) | collective-permute-done | bytes 589856 | tf_op jit(solution)/shard_map/ppermute | solution.py:742
  563.3 13.8 %collective-permute-done.58 = bf16[48,2304]{1,0:T(8,128)(2,1)S(1)} collective-permute-done((bf16[48,2304]{1,0:T(8,128)(2,1)S(1)}, bf16[48,2304]{1,0:T(8,128)(2,1)S(1)}, u32[]{:S(2)}, u32[]{:S(2)}) %collective-permute-start.58) | collective-permute-done | bytes 221216 | tf_op jit(solution)/shard_map/ppermute | solution.py:742
  (315 shorter events, 207.4 us)
Async XLA Ops:
  0.6 50.7 %collective-permute-start.21 = (bf16[96,768]{1,0:T(8,128)(2,1)}, bf16[96,768]{1,0:T(8,128)(2,1)S(1)}, u32[]{:S(2)}, u32[]{:S(2)}) collective-permute-start(bf16[96,768]{1,0:T(8,128)(2,1)} %rest_0_.5), channel_id=1, source_target_pairs={{0,8},{4,12},{8,0},{12,4},{16,24},{20,28},{24,16},{28,20},{1,9},{5... | collective-permute-start | bytes 442376 | tf_op jit(solution)/shard_map/ppermute | solution.py:742
  3.6 49.6 %collective-permute-start.22 = (bf16[96,768]{1,0:T(8,128)(2,1)}, bf16[96,768]{1,0:T(8,128)(2,1)S(1)}, u32[]{:S(2)}, u32[]{:S(2)}) collective-permute-start(bf16[96,768]{1,0:T(8,128)(2,1)} %rest_0_.5), channel_id=1, source_target_pairs={{0,16},{4,20},{8,24},{12,28},{16,0},{20,4},{24,8},{28,12},{1,17},{... | collective-permute-start | bytes 442376 | tf_op jit(solution)/shard_map/ppermute | solution.py:742
  5.2 48.1 %collective-permute-start.23 = (bf16[96,768]{1,0:T(8,128)(2,1)}, bf16[96,768]{1,0:T(8,128)(2,1)S(1)}, u32[]{:S(2)}, u32[]{:S(2)}) collective-permute-start(bf16[96,768]{1,0:T(8,128)(2,1)} %rest_0_.5), channel_id=1, source_target_pairs={{0,24},{4,28},{8,16},{12,20},{16,8},{20,12},{24,0},{28,4},{1,25},{... | collective-permute-start | bytes 442376 | tf_op jit(solution)/shard_map/ppermute | solution.py:742
  37.3 47.2 %collective-permute-start.7 = (bf16[2,512,768]{2,1,0:T(8,128)(2,1)}, bf16[2,512,768]{2,1,0:T(8,128)(2,1)S(1)}, u32[]{:S(2)}, u32[]{:S(2)}) collective-permute-start(bf16[2,512,768]{2,1,0:T(8,128)(2,1)} %own_ref.3), channel_id=1, source_target_pairs={{0,1},{1,2},{2,3},{4,5},{5,6},{6,7},{8,9},{9,10},{10,11},{12,13},{... | collective-permute-start | bytes 4718600 | tf_op jit(solution)/shard_map/ppermute | solution.py:747
  73.3 34.5 %collective-permute-start.35 = (bf16[384,768]{1,0:T(8,128)(2,1)}, bf16[384,768]{1,0:T(8,128)(2,1)S(1)}, u32[]{:S(2)}, u32[]{:S(2)}) collective-permute-start(bf16[384,768]{1,0:T(8,128)(2,1)} %rest_16_.1), channel_id=1, source_target_pairs={{0,8},{4,12},{8,0},{12,4},{16,24},{20,28},{24,16},{28,20},{1,9},{5... | collective-permute-start | bytes 1769480 | tf_op jit(solution)/shard_map/ppermute | solution.py:742
  97.1 46.8 %collective-permute-start.36 = (bf16[384,768]{1,0:T(8,128)(2,1)}, bf16[384,768]{1,0:T(8,128)(2,1)}, u32[]{:S(2)}, u32[]{:S(2)}) collective-permute-start(bf16[384,768]{1,0:T(8,128)(2,1)} %rest_16_.1), channel_id=1, source_target_pairs={{0,16},{4,20},{8,24},{12,28},{16,0},{20,4},{24,8},{28,12},{1,17},{... | collective-permute-start | bytes 1769480 | tf_op jit(solution)/shard_map/ppermute | solution.py:742
  107.8 36.7 %collective-permute-start.37 = (bf16[384,768]{1,0:T(8,128)(2,1)}, bf16[384,768]{1,0:T(8,128)(2,1)}, u32[]{:S(2)}, u32[]{:S(2)}) collective-permute-start(bf16[384,768]{1,0:T(8,128)(2,1)} %rest_16_.1), channel_id=1, source_target_pairs={{0,24},{4,28},{8,16},{12,20},{16,8},{20,12},{24,0},{28,4},{1,25},{... | collective-permute-start | bytes 1769480 | tf_op jit(solution)/shard_map/ppermute | solution.py:742
  110.5 34.6 %collective-permute-start.38 = (bf16[384,768]{1,0:T(8,128)(2,1)}, bf16[384,768]{1,0:T(8,128)(2,1)}, u32[]{:S(2)}, u32[]{:S(2)}) collective-permute-start(bf16[384,768]{1,0:T(8,128)(2,1)} %rest_16_.1), channel_id=1, source_target_pairs={{0,4},{4,0},{8,12},{12,8},{16,20},{20,16},{24,28},{28,24},{1,5},{5... | collective-permute-start | bytes 1769480 | tf_op jit(solution)/shard_map/ppermute | solution.py:742
  144.0 37.4 %collective-permute-start.33 = (bf16[96,3072]{1,0:T(8,128)(2,1)}, bf16[96,3072]{1,0:T(8,128)(2,1)}, u32[]{:S(2)}, u32[]{:S(2)}) collective-permute-start(bf16[96,3072]{1,0:T(8,128)(2,1)} %collective-permute-done.29.rest_10_), channel_id=1, source_target_pairs={{0,4},{4,0},{8,12},{12,8},{16,20},{20,16},{24,28},{28,24},{1,5},{5... | collective-permute-start | bytes 1769480 | tf_op jit(solution)/shard_map/ppermute | solution.py:742
  144.5 36.8 %collective-permute-start.34 = (bf16[96,3072]{1,0:T(8,128)(2,1)S(1)}, bf16[96,3072]{1,0:T(8,128)(2,1)}, u32[]{:S(2)}, u32[]{:S(2)}) collective-permute-start(bf16[96,3072]{1,0:T(8,128)(2,1)S(1)} %copy-done.17), channel_id=1, source_target_pairs={{0,4},{4,0},{8,12},{12,8},{16,20},{20,16},{24,28},{28,24},{1,5},{5... | collective-permute-start | bytes 1769480 | tf_op jit(solution)/shard_map/ppermute | solution.py:742
  144.6 36.7 %collective-permute-start.39 = (bf16[384,768]{1,0:T(8,128)(2,1)S(1)}, bf16[384,768]{1,0:T(8,128)(2,1)}, u32[]{:S(2)}, u32[]{:S(2)}) collective-permute-start(bf16[384,768]{1,0:T(8,128)(2,1)S(1)} %copy-done.19), channel_id=1, source_target_pairs={{0,4},{4,0},{8,12},{12,8},{16,20},{20,16},{24,28},{28,24},{1,5},{5... | collective-permute-start | bytes 1769480 | tf_op jit(solution)/shard_map/ppermute | solution.py:742
  145.1 36.3 %collective-permute-start.40 = (bf16[384,768]{1,0:T(8,128)(2,1)}, bf16[384,768]{1,0:T(8,128)(2,1)}, u32[]{:S(2)}, u32[]{:S(2)}) collective-permute-start(bf16[384,768]{1,0:T(8,128)(2,1)} %collective-permute-done.36.rest_18_), channel_id=1, source_target_pairs={{0,4},{4,0},{8,12},{12,8},{16,20},{20,16},{24,28},{28,24},{1,5},{5... | collective-permute-start | bytes 1769480 | tf_op jit(solution)/shard_map/ppermute | solution.py:742
  145.2 36.2 %collective-permute-start.41 = (bf16[384,768]{1,0:T(8,128)(2,1)}, bf16[384,768]{1,0:T(8,128)(2,1)}, u32[]{:S(2)}, u32[]{:S(2)}) collective-permute-start(bf16[384,768]{1,0:T(8,128)(2,1)} %collective-permute-done.37.rest_19_), channel_id=1, source_target_pairs={{0,4},{4,0},{8,12},{12,8},{16,20},{20,16},{24,28},{28,24},{1,5},{5... | collective-permute-start | bytes 1769480 | tf_op jit(solution)/shard_map/ppermute | solution.py:742
  237.9 156.0 %collective-permute-start.60 = (bf16[4,96,768]{2,1,0:T(8,128)(2,1)S(1)}, bf16[4,96,768]{2,1,0:T(8,128)(2,1)}, u32[]{:S(2)}, u32[]{:S(2)}) collective-permute-start(bf16[4,96,768]{2,1,0:T(8,128)(2,1)S(1)} %dynamic-slice_bitcast_fusion.9), channel_id=1, source_target_pairs={{0,4},{4,0},{8,12},{12,8},{16,20},{20,16},{24,28},{28,24},{1,5},{5... | collective-permute-start | bytes 1769480 | tf_op jit(solution)/shard_map/ppermute | solution.py:742
  306.7 52.2 %collective-permute-start.48 = (f32[3072]{0:T(1024)S(1)}, f32[3072]{0:T(1024)S(1)}, u32[]{:S(2)}, u32[]{:S(2)}) collective-permute-start(f32[3072]{0:T(1024)S(1)} %constant_dynamic-update-slice_fusion.1), channel_id=1, source_target_pairs={{0,1},{1,0},{2,3},{3,2},{4,5},{5,4},{6,7},{7,6},{8,9},{9,8},{10,11... | collective-permute-start | bytes 36872 | tf_op jit(solution)/shard_map/ppermute | solution.py:742
  337.9 55.3 %collective-permute-start.42 = (f32[6145]{0:T(1024)S(1)}, f32[6145]{0:T(1024)S(1)}, u32[]{:S(2)}, u32[]{:S(2)}) collective-permute-start(f32[6145]{0:T(1024)S(1)} %pad_maximum_fusion), channel_id=1, source_target_pairs={{0,1},{1,0},{2,3},{3,2},{4,5},{5,4},{6,7},{7,6},{8,9},{9,8},{10,11... | collective-permute-start | bytes 73748 | tf_op jit(solution)/shard_map/ppermute | solution.py:742
  358.9 43.4 %collective-permute-start.49 = (f32[3072]{0:T(1024)S(1)}, f32[3072]{0:T(1024)S(1)}, u32[]{:S(2)}, u32[]{:S(2)}) collective-permute-start(f32[3072]{0:T(1024)S(1)} %add.338), channel_id=1, source_target_pairs={{0,2},{1,3},{2,0},{3,1},{4,6},{5,7},{6,4},{7,5},{8,10},{9,11},{10,... | collective-permute-start | bytes 36872 | tf_op jit(solution)/shard_map/ppermute | solution.py:742
  402.3 70.8 %collective-permute-start.53 = (bf16[4,96,2304]{2,1,0:T(8,128)(2,1)}, bf16[4,96,2304]{2,1,0:T(8,128)(2,1)S(1)}, u32[]{:S(2)}, u32[]{:S(2)}) collective-permute-start(bf16[4,96,2304]{2,1,0:T(8,128)(2,1)} %dynamic-slice_bitcast_fusion.2), channel_id=1, source_target_pairs={{0,4},{4,0},{8,12},{12,8},{16,20},{20,16},{24,28},{28,24},{1,5},{5... | collective-permute-start | bytes 5308424 | tf_op jit(solution)/shard_map/ppermute | solution.py:742
  430.3 51.5 %collective-permute-start.47 = (bf16[2,512,768]{2,1,0:T(8,128)(2,1)S(1)}, bf16[2,512,768]{2,1,0:T(8,128)(2,1)}, u32[]{:S(2)}, u32[]{:S(2)}) collective-permute-start(bf16[2,512,768]{2,1,0:T(8,128)(2,1)S(1)} %slice.91), channel_id=1, source_target_pairs={{1,0},{2,1},{3,2},{5,4},{6,5},{7,6},{9,8},{10,9},{11,10},{13,12},{... | collective-permute-start | bytes 4718600 | tf_op jit(solution)/shard_map/ppermute | solution.py:747
  434.1 38.6 %collective-permute-start.65 = (bf16[48,768]{1,0:T(8,128)(2,1)S(1)}, bf16[48,768]{1,0:T(8,128)(2,1)S(1)}, u32[]{:S(2)}, u32[]{:S(2)}) collective-permute-start(bf16[48,768]{1,0:T(8,128)(2,1)S(1)} %fusion.24), channel_id=1, source_target_pairs={{0,2},{1,3},{2,0},{3,1},{4,6},{5,7},{6,4},{7,5},{8,10},{9,11},{10,... | collective-permute-start | bytes 221192 | tf_op jit(solution)/shard_map/ppermute | solution.py:742
  441.3 58.5 %collective-permute-start.74 = (bf16[4,384,768]{2,1,0:T(8,128)(2,1)}, bf16[4,384,768]{2,1,0:T(8,128)(2,1)}, u32[]{:S(2)}, u32[]{:S(2)}) collective-permute-start(bf16[4,384,768]{2,1,0:T(8,128)(2,1)} %dynamic-slice_bitcast_fusion), channel_id=1, source_target_pairs={{0,4},{4,0},{8,12},{12,8},{16,20},{20,16},{24,28},{28,24},{1,5},{5... | collective-permute-start | bytes 7077896 | tf_op jit(solution)/shard_map/ppermute | solution.py:742
  441.4 65.3 %collective-permute-start.67 = (bf16[4,96,3072]{2,1,0:T(8,128)(2,1)}, bf16[4,96,3072]{2,1,0:T(8,128)(2,1)}, u32[]{:S(2)}, u32[]{:S(2)}) collective-permute-start(bf16[4,96,3072]{2,1,0:T(8,128)(2,1)} %dynamic-slice_bitcast_fusion.1), channel_id=1, source_target_pairs={{0,4},{4,0},{8,12},{12,8},{16,20},{20,16},{24,28},{28,24},{1,5},{5... | collective-permute-start | bytes 7077896 | tf_op jit(solution)/shard_map/ppermute | solution.py:742
  509.3 35.4 %collective-permute-start.68 = (bf16[96,3072]{1,0:T(8,128)(2,1)S(1)}, bf16[96,3072]{1,0:T(8,128)(2,1)S(1)}, u32[]{:S(2)}, u32[]{:S(2)}) collective-permute-start(bf16[96,3072]{1,0:T(8,128)(2,1)S(1)} %get-tuple-element.140), channel_id=1, source_target_pairs={{0,8},{4,12},{8,0},{12,4},{16,24},{20,28},{24,16},{28,20},{1,9},{5... | collective-permute-start | bytes 1769480 | tf_op jit(solution)/shard_map/ppermute | solution.py:742
  511.2 42.0 %collective-permute-start.69 = (bf16[96,3072]{1,0:T(8,128)(2,1)S(1)}, bf16[96,3072]{1,0:T(8,128)(2,1)S(1)}, u32[]{:S(2)}, u32[]{:S(2)}) collective-permute-start(bf16[96,3072]{1,0:T(8,128)(2,1)S(1)} %get-tuple-element.142), channel_id=1, source_target_pairs={{0,16},{4,20},{8,24},{12,28},{16,0},{20,4},{24,8},{28,12},{1,17},{... | collective-permute-start | bytes 1769480 | tf_op jit(solution)/shard_map/ppermute | solution.py:742
  (86 other events, 1178.3 us)

commit v2 on v1

--- a/solution.py
+++ b/solution.py
@@ -15,6 +15,7 @@
 QUERY_TILE = 256
 ROW_TILE = 256
 HALO_CHUNK = 128
+SHARES = 8
 VMEM_LIMIT = 62 * 1024 * 1024
 
 NT = (((1,), (1,)), ((), ()))
@@ -344,9 +345,35 @@
     )(low, first, query, keys, values, starts, mixed, grad, logs)
 
 
+def slab_copies(slab_ref, merge_ref, up_ref, down_ref, sems):
+    owners = slab_ref.shape[0]
+    width = slab_ref.shape[2]
+    rows = width // owners
+    chunks = up_ref.shape[1] // width
+    groups = [[], [], []]
+    for owner in range(owners):
+        here = pl.ds(owner * rows, rows)
+        groups[0].append((slab_ref.at[owner, pl.ds(0, rows), :], merge_ref.at[here, :]))
+        for c in range(chunks):
+            groups[1].append(
+                (
+                    slab_ref.at[owner, pl.ds((1 + c) * rows, rows), :],
+                    up_ref.at[here, pl.ds(c * width, width)],
+                )
+            )
+        groups[2].append(
+            (
+                slab_ref.at[owner, pl.ds((1 + chunks) * rows, chunks * rows), :],
+                down_ref.at[pl.ds(owner * chunks * rows, chunks * rows), :],
+            )
+        )
+    return [
+        [pltpu.make_async_copy(*pair, sems.at[k, n]) for n, pair in enumerate(group)]
+        for k, group in enumerate(groups)
+    ]
+
+
 def mlp_kernel(
-    counts,
-    order_ref,
     factor_ref,
     mixed_ref,
     token_ref,
@@ -357,39 +384,29 @@
     shift_ref,
     upbias_ref,
     downbias_ref,
-    *rest,
+    slab_ref,
+    layer_ref,
+    gresid_ref,
+    gmixed_ref,
+    normed_ref,
+    active_ref,
+    ghidden_ref,
+    gmlp_ref,
+    gbranch_ref,
+    sums_ref,
+    upsums_ref,
+    merge_ref,
+    up_ref,
+    down_ref,
+    slope_ref,
+    resid_ref,
+    total_ref,
+    sems,
 ):
-    out_pieces = rest[: counts[0]]
-    up_pieces = rest[counts[0] : counts[0] + counts[1]]
-    down_pieces = rest[counts[0] + counts[1] : sum(counts)]
-    (
-        layer_ref,
-        gresid_ref,
-        gmixed_ref,
-        normed_ref,
-        active_ref,
-        ghidden_ref,
-        gmlp_ref,
-        gbranch_ref,
-        sums_ref,
-        upsums_ref,
-        merge_ref,
-        up_ref,
-        down_ref,
-        slope_ref,
-        resid_ref,
-        total_ref,
-        sems,
-    ) = rest[sum(counts) :]
     width = token_ref.shape[-1]
     chunks = active_ref.shape[-1] // width
     step = pl.program_id(0)
-    copies = [
-        piece_copies(order_ref, pieces, whole, sems.at[k])
-        for k, (pieces, whole) in enumerate(
-            ((out_pieces, merge_ref), (up_pieces, up_ref), (down_pieces, down_ref))
-        )
-    ]
+    copies = slab_copies(slab_ref, merge_ref, up_ref, down_ref, sems)
 
     def arrive(k):
         @pl.when(step == 0)
@@ -465,19 +482,17 @@
     gmixed_ref[...] = dot(gbranch, merge_ref[...], NT).astype(BF16)
 
 
-def mlp(order, factor, mixed, tokens, teacher, weight, vectors, out_pieces, up_pieces, down_pieces):
+def mlp(factor, mixed, tokens, teacher, weight, vectors, slab):
     rows, width = tokens.shape
     outbias, gain, shift, upbias, downbias = vectors
     hidden = upbias.shape[1]
-    tile = lambda n: pl.BlockSpec((ROW_TILE, n), lambda i, order: (i, 0))
-    fixed = lambda m, n: pl.BlockSpec((m, n), lambda i, order: (0, 0))
-    pieces = [*out_pieces, *up_pieces, *down_pieces]
-    counts = (len(out_pieces), len(up_pieces), len(down_pieces))
+    tile = lambda n: pl.BlockSpec((ROW_TILE, n), lambda i: (i, 0))
+    fixed = lambda m, n: pl.BlockSpec((m, n), lambda i: (0, 0))
     shape = jax.ShapeDtypeStruct
     return pl.pallas_call(
-        functools.partial(mlp_kernel, counts),
+        mlp_kernel,
         grid_spec=pltpu.PrefetchScalarGridSpec(
-            num_scalar_prefetch=1,
+            num_scalar_prefetch=0,
             grid=(rows // ROW_TILE,),
             in_specs=[
                 pl.BlockSpec(memory_space=pltpu.SMEM),
@@ -490,8 +505,8 @@
                 fixed(1, width),
                 fixed(1, hidden),
                 fixed(1, width),
-            ]
-            + [pl.BlockSpec(memory_space=pl.ANY)] * len(pieces),
+                pl.BlockSpec(memory_space=pl.ANY),
+            ],
             out_specs=[
                 tile(width),
                 tile(width),
@@ -511,7 +526,7 @@
                 pltpu.VMEM((ROW_TILE, hidden), F32),
                 pltpu.VMEM((ROW_TILE, width), F32),
                 pltpu.VMEM((ROW_TILE, width), F32),
-                pltpu.SemaphoreType.DMA((3, max(counts))),
+                pltpu.SemaphoreType.DMA((3, slab.shape[0] * (hidden // width))),
             ],
         ),
         out_shape=[
@@ -533,20 +548,123 @@
             transcendentals=rows * hidden,
         ),
         name="mlp",
-    )(
-        order,
-        factor,
-        mixed,
-        tokens,
-        teacher,
-        weight,
-        outbias,
-        gain,
-        shift,
-        upbias,
-        downbias,
-        *pieces,
-    )
+    )(factor, mixed, tokens, teacher, weight, outbias, gain, shift, upbias, downbias, slab)
+
+
+def outer_kernel(
+    mixed_ref,
+    gbranch_ref,
+    normed_ref,
+    ghidden_ref,
+    active_ref,
+    gmlp_ref,
+    small_ref,
+    slab_ref,
+    split_ref,
+    block_ref,
+    small_sem,
+    split_sems,
+    block_sems,
+):
+    owners, rows, width = split_ref.shape[1:]
+    chunks = block_ref.shape[2] // rows
+    share = owners // chunks
+    step = pl.program_id(0)
+    small = pltpu.make_async_copy(
+        small_ref, slab_ref.at[:, pl.ds((1 + 2 * chunks) * rows, small_ref.shape[1]), :], small_sem
+    )
+
+    def split_copy(index):
+        return pltpu.make_async_copy(
+            split_ref.at[index % 2],
+            slab_ref.at[:, pl.ds(pl.multiple_of(index * rows, 16), rows), :],
+            split_sems.at[index % 2],
+        )
+
+    def block_copy(index):
+        return pltpu.make_async_copy(
+            block_ref.at[index % 2],
+            slab_ref.at[
+                pl.ds(index * share, share), pl.ds((1 + chunks) * rows, chunks * rows), :
+            ],
+            block_sems.at[index % 2],
+        )
+
+    @pl.when(step == 0)
+    def _():
+        small.start()
+        out = dot(mixed_ref[...], gbranch_ref[...], TN).astype(BF16)
+        split_ref[0] = out.reshape(owners, rows, width)
+        split_copy(0).start()
+
+    @pl.when((step >= 1) & (step <= chunks))
+    def _():
+        @pl.when(step >= 2)
+        def _():
+            split_copy(step - 2).wait()
+
+        out = dot(normed_ref[...], ghidden_ref[...], TN).astype(BF16)
+        split_ref[step % 2] = out.reshape(owners, rows, width)
+        split_copy(step).start()
+
+    @pl.when(step > chunks)
+    def _():
+        index = step - 1 - chunks
+
+        @pl.when(index >= 2)
+        def _():
+            block_copy(index - 2).wait()
+
+        out = dot(active_ref[...], gmlp_ref[...], TN).astype(BF16)
+        block_ref[index % 2] = out.reshape(share, chunks * rows, width)
+        block_copy(index).start()
+
+    @pl.when(step == 2 * chunks)
+    def _():
+        small.wait()
+        split_copy(chunks - 1).wait()
+        split_copy(chunks).wait()
+        block_copy(chunks - 2).wait()
+        block_copy(chunks - 1).wait()
+
+
+def outer_all(mixed, gbranch, normed, ghidden, active, gmlp, small):
+    tokens, width = mixed.shape
+    owners, extra, _ = small.shape
+    chunks = ghidden.shape[1] // width
+    rows = width // owners
+    whole = pl.BlockSpec((tokens, width), lambda i: (0, 0))
+    return pl.pallas_call(
+        outer_kernel,
+        grid=(1 + 2 * chunks,),
+        in_specs=[
+            whole,
+            whole,
+            whole,
+            pl.BlockSpec((tokens, width), lambda i: (0, jnp.clip(i - 1, 0, chunks - 1))),
+            pl.BlockSpec((tokens, width), lambda i: (0, jnp.clip(i - 1 - chunks, 0, chunks - 1))),
+            whole,
+            pl.BlockSpec((owners, extra, width), lambda i: (0, 0, 0)),
+        ],
+        out_specs=pl.BlockSpec(memory_space=pl.ANY),
+        out_shape=jax.ShapeDtypeStruct(
+            (owners, (1 + 2 * chunks) * rows + extra, width), BF16
+        ),
+        scratch_shapes=[
+            pltpu.VMEM((2, owners, rows, width), BF16),
+            pltpu.VMEM((2, owners // chunks, chunks * rows, width), BF16),
+            pltpu.SemaphoreType.DMA,
+            pltpu.SemaphoreType.DMA((2,)),
+            pltpu.SemaphoreType.DMA((2,)),
+        ],
+        compiler_params=pltpu.CompilerParams(vmem_limit_bytes=VMEM_LIMIT),
+        cost_estimate=pl.CostEstimate(
+            flops=2 * tokens * width * width * (1 + 2 * chunks),
+            bytes_accessed=30 << 20,
+            transcendentals=0,
+        ),
+        name="outer_all",
+    )(mixed, gbranch, normed, ghidden, active, gmlp, small)
 
 
 def halo_back_kernel(
@@ -715,26 +833,45 @@
     )(low, order, own, normed, gquery, gkeys, gvalues, *pieces)
 
 
-def finish_kernel(own_ref, gnormed_ref, more_ref, gresid_ref, gain_ref, out_ref):
-    unit, scale = norm_parts(own_ref[...].astype(F32))
-    grad = gnormed_ref[...] + more_ref[...].astype(F32)
-    out_ref[...] = (gresid_ref[...] + norm_back(grad, gain_ref[...], unit, scale)).astype(BF16)
-
-
-def finish(own, gnormed, more, gresid, gain):
-    rows, width = own.shape
-    tile = pl.BlockSpec((ROW_TILE, width), lambda i: (i, 0))
+def finish_kernel(seqs, own_ref, gnormed_ref, gresid_ref, gain_ref, *rest):
+    near_refs, far_refs = rest[:seqs], rest[seqs:-2]
+    out_ref, total_ref = rest[-2:]
+    unit, scale = norm_parts(own_ref[0].astype(F32))
+    for seq, near_ref in enumerate(near_refs):
+
+        @pl.when(pl.program_id(0) == seq)
+        def _():
+            total_ref[...] = gnormed_ref[0] + near_ref[...].astype(F32)
+
+    for far_ref in far_refs:
+
+        @pl.when(pl.program_id(1) == pl.num_programs(1) - 1)
+        def _():
+            total_ref[-HALO_CHUNK:, :] += far_ref[0].astype(F32)
+
+    out_ref[0] = (gresid_ref[0] + norm_back(total_ref[...], gain_ref[...], unit, scale)).astype(BF16)
+
+
+def finish(own, gnormed, near, far, gresid, gain):
+    seqs, block, width = own.shape
+    tile = pl.BlockSpec((1, ROW_TILE, width), lambda s, t: (s, t, 0))
+    last = pl.BlockSpec((1, HALO_CHUNK, width), lambda s, t: (s, 0, 0))
     return pl.pallas_call(
-        finish_kernel,
-        grid=(rows // ROW_TILE,),
-        in_specs=[tile, tile, tile, tile, pl.BlockSpec((1, width), lambda i: (0, 0))],
+        functools.partial(finish_kernel, seqs),
+        grid=(seqs, block // ROW_TILE),
+        in_specs=[tile, tile, tile, pl.BlockSpec((1, width), lambda s, t: (0, 0))]
+        + [pl.BlockSpec((ROW_TILE, width), lambda s, t: (t, 0))] * seqs
+        + [last] * len(far),
         out_specs=tile,
-        out_shape=jax.ShapeDtypeStruct((rows, width), BF16),
+        out_shape=jax.ShapeDtypeStruct(own.shape, BF16),
+        scratch_shapes=[pltpu.VMEM((ROW_TILE, width), F32)],
         cost_estimate=pl.CostEstimate(
-            flops=20 * rows * width, bytes_accessed=14 * rows * width, transcendentals=0
+            flops=20 * seqs * block * width,
+            bytes_accessed=14 * seqs * block * width,
+            transcendentals=0,
         ),
         name="finish",
-    )(own, gnormed, more, gresid, gain)
+    )(own, gnormed, gresid, gain, *near, *far)
 
 
 def swap(x, axis, bit):
@@ -765,11 +902,16 @@
     return x
 
 
-def gather_pieces(shard):
+def gather_near(shard):
     size = lax.axis_size("fsdp")
     if size != 8:
         return [lax.all_gather(shard, "fsdp", axis=0, tiled=True)]
-    near = [shard] + [swap(shard, "fsdp", 2 * d) for d in range(1, size // 2)]
+    return [shard] + [swap(shard, "fsdp", 2 * d) for d in range(1, size // 2)]
+
+
+def gather_rest(near):
+    if lax.axis_size("fsdp") != 8:
+        return near
     return near + [swap(piece, "fsdp", 1) for piece in near]
 
 
@@ -783,41 +925,99 @@
     )
 
 
-def reduce_rows(parts):
+def sum_seq(total):
+    if lax.axis_size("seq") != 4:
+        return lax.psum(total, "seq")
+    return sum_seq_rest(sum_seq_first(total))
+
+
+def sum_seq_first(total):
+    rows, columns = total.shape
+    odd = lax.axis_index("seq") % 2
+    halves = total.reshape(2, rows // 2, columns)
+    pick = lambda k: lax.dynamic_index_in_dim(halves, k, 0, keepdims=False)
+    return (pick(odd).astype(F32) + swap(pick(1 - odd), "seq", 1).astype(F32)).astype(BF16)
+
+
+def sum_seq_rest(half):
+    odd = lax.axis_index("seq") % 2
+    half = (half.astype(F32) + swap(half, "seq", 2).astype(F32)).astype(BF16)
+    back = swap(half, "seq", 1)
+    return jnp.where(
+        odd == 0, jnp.concatenate([half, back], 0), jnp.concatenate([back, half], 0)
+    )
+
+
+def reduce_rows(parts, extra, *first):
     size = lax.axis_size("fsdp")
     me = lax.axis_index("fsdp")
+    if size != 8:
+        parts = jnp.concatenate([parts, extra], 1)
+        total = lax.psum_scatter(parts, "fsdp", scatter_dimension=0, tiled=False)
+        return lax.psum(total, "seq"), *first
     rows, columns = parts.shape[1:]
-    if size != 8:
-        total = lax.psum_scatter(parts, "fsdp", scatter_dimension=0, tiled=False)
-        return lax.psum(total, "seq").astype(F32)
-    pairs = parts.reshape(size // 2, 2, rows, columns)
+    few = extra.shape[1]
     core = me % 2
     chip = me // 2
     pick = lambda a, k, ax: lax.dynamic_index_in_dim(a, k, ax, keepdims=False)
-    other = swap(pick(pairs, 1 - core, 1), "fsdp", 1)
-    mine = (pick(pairs, core, 1).astype(F32) + other.astype(F32)).astype(BF16)
+    parts = parts.reshape(size // 2, 2, rows, columns)
+    extra = extra.reshape(size // 2, 2, few, columns)
+    half = lambda k: jnp.concatenate([pick(parts, k, 1), pick(extra, k, 1)], 1)
+    other = swap(half(1 - core), "fsdp", 1)
+    mine = (half(core).astype(F32) + other.astype(F32)).astype(BF16)
     arrived = [
         swap(pick(mine, chip ^ d, 0), "fsdp", 2 * d) for d in range(1, size // 2)
     ]
+    arrived, *first = lax.optimization_barrier((arrived, *first))
     total = pick(mine, chip, 0).astype(F32)
     for part in arrived:
         total = total + part.astype(F32)
-    total = total.astype(BF16)
-    groups = lax.axis_size("seq")
-    place = lax.axis_index("seq")
-    if groups == 4:
-        halves = total.reshape(2, rows // 2, columns)
-        odd = place % 2
-        half = pick(halves, odd, 0).astype(F32) + swap(pick(halves, 1 - odd, 0), "seq", 1).astype(F32)
-        half = half.astype(BF16)
-        half = (half.astype(F32) + swap(half, "seq", 2).astype(F32)).astype(BF16)
-        back = swap(half, "seq", 1)
-        return jnp.where(
-            odd == 0,
-            jnp.concatenate([half, back], 0),
-            jnp.concatenate([back, half], 0),
+    return sum_seq(total.astype(BF16)), *first
+
+
+def gather_slab(outweight, fcweight, projweight, *first):
+    width = outweight.shape[1]
+    cuts = fcweight.shape[1] // width
+
+    def join(out, up, down, axis):
+        ups = [lax.slice_in_dim(up, c * width, (c + 1) * width, axis=-1) for c in range(cuts)]
+        return jnp.concatenate([out, *ups, down], axis)
+
+    if lax.axis_size("fsdp") == SHARES:
+        slab = join(outweight, fcweight, projweight, 0)
+        slab, *first = lax.optimization_barrier((slab, *first))
+        return lax.all_gather(slab, "fsdp", axis=0, tiled=False), *first
+    whole = [
+        lax.all_gather(w, "fsdp", axis=0, tiled=True) for w in (outweight, fcweight, projweight)
+    ]
+    return join(*(w.reshape(SHARES, -1, w.shape[1]) for w in whole), 1), *first
+
+
+def reduce_slab(slab, width, hidden):
+    owners = lax.axis_size("fsdp")
+    cuts = hidden // width
+    rows = width // SHARES
+
+    def part(array, axis):
+        at = lambda a, b: lax.slice_in_dim(array, a * rows, b * rows, axis=axis)
+        ups = [at(1 + c, 2 + c) for c in range(cuts)]
+        rest = lax.slice_in_dim(array, (1 + 2 * cuts) * rows, array.shape[axis], axis=axis)
+        return at(0, 1), jnp.concatenate(ups, -1), at(1 + cuts, 1 + 2 * cuts), rest
+
+    if owners == SHARES:
+        return part(slab.astype(F32), 0)
+    *grads, rest = part(slab, 1)
+    grads = [
+        lax.psum(
+            lax.psum_scatter(
+                g.reshape(-1, g.shape[-1]), "fsdp", scatter_dimension=0, tiled=True
+            ),
+            "seq",
         ).astype(F32)
-    return lax.psum(total, "seq").astype(F32)
+        for g in grads
+    ]
+    rest = lax.psum(rest.astype(F32), ("fsdp", "seq"))
+    return *grads, rest
 
 
 def local(
@@ -849,32 +1049,8 @@
     place = lax.axis_index("seq").astype(jnp.int32)
     hidden = fcweight.shape[1]
 
-    near = shift(tokens, "seq", 1)
-
-    shards = [attngain, attnshift, qvbias, outbias, mlpgain, mlpshift, fcbias, projbias]
-    packed = jnp.concatenate(shards)
-    table = jnp.where(
-        lax.broadcasted_iota(jnp.int32, (owners, packed.shape[0]), 0) == me,
-        packed[None],
-        jnp.zeros((), BF16),
-    )
-    if owners == 8:
-        table = sum_over(table, "fsdp")
-    else:
-        table = lax.psum(table, "fsdp")
-    vectors = []
-    at = 0
-    for shard in shards:
-        size = shard.shape[0]
-        vectors.append(table[:, at : at + size].reshape(1, size * owners).astype(F32))
-        at += size
-    gain1, shift1, bias1, outbias_v, gain2, shift2, upbias, downbias = vectors
-
     order = piece_order()
-    qkv_pieces = gather_pieces(qkvweight)
-    out_pieces = gather_pieces(outweight)
-    up_pieces = gather_pieces(fcweight)
-    down_pieces = gather_pieces(projweight)
+    qkv_pieces = gather_near(qkvweight)
 
     weight = (valid_mask * (1 - latent_flags)).astype(F32)
     below = jnp.sum(
@@ -883,6 +1059,10 @@
     facts = jnp.concatenate([below.reshape(-1), jnp.sum(weight).astype(jnp.int32)[None]])
     facts = sum_over(facts, "seq")
     bounds = facts[:-1].reshape(seqs, 3)
+
+    sent, facts = lax.optimization_barrier((tokens, facts))
+    near = [shift(sent[s], "seq", 1) for s in range(seqs)]
+    far = shift(sent[:, block - HALO_CHUNK :], "seq", 2) if far_rows > 0 else None
 
     def start_of(positions):
         found = jnp.zeros((seqs,) + positions.shape, jnp.int32)
@@ -894,8 +1074,44 @@
     firsts = jnp.arange(groups, dtype=jnp.int32) * block
     reach = jnp.max(firsts[None] - start_of(firsts)) - block
     chunks = jnp.maximum(reach + HALO_CHUNK - 1, 0) // HALO_CHUNK
-    chunks = max_over(chunks[None], "fsdp")[0]
-    count = sum_over(facts[-1:], "fsdp")[0].astype(F32)
+
+    shards = [attngain, attnshift, qvbias, outbias, mlpgain, mlpshift, fcbias, projbias]
+    packed = jnp.concatenate(shards).astype(F32)
+    table = jnp.where(
+        lax.broadcasted_iota(jnp.int32, (owners, packed.shape[0]), 0) == me,
+        packed[None],
+        0.0,
+    )
+    line = lax.broadcasted_iota(jnp.int32, (8, packed.shape[0]), 0)
+    table = jnp.concatenate(
+        [
+            table,
+            jnp.where(line == 0, facts[-1].astype(F32), jnp.where(line == 1, chunks.astype(F32), 0.0)),
+        ],
+        0,
+    )
+    is_reach = lax.broadcasted_iota(jnp.int32, table.shape, 0) == owners + 1
+    bit = 1
+    while bit < owners:
+        other = swap(table, "fsdp", bit)
+        table = jnp.where(is_reach, jnp.maximum(table, other), table + other)
+        bit *= 2
+    qkv_pieces = gather_rest(qkv_pieces)
+    slab, qkv_pieces, table, near[0] = gather_slab(
+        outweight, fcweight, projweight, qkv_pieces, table, near[0]
+    )
+
+    count = table[owners, 0]
+    chunks = table[owners + 1, 0].astype(jnp.int32)
+    vectors = []
+    at = 0
+    for shard in shards:
+        size = shard.shape[0]
+        vectors.append(table[:owners, at : at + size].reshape(1, size * owners))
+        at += size
+    gain1, shift1, bias1, outbias_v, gain2, shift2, upbias, downbias = vectors
+
+
     base = (place - (groups - 1)) * block
     starts = start_of(place * block + jnp.arange(block, dtype=jnp.int32)) - base
     low_rows = starts[:, ::QUERY_TILE]
@@ -904,7 +1120,10 @@
     first = low_tile * (ROW_TILE // KEY_TILE)
     starts = starts[:, None, :]
 
-    halo = jnp.concatenate([jnp.zeros((seqs, far_rows, width), BF16), near], 1)
+    halo = jnp.stack(near)
+    if far_rows > 0:
+        blank = jnp.zeros((seqs, far_rows - HALO_CHUNK, width), BF16)
+        halo = jnp.concatenate([blank, far, halo], 1)
 
     def fetch(state):
         j, halo = state
@@ -915,7 +1134,7 @@
         )
 
     if far_rows > 0:
-        _, halo = lax.while_loop(lambda state: state[0] < chunks, fetch, (jnp.int32(0), halo))
+        _, halo = lax.while_loop(lambda state: state[0] < chunks, fetch, (jnp.int32(1), halo))
 
     normed, query, keys, values = project(
         low_tile, order, halo, tokens, gain1, shift1, bias1, qkv_pieces
@@ -935,28 +1154,28 @@
         sums,
         upsums,
     ) = mlp(
-        order,
         factor.reshape(1),
         mixed.reshape(rows, width),
         tokens.reshape(rows, width),
         teacher.reshape(rows, width),
         weight.reshape(rows, 1),
         (outbias_v, gain2, shift2, upbias, downbias),
-        out_pieces,
-        up_pieces,
-        down_pieces,
-    )
-
-    def outer(left, right):
-        return lax.dot_general(left, right, TN, preferred_element_type=F32).astype(BF16)
-
-    grad_down = reduce_rows(outer(active, gmlp).reshape(owners, hidden // owners, width))
-    grad_up = reduce_rows(outer(normed2, ghidden).reshape(owners, width // owners, hidden))
-    grad_merge = reduce_rows(
-        outer(mixed.reshape(rows, width), gbranch).reshape(owners, width // owners, width)
-    )
-    small = jnp.concatenate([sums[:4].reshape(-1), upsums[0], jnp.sum(sums[4:5], 1)])
-    small = sum_over(sum_over(small, "seq"), "fsdp")
+        slab,
+    )
+
+    small = jnp.concatenate(
+        [upsums[0].reshape(SHARES, -1)] + [sums[k].reshape(SHARES, -1) for k in range(4)], 1
+    )
+    line = lax.broadcasted_iota(jnp.int32, (SHARES, 16, width), 1)
+    small = jnp.where(line == 0, small[:, None, :], jnp.where(line == 1, sums[4], 0.0))
+    outer = outer_all(
+        mixed.reshape(rows, width), gbranch, normed2, ghidden, active, gmlp, small.astype(BF16)
+    )
+    outer, gmixed = lax.optimization_barrier((outer, gmixed))
+    staged = owners == SHARES and groups == 4
+    if owners == SHARES:
+        outer = lax.psum_scatter(outer, "fsdp", scatter_dimension=0, tiled=False)
+        outer = sum_seq_first(outer) if staged else sum_seq(outer)
 
     gquery, gkeys, gvalues = attend_back(
         low, first, query, keys, values, starts, mixed, gmixed.reshape(seqs, block, width), logs
@@ -974,45 +1193,77 @@
         return j, lax.dynamic_update_slice_in_dim(ghalo, total, spot, 1)
 
     if far_rows > 0:
-        _, ghalo = lax.while_loop(lambda state: state[0] > 0, give, (chunks, ghalo))
-    more = shift(ghalo[:, far_rows:], "seq", -1)
-
+        _, ghalo = lax.while_loop(lambda state: state[0] > 1, give, (chunks, ghalo))
+
+    ghalo, gquery = lax.optimization_barrier((ghalo, gquery))
+    near = [shift(ghalo[s, far_rows:], "seq", -1) for s in range(seqs)]
+    far = []
+    if far_rows > 0:
+        far = [shift(ghalo[:, far_rows - HALO_CHUNK : far_rows], "seq", -2)]
     gnormed, gweight, own_sums = own_back(
         low_tile, order, tokens, normed, gquery, gkeys, gvalues, qkv_pieces
     )
-    late = jnp.concatenate([(own_sums[:2] + halo_sums[:2]).reshape(-1), own_sums[2:4].reshape(-1)])
-    late = sum_over(sum_over(late, "seq"), "fsdp")
-    grad_joint = reduce_rows(gweight.reshape(owners, width // owners, 3 * width))
-
+    late = jnp.concatenate(
+        [(own_sums[k] + halo_sums[k]).reshape(owners, -1) for k in range(2)]
+        + [own_sums[2:4].reshape(owners, -1)],
+        1,
+    ).astype(BF16)
+    late = jnp.pad(late, ((0, 0), (0, 2 * width + width - late.shape[1])))
+    line = lax.broadcasted_iota(jnp.int32, (owners, 16, 3 * width), 1)
+    late = jnp.where(line == 0, late[:, None, :], jnp.zeros((), BF16))
+    gweight, near[0] = lax.optimization_barrier((gweight, near[0]))
     grad_tokens = finish(
-        tokens.reshape(rows, width),
-        gnormed.reshape(rows, width),
-        more.reshape(rows, width),
-        gresid,
+        tokens,
+        gnormed,
+        near,
+        far,
+        gresid.reshape(tokens.shape),
         gain1,
-    ).reshape(tokens.shape)
-
-    def own_part(vector, at, size):
-        share = size // owners
-        return lax.dynamic_slice_in_dim(vector, at + me * share, share)
-
-    loss = small[-1] / (width * count)
+    )
+
+    joint, outer, grad_tokens = reduce_rows(
+        gweight.reshape(owners, width // owners, 3 * width), late, outer, grad_tokens
+    )
+    joint = joint.astype(F32)
+    if staged:
+        outer = sum_seq_rest(outer)
+    grad_merge, grad_up, grad_down, small = reduce_slab(outer, width, hidden)
+
+    share = width // owners
+    if owners == SHARES:
+        at = hidden // owners
+        cuts = [small[0, :at]] + [
+            small[0, at + k * share : at + (k + 1) * share] for k in range(4)
+        ]
+        loss_row = small[1]
+    else:
+        at = hidden // SHARES
+        wide = width // SHARES
+        full = [small[:, 0, :at].reshape(-1)] + [
+            small[:, 0, at + k * wide : at + (k + 1) * wide].reshape(-1) for k in range(4)
+        ]
+        cuts = [
+            lax.dynamic_slice_in_dim(v, me * (v.shape[0] // owners), v.shape[0] // owners)
+            for v in full
+        ]
+        loss_row = small[0, 1]
+    loss = jnp.sum(loss_row) / (width * count)
     return (
         loss,
         layer_out.reshape(tokens.shape),
         grad_tokens,
-        own_part(late, 0, width),
-        own_part(late, width, width),
-        grad_joint,
-        own_part(late, 2 * width, 2 * width),
+        joint[share, :share],
+        joint[share, share : 2 * share],
+        joint[:share],
+        joint[share, 2 * share : 4 * share],
         grad_merge,
-        own_part(small, 0, width),
-        own_part(small, width, width),
-        own_part(small, 2 * width, width),
+        cuts[1],
+        cuts[2],
+        cuts[3],
         grad_up,
-        own_part(small, 4 * width, hidden),
+        cuts[0],
         grad_down,
-        own_part(small, 3 * width, width),
+        cuts[4],
     )
 
 

time: 602 us -> 503 us (0.84); the launches traced: 605 us -> 498 us
  starting transfers between devices: 151 us -> 66.2 us
  waiting for transfers between devices: 187 us -> 152 us
  Pallas kernels: 173 us -> 194 us
  matrix products: 20.7 us -> 0 us
  between operations: 9.12 us -> 20.3 us
  local copies, waits for them, and re-layouts: 37.6 us -> 43.8 us
    ppermute x77 -> x22, waiting for transfers between devices: 166 us -> 71.9 us  [swap(): return lax.ppermute(x, axis, [(i, i ^ bit) for i in range(size)])]
    ppermute x77 -> x22, starting transfers between devices: 141 us -> 50 us  [swap(): return lax.ppermute(x, axis, [(i, i ^ bit) for i in range(size)])]
    ppermute x4 -> x6, waiting for transfers between devices: 20.8 us -> 80.1 us  [shift(): lax.ppermute(x, axis, [(i, i + step) for i in range(size) if 0 <= i + ste...]
    dot_general x3 -> x0, matrix products: 20.7 us -> none  [outer(): lax.dot_general(left, right, TN, preferred_element_type=F32).astype(BF16)]
    pallas_call x2 -> x3, Pallas kernels: 57.4 us -> 77.3 us  [the longest x1 50.6 us: mlp(): pl.pallas_call(mlp_kernel, grid_spec=pltpu.PrefetchScalarGridSpec(num_sca...]
    squeeze x0 -> x6, local copies, waits for them, and re-layouts: none -> 7.43 us  [the longest x1 3 us: local(): near = [shift(ghalo[s, far_rows:], 'seq', -1) for s in range(seqs)]]
    convert_element_type x22 -> x10, other arithmetic: 13.8 us -> 6.86 us  [the longest x1 2.57 us: reduce_rows(): mine = (half(core).astype(F32) + other.astype(F32)).astype(BF16)]
    ppermute x4 -> x6, starting transfers between devices: 9.84 us -> 16.1 us  [shift(): lax.ppermute(x, axis, [(i, i + step) for i in range(size) if 0 <= i + ste...]
  transfers between devices with their start and end apart: 81 -> 30, of which waited for: 31 -> 14; matrix products, arithmetic and copies ran while one was open for 12% -> 11% of each run, Pallas kernels for 20% -> 25%
where the time goes in v2:
time: 503 us; the launch traced here: 498 us
  Pallas kernels  194 us (39%)
  waiting for transfers between devices  152 us (30%)
  starting transfers between devices  66.2 us (13%)
  local copies, waits for them, and re-layouts  43.8 us (9%)
  other arithmetic  21.5 us (4%)
  between operations  20.3 us (4%)
    ppermute x6, waiting for transfers between devices, shift(): lax.ppermute(x, axis, [(i, i + step) for i in range(size) if 0 <= i + ste...  80.1 us
    ppermute x22, waiting for transfers between devices, swap(): return lax.ppermute(x, axis, [(i, i ^ bit) for i in range(size)])  71.9 us
    pallas_call x1, Pallas kernels, mlp(): pl.pallas_call(mlp_kernel, grid_spec=pltpu.PrefetchScalarGridSpec(num_sca...  50.6 us
    ppermute x22, starting transfers between devices, swap(): return lax.ppermute(x, axis, [(i, i ^ bit) for i in range(size)])  50 us
    pallas_call x1, Pallas kernels, attend_back(): pl.pallas_call(functools.partial(attend_back_kernel, length - block), gri...  40.6 us
    pallas_call x1, Pallas kernels, attend(): pl.pallas_call(functools.partial(attend_kernel, length - block), grid_spe...  35.7 us
    pallas_call x1, Pallas kernels, outer_all(): pl.pallas_call(outer_kernel, grid=(1 + 2 * chunks,), in_specs=[whole, who...  19.5 us
    pallas_call x1, Pallas kernels, own_back(): pl.pallas_call(functools.partial(own_back_kernel, halo_tiles, len(pieces)...  17.4 us
  transfers between devices with their start and end apart: 30, of which 14 were waited for; matrix products, arithmetic and copies ran while one was open for 11% of the time, Pallas kernels for 25%

profile of v2, /device:TPU:0, one launch (start us, length us, event | category | flops | bytes accessed | tf_op | source)
XLA Modules:
  0.0 497.6 jit_solution(3072703187425361505)
XLA Ops:
  17.0 5.4 %concatenate.49 = bf16[1152]{0:T(1024)(128)(2,1)S(1)} concatenate(bf16[96]{0:T(256)(128)(2,1)} %param.26, bf16[96]{0:T(256)(128)(2,1)} %param.27, bf16[192]{0:T(256)(128)(2,1)} %param.29, bf16[96]{0:T(256)(128)(2,1)} %param.31, bf16[96]{0:T(256)(128)(2,1)} %param.32, bf16[96]{0:T(256)(128)(2,1)} %param.33, bf16[384]{0:T(512)(128)(2,1)} %param.35, bf16[96]{0:T(256)(128)(2,1)} %param.37), dimensions={0} | concatenate | bytes 4608 | tf_op jit(solution)/shard_map/concatenate | solution.py:1079
  50.1 8.3 %collective-permute-done.15 = bf16[512,768]{1,0:T(8,128)(2,1)} collective-permute-done((bf16[512,768]{1,0:T(8,128)(2,1)}, bf16[512,768]{1,0:T(8,128)(2,1)}, u32[]{:S(2)}, u32[]{:S(2)}) %collective-permute-start.15) | collective-permute-done | bytes 786464 | tf_op jit(solution)/shard_map/ppermute | solution.py:884
  60.3 4.7 collective-permute-start.16
  64.9 4.3 collective-permute-start.4
  78.6 10.9 %collective-permute-done.4 = bf16[2,128,768]{2,1,0:T(8,128)(2,1)S(1)} collective-permute-done((bf16[2,128,768]{2,1,0:T(8,128)(2,1)S(1)}, bf16[2,128,768]{2,1,0:T(8,128)(2,1)S(1)}, u32[]{:S(2)}, u32[]{:S(2)}) %collective-permute-start.4) | collective-permute-done | bytes 393248 | tf_op jit(solution)/shard_map/ppermute | solution.py:884
  93.6 11.7 %project.1 = (bf16[2,2048,768]{2,1,0:T(8,128)(2,1)}, bf16[2,512,768]{2,1,0:T(8,128)(2,1)}, bf16[2,2048,768]{2,1,0:T(8,128)(2,1)}, bf16[2,2048,768]{2,1,0:T(8,128)(2,1)}) custom-call(s32[2]{0:T(128)} %get-tuple-element.191.low_ref, s32[8]{0:T(128)} %stack.44.order_ref, bf16[2,1536,768]{2,1,0:T(8,128)(2,1)} %get-tuple-element.124.halo_ref, ...), custom_call_target="tpu_custom_call" | custom-call | flops 6039797760 | bytes 25165824 | tf_op jit(solution)/shard_map/project/pallas_call | solution.py:109
  105.3 35.7 %attend.1 = (bf16[2,512,768]{2,1,0:T(8,128)(2,1)}, f32[2,6,2,512]{3,2,1,0:T(2,128)}) custom-call(s32[4]{0:T(128)} %reshape.426.low_ref, bf16[2,512,768]{2,1,0:T(8,128)(2,1)} %get-tuple-element.134.query_ref, bf16[2,2048,768]{2,1,0:T(8,128)(2,1)} %get-tuple-element.135.key_ref, bf16[2,2048,768]{2,1,0:T(8,128)(2,1)} %get-tuple-element.136.value_ref, ...), custom_call_target="tpu_custom_call" | custom-call | flops 17179869184 | bytes 16777216 | tf_op jit(solution)/shard_map/attend/pallas_call | solution.py:220
  141.0 50.6 %mlp.1 = (bf16[1024,768]{1,0:T(8,128)(2,1)}, f32[1024,768]{1,0:T(8,128)}, bf16[1024,768]{1,0:T(8,128)(2,1)}, bf16[1024,768]{1,0:T(8,128)(2,1)}, bf16[1024,3072]{...) custom-call(f32[1]{0:T(128)} %bitcast.16.factor_ref, ...), custom_call_target="tpu_custom_call" | custom-call | flops 21743271936 | bytes 41943040 | tf_op jit(solution)/shard_map/mlp/pallas_call | solution.py:492
  194.7 19.5 %outer_all.1 = bf16[8,880,768]{2,1,0:T(8,128)(2,1)} custom-call(bf16[1024,768]{1,0:T(8,128)(2,1)} %bitcast.99, bf16[1024,768]{1,0:T(8,128)(2,1)} %get-tuple-element.139.gbranch_ref, bf16[1024,768]{1,0:T(8,128)(2,1)} %get-tuple-element.140.normed_ref, bf16[1024,3072]{1,0:T(8,128)(2,1)} %get-tuple-element.141.ghidden_ref, ...), custom_call_target="tpu_custom_call" | custom-call | flops 10871635968 | bytes 31457280 | tf_op jit(solution)/shard_map/outer_all/pallas_call | solution.py:637
  214.3 40.6 %attend_back.1 = (bf16[2,512,768]{2,1,0:T(8,128)(2,1)}, bf16[2,2048,768]{2,1,0:T(8,128)(2,1)}, bf16[2,2048,768]{2,1,0:T(8,128)(2,1)}) custom-call(s32[4]{0:T(128)} %reshape.426.low_ref, s32[2]{0:T(128)} %get-tuple-element.190.first_ref, bf16[2,512,768]{2,1,0:T(8,128)(2,1)} %get-tuple-element.134.query_ref, bf16[2,2048,768]{2,1,0:T(8,128)(2,1)} %get-tuple-element.135.key_ref, ...), custom_call_target="tpu_custom_call" | custom-call | flops 42949672960 | bytes 29360128 | tf_op jit(solution)/shard_map/attend_back/pallas_call | solution.py:313
  254.9 11.1 %halo_back.1 = (bf16[2,1536,768]{2,1,0:T(8,128)(2,1)}, f32[8,768]{1,0:T(8,128)}) custom-call(s32[2]{0:T(128)} %get-tuple-element.191.low_ref, s32[8]{0:T(128)} %stack.44.order_ref, bf16[2,1536,768]{2,1,0:T(8,128)(2,1)} %get-tuple-element.124.halo_ref, bf16[2,2048,768]{2,1,0:T(8,128)(2,1)} %get-tuple-element.149.gkey_ref, ...), custom_call_target="tpu_custom_call" | custom-call | flops 4294967296 | bytes 16777216 | tf_op jit(solution)/shard_map/halo_back/pallas_call | solution.py:707
  270.3 17.4 %own_back.1 = (f32[2,512,768]{2,1,0:T(8,128)}, bf16[768,2304]{1,0:T(8,128)(2,1)}, f32[8,768]{1,0:T(8,128)}) custom-call(s32[2]{0:T(128)} %get-tuple-element.191.low_ref, s32[8]{0:T(128)} %stack.44.order_ref, bf16[2,512,768]{2,1,0:T(8,128)(2,1)} %own_ref.5, bf16[2,2048,768]{2,1,0:T(8,128)(2,1)} %get-tuple-element.133.normed_ref, ...), custom_call_target="tpu_custom_call" | custom-call | flops 17179869184 | bytes 25165824 | tf_op jit(solution)/shard_map/own_back/pallas_call | solution.py:799
  289.9 37.8 %collective-permute-done.17.rest_0_ = bf16[512,768]{1,0:T(8,128)(2,1)S(1)} collective-permute-done((bf16[512,768]{1,0:T(8,128)(2,1)}, bf16[512,768]{1,0:T(8,128)(2,1)S(1)}, u32[]{:S(2)}, u32[]{:S(2)}) %collective-permute-start.17) | collective-permute-done | bytes 786464 | tf_op jit(solution)/shard_map/ppermute | solution.py:884
  333.0 9.7 %collective-permute-start.18 = (bf16[4,112,2304]{2,1,0:T(8,128)(2,1)}, bf16[4,112,2304]{2,1,0:T(8,128)(2,1)S(1)}, u32[]{:S(2)}, u32[]{:S(2)}) collective-permute-start(bf16[4,112,2304]{2,1,0:T(8,128)(2,1)} %pad_maximum_fusion), channel_id=1, source_target_pairs={{0,4},{4,0},{8,12},{12,8},{16,20},{20,16},{24,28},{28,24},{1,5},{5... | collective-permute-start | bytes 6193160 | tf_op jit(solution)/shard_map/ppermute | solution.py:879
  349.0 15.2 %collective-permute-start.22 = (bf16[440,768]{1,0:T(8,128)(2,1)}, bf16[440,768]{1,0:T(8,128)(2,1)}, u32[]{:S(2)}, u32[]{:S(2)}) collective-permute-start(bf16[440,768]{1,0:T(8,128)(2,1)} %dynamic-slice_bitcast_fusion.2), channel_id=1, source_target_pairs={{0,1},{1,0},{2,3},{3,2},{4,5},{5,4},{6,7},{7,6},{8,9},{9,8},{10,11... | collective-permute-start | bytes 2027528 | tf_op jit(solution)/shard_map/ppermute | solution.py:879
  369.5 4.3 collective-permute-start.20
  373.8 23.1 %collective-permute-done.24.rest_2_ = bf16[2,128,768]{2,1,0:T(8,128)(2,1)S(1)} collective-permute-done((bf16[2,128,768]{2,1,0:T(8,128)(2,1)}, bf16[2,128,768]{2,1,0:T(8,128)(2,1)S(1)}, u32[]{:S(2)}, u32[]{:S(2)}) %collective-permute-start.24) | collective-permute-done | bytes 393248 | tf_op jit(solution)/shard_map/ppermute | solution.py:884
  396.9 4.3 collective-permute-start.21
  402.1 7.2 %finish.1 = bf16[2,512,768]{2,1,0:T(8,128)(2,1)} custom-call(bf16[2,512,768]{2,1,0:T(8,128)(2,1)} %own_ref.5, f32[2,512,768]{2,1,0:T(8,128)} %get-tuple-element.161.gnormed_ref, f32[2,512,768]{2,1,0:T(8,128)} %bitcast.85, f32[1,768]{1,0:T(1,128)} %reshape.423.gain_ref, bf16[512,768]{1,0:T(8,128)(2,1)} %copy-done.4, bf16[512,768]{1,0:T(8,128)(2,1)} %copy-done.5, ...), custom_call_target="tpu_custom_call" | custom-call | flops 15728640 | bytes 11010048 | tf_op jit(solution)/shard_map/finish/pallas_call | solution.py:859
  414.8 7.2 %collective-permute-done.27 = bf16[56,2304]{1,0:T(8,128)(2,1)S(1)} collective-permute-done((bf16[56,2304]{1,0:T(8,128)(2,1)S(1)}, bf16[56,2304]{1,0:T(8,128)(2,1)S(1)}, u32[]{:S(2)}, u32[]{:S(2)}) %collective-permute-start.27) | collective-permute-done | bytes 258080 | tf_op jit(solution)/shard_map/ppermute | solution.py:879
  425.1 24.4 %collective-permute-done.28 = bf16[56,2304]{1,0:T(8,128)(2,1)S(1)} collective-permute-done((bf16[56,2304]{1,0:T(8,128)(2,1)S(1)}, bf16[56,2304]{1,0:T(8,128)(2,1)S(1)}, u32[]{:S(2)}, u32[]{:S(2)}) %collective-permute-start.28) | collective-permute-done | bytes 258080 | tf_op jit(solution)/shard_map/ppermute | solution.py:879
  449.6 14.3 %collective-permute-done.25 = bf16[440,768]{1,0:T(8,128)(2,1)S(1)} collective-permute-done((bf16[440,768]{1,0:T(8,128)(2,1)S(1)}, bf16[440,768]{1,0:T(8,128)(2,1)S(1)}, u32[]{:S(2)}, u32[]{:S(2)}) %collective-permute-start.25) | collective-permute-done | bytes 675872 | tf_op jit(solution)/shard_map/ppermute | solution.py:879
  464.9 4.6 collective-permute-done.29
  471.7 12.1 %collective-permute-done.26 = bf16[440,768]{1,0:T(8,128)(2,1)S(1)} collective-permute-done((bf16[440,768]{1,0:T(8,128)(2,1)S(1)}, bf16[440,768]{1,0:T(8,128)(2,1)S(1)}, u32[]{:S(2)}, u32[]{:S(2)}) %collective-permute-start.26) | collective-permute-done | bytes 675872 | tf_op jit(solution)/shard_map/ppermute | solution.py:879
  (173 shorter events, 92.9 us)
Async XLA Ops:
  7.2 133.8 %all-gather.3.cloned.1.call-start = ((), (), s32[]{:S(2)}) async-start(), calls=%async_computation.2 | async-start | bytes 11943936 | tf_op jit(solution)/shard_map/all_gather | solution.py:989
  7.2 40.3 %collective-permute-start.6 = (bf16[96,2304]{1,0:T(8,128)(2,1)}, bf16[96,2304]{1,0:T(8,128)(2,1)}, u32[]{:S(2)}, u32[]{:S(2)}) collective-permute-start(bf16[96,2304]{1,0:T(8,128)(2,1)} %rest_0_.2), channel_id=1, source_target_pairs={{0,16},{4,20},{8,24},{12,28},{16,0},{20,4},{24,8},{28,12},{1,17},{... | collective-permute-start | bytes 1327112 | tf_op jit(solution)/shard_map/ppermute | solution.py:879
  10.3 37.8 %collective-permute-start.7 = (bf16[96,2304]{1,0:T(8,128)(2,1)}, bf16[96,2304]{1,0:T(8,128)(2,1)}, u32[]{:S(2)}, u32[]{:S(2)}) collective-permute-start(bf16[96,2304]{1,0:T(8,128)(2,1)} %rest_0_.2), channel_id=1, source_target_pairs={{0,24},{4,28},{8,16},{12,20},{16,8},{20,12},{24,0},{28,4},{1,25},{... | collective-permute-start | bytes 1327112 | tf_op jit(solution)/shard_map/ppermute | solution.py:879
  11.7 36.5 %collective-permute-start.5 = (bf16[96,2304]{1,0:T(8,128)(2,1)}, bf16[96,2304]{1,0:T(8,128)(2,1)}, u32[]{:S(2)}, u32[]{:S(2)}) collective-permute-start(bf16[96,2304]{1,0:T(8,128)(2,1)} %rest_0_.2), channel_id=1, source_target_pairs={{0,8},{4,12},{8,0},{12,4},{16,24},{20,28},{24,16},{28,20},{1,9},{5... | collective-permute-start | bytes 1327112 | tf_op jit(solution)/shard_map/ppermute | solution.py:879
  14.9 12.2 %collective-permute-start.2 = (s32[7]{0:T(128)S(1)}, s32[7]{0:T(128)S(1)}, u32[]{:S(2)}, u32[]{:S(2)}) collective-permute-start(s32[7]{0:T(128)S(1)} %pad_add_fusion), channel_id=1, source_target_pairs={{0,1},{1,0},{2,3},{3,2},{4,5},{5,4},{6,7},{7,6},{8,9},{9,8},{10,11... | collective-permute-start | bytes 92 | tf_op jit(solution)/shard_map/ppermute | solution.py:879
  38.8 19.6 %collective-permute-start.15 = (bf16[512,768]{1,0:T(8,128)(2,1)}, bf16[512,768]{1,0:T(8,128)(2,1)}, u32[]{:S(2)}, u32[]{:S(2)}) collective-permute-start(bf16[512,768]{1,0:T(8,128)(2,1)} %get-tuple-element.208), channel_id=1, source_target_pairs={{0,1},{1,2},{2,3},{4,5},{5,6},{6,7},{8,9},{9,10},{10,11},{12,13},{... | collective-permute-start | bytes 2359304 | tf_op jit(solution)/shard_map/ppermute | solution.py:884
  47.6 10.9 %collective-permute-start.10 = (bf16[96,2304]{1,0:T(8,128)(2,1)}, bf16[96,2304]{1,0:T(8,128)(2,1)}, u32[]{:S(2)}, u32[]{:S(2)}) collective-permute-start(bf16[96,2304]{1,0:T(8,128)(2,1)} %collective-permute-done.6.rest_2_), channel_id=1, source_target_pairs={{0,4},{4,0},{8,12},{12,8},{16,20},{20,16},{24,28},{28,24},{1,5},{5... | collective-permute-start | bytes 1327112 | tf_op jit(solution)/shard_map/ppermute | solution.py:879
  48.1 10.4 %collective-permute-start.11 = (bf16[96,2304]{1,0:T(8,128)(2,1)}, bf16[96,2304]{1,0:T(8,128)(2,1)}, u32[]{:S(2)}, u32[]{:S(2)}) collective-permute-start(bf16[96,2304]{1,0:T(8,128)(2,1)} %collective-permute-done.7.rest_3_), channel_id=1, source_target_pairs={{0,4},{4,0},{8,12},{12,8},{16,20},{20,16},{24,28},{28,24},{1,5},{5... | collective-permute-start | bytes 1327112 | tf_op jit(solution)/shard_map/ppermute | solution.py:879
  48.2 10.3 %collective-permute-start.9 = (bf16[96,2304]{1,0:T(8,128)(2,1)}, bf16[96,2304]{1,0:T(8,128)(2,1)}, u32[]{:S(2)}, u32[]{:S(2)}) collective-permute-start(bf16[96,2304]{1,0:T(8,128)(2,1)} %collective-permute-done.5.rest_1_), channel_id=1, source_target_pairs={{0,4},{4,0},{8,12},{12,8},{16,20},{20,16},{24,28},{28,24},{1,5},{5... | collective-permute-start | bytes 1327112 | tf_op jit(solution)/shard_map/ppermute | solution.py:879
  58.5 288.6 %reduce-scatter.2.cloned.1.call-start = ((), (), s32[]{:S(2)}) async-start(), calls=%async_computation.1 | async-start | bytes 12165120 | tf_op jit(solution)/shard_map/reduce_scatter | solution.py:1177
  60.3 29.3 %collective-permute-start.16 = (bf16[512,768]{1,0:T(8,128)(2,1)}, bf16[512,768]{1,0:T(8,128)(2,1)S(1)}, u32[]{:S(2)}, u32[]{:S(2)}) collective-permute-start(bf16[512,768]{1,0:T(8,128)(2,1)} %get-tuple-element.209), channel_id=1, source_target_pairs={{0,1},{1,2},{2,3},{4,5},{5,6},{6,7},{8,9},{9,10},{10,11},{12,13},{... | collective-permute-start | bytes 2359304 | tf_op jit(solution)/shard_map/ppermute | solution.py:884
  64.9 24.6 %collective-permute-start.4 = (bf16[2,128,768]{2,1,0:T(8,128)(2,1)S(1)}, bf16[2,128,768]{2,1,0:T(8,128)(2,1)S(1)}, u32[]{:S(2)}, u32[]{:S(2)}) collective-permute-start(bf16[2,128,768]{2,1,0:T(8,128)(2,1)S(1)} %slice.178), channel_id=1, source_target_pairs={{0,2},{1,3},{4,6},{5,7},{8,10},{9,11},{12,14},{13,15},{16,18},{17,... | collective-permute-start | bytes 1179656 | tf_op jit(solution)/shard_map/ppermute | solution.py:884
  269.1 58.6 %collective-permute-start.17 = (bf16[512,768]{1,0:T(8,128)(2,1)}, bf16[512,768]{1,0:T(8,128)(2,1)S(1)}, u32[]{:S(2)}, u32[]{:S(2)}) collective-permute-start(bf16[512,768]{1,0:T(8,128)(2,1)} %get-tuple-element.193), channel_id=1, source_target_pairs={{1,0},{2,1},{3,2},{5,4},{6,5},{7,6},{9,8},{10,9},{11,10},{13,12},{... | collective-permute-start | bytes 2359304 | tf_op jit(solution)/shard_map/ppermute | solution.py:884
  333.0 31.3 %collective-permute-start.18 = (bf16[4,112,2304]{2,1,0:T(8,128)(2,1)}, bf16[4,112,2304]{2,1,0:T(8,128)(2,1)S(1)}, u32[]{:S(2)}, u32[]{:S(2)}) collective-permute-start(bf16[4,112,2304]{2,1,0:T(8,128)(2,1)} %pad_maximum_fusion), channel_id=1, source_target_pairs={{0,4},{4,0},{8,12},{12,8},{16,20},{20,16},{24,28},{28,24},{1,5},{5... | collective-permute-start | bytes 6193160 | tf_op jit(solution)/shard_map/ppermute | solution.py:879
  344.4 56.8 %collective-permute-start.23 = (bf16[512,768]{1,0:T(8,128)(2,1)}, bf16[512,768]{1,0:T(8,128)(2,1)S(1)}, u32[]{:S(2)}, u32[]{:S(2)}) collective-permute-start(bf16[512,768]{1,0:T(8,128)(2,1)} %get-tuple-element.192), channel_id=1, source_target_pairs={{1,0},{2,1},{3,2},{5,4},{6,5},{7,6},{9,8},{10,9},{11,10},{13,12},{... | collective-permute-start | bytes 2359304 | tf_op jit(solution)/shard_map/ppermute | solution.py:884
  345.7 51.2 %collective-permute-start.24 = (bf16[2,128,768]{2,1,0:T(8,128)(2,1)}, bf16[2,128,768]{2,1,0:T(8,128)(2,1)S(1)}, u32[]{:S(2)}, u32[]{:S(2)}) collective-permute-start(bf16[2,128,768]{2,1,0:T(8,128)(2,1)} %slice.210), channel_id=1, source_target_pairs={{2,0},{3,1},{6,4},{7,5},{10,8},{11,9},{14,12},{15,13},{18,16},{19,... | collective-permute-start | bytes 1179656 | tf_op jit(solution)/shard_map/ppermute | solution.py:884
  349.0 60.3 %collective-permute-start.22 = (bf16[440,768]{1,0:T(8,128)(2,1)}, bf16[440,768]{1,0:T(8,128)(2,1)}, u32[]{:S(2)}, u32[]{:S(2)}) collective-permute-start(bf16[440,768]{1,0:T(8,128)(2,1)} %dynamic-slice_bitcast_fusion.2), channel_id=1, source_target_pairs={{0,1},{1,0},{2,3},{3,2},{4,5},{5,4},{6,7},{7,6},{8,9},{9,8},{10,11... | collective-permute-start | bytes 2027528 | tf_op jit(solution)/shard_map/ppermute | solution.py:879
  369.4 41.2 %collective-permute-start.19 = (bf16[112,2304]{1,0:T(8,128)(2,1)}, bf16[112,2304]{1,0:T(8,128)(2,1)}, u32[]{:S(2)}, u32[]{:S(2)}) collective-permute-start(bf16[112,2304]{1,0:T(8,128)(2,1)} %get-tuple-element.207), channel_id=1, source_target_pairs={{0,8},{4,12},{8,0},{12,4},{16,24},{20,28},{24,16},{28,20},{1,9},{5... | collective-permute-start | bytes 1548296 | tf_op jit(solution)/shard_map/ppermute | solution.py:879
  369.5 41.2 %collective-permute-start.20 = (bf16[112,2304]{1,0:T(8,128)(2,1)}, bf16[112,2304]{1,0:T(8,128)(2,1)}, u32[]{:S(2)}, u32[]{:S(2)}) collective-permute-start(bf16[112,2304]{1,0:T(8,128)(2,1)} %get-tuple-element.206), channel_id=1, source_target_pairs={{0,16},{4,20},{8,24},{12,28},{16,0},{20,4},{24,8},{28,12},{1,17},{... | collective-permute-start | bytes 1548296 | tf_op jit(solution)/shard_map/ppermute | solution.py:879
  396.9 16.2 %collective-permute-start.21 = (bf16[112,2304]{1,0:T(8,128)(2,1)}, bf16[112,2304]{1,0:T(8,128)(2,1)}, u32[]{:S(2)}, u32[]{:S(2)}) collective-permute-start(bf16[112,2304]{1,0:T(8,128)(2,1)} %get-tuple-element.205), channel_id=1, source_target_pairs={{0,24},{4,28},{8,16},{12,20},{16,8},{20,12},{24,0},{28,4},{1,25},{... | collective-permute-start | bytes 1548296 | tf_op jit(solution)/shard_map/ppermute | solution.py:879
  422.1 27.4 %collective-permute-start.28 = (bf16[56,2304]{1,0:T(8,128)(2,1)S(1)}, bf16[56,2304]{1,0:T(8,128)(2,1)S(1)}, u32[]{:S(2)}, u32[]{:S(2)}) collective-permute-start(bf16[56,2304]{1,0:T(8,128)(2,1)S(1)} %fusion.7), channel_id=1, source_target_pairs={{0,2},{1,3},{2,0},{3,1},{4,6},{5,7},{6,4},{7,5},{8,10},{9,11},{10,... | collective-permute-start | bytes 774152 | tf_op jit(solution)/shard_map/ppermute | solution.py:879
  422.2 41.8 %collective-permute-start.25 = (bf16[440,768]{1,0:T(8,128)(2,1)S(1)}, bf16[440,768]{1,0:T(8,128)(2,1)S(1)}, u32[]{:S(2)}, u32[]{:S(2)}) collective-permute-start(bf16[440,768]{1,0:T(8,128)(2,1)S(1)} %fusion.2), channel_id=1, source_target_pairs={{0,2},{1,3},{2,0},{3,1},{4,6},{5,7},{6,4},{7,5},{8,10},{9,11},{10,... | collective-permute-start | bytes 2027528 | tf_op jit(solution)/shard_map/ppermute | solution.py:879
  449.5 19.9 %collective-permute-start.29 = (bf16[56,2304]{1,0:T(8,128)(2,1)S(1)}, bf16[56,2304]{1,0:T(8,128)(2,1)S(1)}, u32[]{:S(2)}, u32[]{:S(2)}) collective-permute-start(bf16[56,2304]{1,0:T(8,128)(2,1)S(1)} %add_convert_fusion.3), channel_id=1, source_target_pairs={{0,1},{1,0},{2,3},{3,2},{4,5},{5,4},{6,7},{7,6},{8,9},{9,8},{10,11... | collective-permute-start | bytes 774152 | tf_op jit(solution)/shard_map/ppermute | solution.py:879
  464.1 19.7 %collective-permute-start.26 = (bf16[440,768]{1,0:T(8,128)(2,1)S(1)}, bf16[440,768]{1,0:T(8,128)(2,1)S(1)}, u32[]{:S(2)}, u32[]{:S(2)}) collective-permute-start(bf16[440,768]{1,0:T(8,128)(2,1)S(1)} %add_convert_fusion.2), channel_id=1, source_target_pairs={{0,1},{1,0},{2,3},{3,2},{4,5},{5,4},{6,7},{7,6},{8,9},{9,8},{10,11... | collective-permute-start | bytes 2027528 | tf_op jit(solution)/shard_map/ppermute | solution.py:879
  (17 other events, 189.7 us)
Sparse Core Ops, SparseCore 0:
  58.6 65.1 all-gather.2
  214.4 121.3 reduce-scatter.1

commit v3 on v2

v3 whole, which is shorter than its diff:
```python
import functools

import jax
import jax.numpy as jnp
from jax import lax
from jax.experimental import pallas as pl
from jax.experimental.pallas import tpu as pltpu
from jax.sharding import PartitionSpec as P

H = 12
HD = 64
PAIR = 2 * HD
EPSILON = 1e-05
KEY_TILE = 128
QUERY_TILE = 128
ROW_TILE = 256
MLP_TILE = 256
MLP_CHUNK = 1536
HALO_CHUNK = 128
SHARES = 8
SMALL_ROWS = 16
VMEM_LIMIT = 62 * 1024 * 1024

NT = (((1,), (1,)), ((), ()))
NN = (((1,), (0,)), ((), ()))
TN = (((0,), (0,)), ((), ()))
F32 = jnp.float32
BF16 = jnp.bfloat16


def dot(left, right, dims=NN):
    return lax.dot_general(left, right, dims, preferred_element_type=F32)


def norm_parts(values):
    center = values - jnp.mean(values, -1, keepdims=True)
    spread = jnp.mean(center * center, -1, keepdims=True)
    scale = lax.rsqrt(spread + EPSILON)
    return center * scale, scale


def norm_back(grad, gain, unit, scale):
    weighted = grad * gain
    first = jnp.mean(weighted, -1, keepdims=True)
    second = jnp.mean(weighted * unit, -1, keepdims=True)
    return scale * (weighted - first - unit * second)


def piece_copies(order_ref, pieces, whole_ref, sems):
    copies = []
    for place, piece in enumerate(pieces):
        rows = piece.shape[0]
        if len(pieces) == 1:
            target = whole_ref
        else:
            target = whole_ref.at[pl.ds(pl.multiple_of(order_ref[place] * rows, 16), rows), :]
        copies.append(pltpu.make_async_copy(piece, target, sems.at[place]))
    return copies


def project_own_kernel(count, order_ref, own_ref, gain_ref, shift_ref, bias_ref, *rest):
    pieces = rest[:count]
    normed_ref, query_ref, keyvalue_ref, whole_ref, weight_ref, sems, whole_sem = rest[count:]
    width = own_ref.shape[-1]
    seq = pl.program_id(0)
    whole = pltpu.make_async_copy(weight_ref, whole_ref, whole_sem)

    @pl.when(seq == 0)
    def _():
        copies = piece_copies(order_ref, pieces, weight_ref, sems)
        for copy in copies:
            copy.start()
        for copy in copies:
            copy.wait()
        whole.start()

    unit, _ = norm_parts(own_ref[0].astype(F32))
    normed = (unit * gain_ref[...] + shift_ref[...]).astype(BF16)
    normed_ref[0] = normed
    joint = (dot(normed, weight_ref[...]) + bias_ref[...]).astype(BF16)
    query_ref[0] = joint[:, :width]
    keyvalue_ref[0] = joint[:, width:]

    @pl.when(seq == pl.num_programs(0) - 1)
    def _():
        whole.wait()


def project_own(order, own, gain, shift, bias, pieces, length):
    seqs, block, width = own.shape
    last = length // block - 1
    fixed = lambda s, order: (0, 0)
    spot = lambda s, order: (s, 0, 0)
    end = lambda s, order: (s, last, 0)
    return pl.pallas_call(
        functools.partial(project_own_kernel, len(pieces)),
        grid_spec=pltpu.PrefetchScalarGridSpec(
            num_scalar_prefetch=1,
            grid=(seqs,),
            in_specs=[
                pl.BlockSpec((1, block, width), spot),
                pl.BlockSpec((1, width), fixed),
                pl.BlockSpec((1, width), fixed),
                pl.BlockSpec((1, 3 * width), fixed),
            ]
            + [pl.BlockSpec(memory_space=pl.ANY)] * len(pieces),
            out_specs=[
                pl.BlockSpec((1, block, width), end),
                pl.BlockSpec((1, block, width), spot),
                pl.BlockSpec((1, block, 2 * width), end),
                pl.BlockSpec(memory_space=pl.ANY),
            ],
            scratch_shapes=[
                pltpu.VMEM((width, 3 * width), BF16),
                pltpu.SemaphoreType.DMA((len(pieces),)),
                pltpu.SemaphoreType.DMA,
            ],
        ),
        out_shape=[
            jax.ShapeDtypeStruct((seqs, length, width), BF16),
            jax.ShapeDtypeStruct((seqs, block, width), BF16),
            jax.ShapeDtypeStruct((seqs, length, 2 * width), BF16),
            jax.ShapeDtypeStruct((width, 3 * width), BF16),
        ],
        compiler_params=pltpu.CompilerParams(vmem_limit_bytes=VMEM_LIMIT),
        cost_estimate=pl.CostEstimate(
            flops=6 * seqs * block * width * width, bytes_accessed=16 << 20, transcendentals=0
        ),
        name="project_own",
    )(order, own, gain, shift, bias, *pieces)


def every_tile(low_ref, seqs, tiles, work, every=False):
    for seq in range(seqs):

        def one(tile, nothing):
            work(seq, tile, pl.ds(pl.multiple_of(tile * ROW_TILE, ROW_TILE), ROW_TILE))
            return nothing

        lax.fori_loop(0 if every else low_ref[seq], tiles, one, 0)


def project_halo_kernel(
    low_ref, gain_ref, shift_ref, bias_ref, halo_any, whole_any, *rest
):
    (
        normed_any,
        keyvalue_any,
        halo_ref,
        normed_ref,
        keyvalue_ref,
        weight_ref,
        in_sems,
        normed_sems,
        keyvalue_sems,
        sem,
    ) = rest[2:]
    seqs, rows, width = halo_ref.shape
    tiles = rows // ROW_TILE
    weight = pltpu.make_async_copy(whole_any.at[:, pl.ds(width, 2 * width)], weight_ref, sem)
    weight.start()

    def arrive(seq, tile, at):
        return pltpu.make_async_copy(
            halo_any.at[seq, at], halo_ref.at[seq, at], in_sems.at[seq, tile]
        )

    def leave(seq, tile, at):
        return (
            pltpu.make_async_copy(
                normed_ref.at[seq, at], normed_any.at[seq, at], normed_sems.at[seq, tile]
            ),
            pltpu.make_async_copy(
                keyvalue_ref.at[seq, at], keyvalue_any.at[seq, at], keyvalue_sems.at[seq, tile]
            ),
        )

    def begin(seq, tile, at):
        arrive(seq, tile, at).start()

    def work(seq, tile, at):
        arrive(seq, tile, at).wait()
        unit, _ = norm_parts(halo_ref[seq, at, :].astype(F32))
        normed = (unit * gain_ref[...] + shift_ref[...]).astype(BF16)
        normed_ref[seq, at, :] = normed
        keyvalue_ref[seq, at, :] = (
            dot(normed, weight_ref[...]) + bias_ref[:, width:]
        ).astype(BF16)
        for copy in leave(seq, tile, at):
            copy.start()

    def end(seq, tile, at):
        for copy in leave(seq, tile, at):
            copy.wait()

    every_tile(low_ref, seqs, tiles, begin)
    weight.wait()
    every_tile(low_ref, seqs, tiles, work)
    every_tile(low_ref, seqs, tiles, end)


def project_halo(low, halo, gain, shift, bias, whole, normed, keyvalues):
    seqs, rows, width = halo.shape
    tiles = rows // ROW_TILE
    fixed = lambda i, low: (0, 0)
    anywhere = pl.BlockSpec(memory_space=pl.ANY)
    return pl.pallas_call(
        project_halo_kernel,
        grid_spec=pltpu.PrefetchScalarGridSpec(
            num_scalar_prefetch=1,
            grid=(1,),
            in_specs=[
                pl.BlockSpec((1, width), fixed),
                pl.BlockSpec((1, width), fixed),
                pl.BlockSpec((1, 3 * width), fixed),
                anywhere,
                anywhere,
                anywhere,
                anywhere,
            ],
            out_specs=[anywhere, anywhere],
            scratch_shapes=[
                pltpu.VMEM((seqs, rows, width), BF16),
                pltpu.VMEM((seqs, rows, width), BF16),
                pltpu.VMEM((seqs, rows, 2 * width), BF16),
                pltpu.VMEM((width, 2 * width), BF16),
                pltpu.SemaphoreType.DMA((seqs, tiles)),
                pltpu.SemaphoreType.DMA((seqs, tiles)),
                pltpu.SemaphoreType.DMA((seqs, tiles)),
                pltpu.SemaphoreType.DMA,
            ],
        ),
        out_shape=[
            jax.ShapeDtypeStruct(normed.shape, BF16),
            jax.ShapeDtypeStruct(keyvalues.shape, BF16),
        ],
        input_output_aliases={6: 0, 7: 1},
        compiler_params=pltpu.CompilerParams(vmem_limit_bytes=VMEM_LIMIT),
        cost_estimate=pl.CostEstimate(
            flops=2 * seqs * rows * width * width, bytes_accessed=16 << 20, transcendentals=0
        ),
        name="project_halo",
    )(low, gain, shift, bias, halo, whole, normed, keyvalues)


def two_heads(tile):
    left = lax.broadcasted_iota(jnp.int32, tile.shape, 1) < HD
    zero = jnp.zeros_like(tile)
    return jnp.concatenate([jnp.where(left, tile, zero), jnp.where(left, zero, tile)], 0)


def visible(first_key, starts, first_query):
    shape = (KEY_TILE, starts.shape[1])
    keys = first_key + lax.broadcasted_iota(jnp.int32, shape, 0)
    queries = first_query + lax.broadcasted_iota(jnp.int32, shape, 1)
    return (keys >= starts) & (keys <= queries)


def head_rows(first, second):
    shape = (HD, first.shape[1])
    return jnp.concatenate(
        [jnp.broadcast_to(first, shape), jnp.broadcast_to(second, shape)], 0
    )


def attend_kernel(halo, low_ref, query_ref, keyvalue_ref, start_ref, out_ref, log_ref):
    seq = pl.program_id(0)
    block = query_ref.shape[1]
    width = query_ref.shape[2]
    pairs = width // PAIR
    after = lambda c: slice(width + c.start, width + c.stop)
    tiles = block // QUERY_TILE
    def rows(tile, nothing):
        here = pl.ds(pl.multiple_of(tile * QUERY_TILE, QUERY_TILE), QUERY_TILE)
        starts = start_ref[0, :, here]
        cols = [slice(p * PAIR, (p + 1) * PAIR) for p in range(pairs)]

        def step(j, carry):
            place = pl.ds(pl.multiple_of(j * KEY_TILE, KEY_TILE), KEY_TILE)
            ok = visible(j * KEY_TILE, starts, halo + tile * QUERY_TILE)
            scores = [
                dot(two_heads(keyvalue_ref[0, place, c]), query_ref[0, here, c] * 0.125, NT)
                for c in cols
            ]
            left = []
            for p in range(pairs):
                highs, totals, mixed = carry[3 * p : 3 * p + 3]
                powers, fades, sums, nexts = [], [], [], []
                for h in range(2):
                    part = jnp.where(ok, scores[p][h * KEY_TILE : (h + 1) * KEY_TILE], -1e30)
                    high = highs[h : h + 1]
                    later = jnp.maximum(high, jnp.max(part, 0, keepdims=True))
                    power = jnp.exp(part - later)
                    fade = jnp.exp(high - later)
                    sums.append(totals[h : h + 1] * fade + jnp.sum(power, 0, keepdims=True))
                    powers.append(power.astype(BF16))
                    fades.append(fade)
                    nexts.append(later)
                added = dot(
                    two_heads(keyvalue_ref[0, place, after(cols[p])]), jnp.concatenate(powers, 0), TN
                )
                left += [
                    jnp.concatenate(nexts, 0),
                    jnp.concatenate(sums, 0),
                    mixed * head_rows(*fades) + added,
                ]
            return tuple(left)

        row = jnp.zeros((2, QUERY_TILE), F32)
        done = lax.fori_loop(
            low_ref[seq * tiles + tile],
            (halo + (tile + 1) * QUERY_TILE) // KEY_TILE,
            step,
            (row - 1e30, row, jnp.zeros((PAIR, QUERY_TILE), F32)) * pairs,
        )
        for p in range(pairs):
            highs, totals, mixed = done[3 * p : 3 * p + 3]
            total = head_rows(totals[0:1], totals[1:2])
            out_ref[0, here, cols[p]] = jnp.transpose(mixed / total).astype(BF16)
            log_ref[0, p, :, here] = highs + jnp.log(totals)
        return nothing

    lax.fori_loop(0, tiles, rows, 0)


def attend(low, query, keyvalues, starts):
    seqs, block, width = query.shape
    length = keyvalues.shape[1]
    pairs = width // PAIR
    rows = pl.BlockSpec((1, block, width), lambda s, low: (s, 0, 0))
    full = pl.BlockSpec((1, length, 2 * width), lambda s, low: (s, 0, 0))
    return pl.pallas_call(
        functools.partial(attend_kernel, length - block),
        grid_spec=pltpu.PrefetchScalarGridSpec(
            num_scalar_prefetch=1,
            grid=(seqs,),
            in_specs=[rows, full, pl.BlockSpec((1, 1, block), lambda s, low: (s, 0, 0))],
            out_specs=[rows, pl.BlockSpec((1, pairs, 2, block), lambda s, low: (s, 0, 0, 0))],
        ),
        out_shape=[
            jax.ShapeDtypeStruct((seqs, block, width), BF16),
            jax.ShapeDtypeStruct((seqs, pairs, 2, block), F32),
        ],
        compiler_params=pltpu.CompilerParams(vmem_limit_bytes=VMEM_LIMIT),
        cost_estimate=pl.CostEstimate(
            flops=16 << 30, bytes_accessed=16 << 20, transcendentals=8 << 20
        ),
        name="attend",
    )(low, query, keyvalues, starts)


def attend_back_kernel(
    halo,
    low_ref,
    first_ref,
    query_ref,
    keyvalue_ref,
    start_ref,
    out_ref,
    grad_ref,
    log_ref,
    gquery_ref,
    gkeyvalue_ref,
    turned_ref,
    center_ref,
    sumk_ref,
    sumv_ref,
):
    seq = pl.program_id(0)
    block = query_ref.shape[1]
    width = query_ref.shape[2]
    pairs = width // PAIR
    after = lambda c: slice(width + c.start, width + c.stop)
    tiles = block // QUERY_TILE
    cols = [slice(p * PAIR, (p + 1) * PAIR) for p in range(pairs)]
    turned_ref[...] = jnp.zeros_like(turned_ref)
    for p in range(pairs):
        products = jnp.transpose(grad_ref[0, :, cols[p]].astype(F32) * out_ref[0, :, cols[p]].astype(F32))
        center_ref[p, 0:1, :] = jnp.sum(products[:HD], 0, keepdims=True)
        center_ref[p, 1:2, :] = jnp.sum(products[HD:], 0, keepdims=True)
    left = lax.broadcasted_iota(jnp.int32, (KEY_TILE, PAIR), 1) < HD

    def step(j, nothing):
        place = pl.ds(pl.multiple_of(j * KEY_TILE, KEY_TILE), KEY_TILE)
        sumk_ref[...] = jnp.zeros_like(sumk_ref)
        sumv_ref[...] = jnp.zeros_like(sumv_ref)
        def rows(tile, nothing):
            here = pl.ds(pl.multiple_of(tile * QUERY_TILE, QUERY_TILE), QUERY_TILE)
            last = (halo + (tile + 1) * QUERY_TILE) // KEY_TILE

            @pl.when((j >= low_ref[seq * tiles + tile]) & (j < last))
            def _():
                ok = visible(j * KEY_TILE, start_ref[0, :, here], halo + tile * QUERY_TILE)
                keys = [two_heads(keyvalue_ref[0, place, c]) for c in cols]
                queries = [query_ref[0, here, c] * 0.125 for c in cols]
                grads = [grad_ref[0, here, c] for c in cols]
                scores = [dot(k, q, NT) for k, q in zip(keys, queries)]
                gprobs = [
                    dot(two_heads(keyvalue_ref[0, place, after(c)]), g, NT) for c, g in zip(cols, grads)
                ]
                for p in range(pairs):
                    probs, gscores = [], []
                    for head in range(2):
                        part = slice(head * KEY_TILE, (head + 1) * KEY_TILE)
                        row = slice(head, head + 1)
                        prob = jnp.exp(
                            jnp.where(ok, scores[p][part] - log_ref[0, p, row, here], -1e30)
                        )
                        gscore = prob * (gprobs[p][part] - center_ref[p, row, here])
                        probs.append(prob.astype(BF16))
                        gscores.append(gscore.astype(BF16))
                    probs = jnp.concatenate(probs, 0)
                    gscores = jnp.concatenate(gscores, 0)
                    sumv_ref[p] += dot(probs, grads[p])
                    sumk_ref[p] += dot(gscores, queries[p])
                    turned_ref[p, :, here] += dot(keys[p], gscores, TN)

            return nothing

        lax.fori_loop(0, tiles, rows, 0)

        for p in range(pairs):
            gkeyvalue_ref[0, place, cols[p]] = jnp.where(
                left, sumk_ref[p, :KEY_TILE], sumk_ref[p, KEY_TILE:]
            ).astype(BF16)
            gkeyvalue_ref[0, place, after(cols[p])] = jnp.where(
                left, sumv_ref[p, :KEY_TILE], sumv_ref[p, KEY_TILE:]
            ).astype(BF16)
        return nothing

    lax.fori_loop(first_ref[seq], (halo + block) // KEY_TILE, step, 0)
    for p in range(pairs):
        gquery_ref[0, :, cols[p]] = (jnp.transpose(turned_ref[p]) * 0.125).astype(BF16)


def attend_back(low, first, query, keyvalues, starts, mixed, grad, logs):
    seqs, block, width = query.shape
    length = keyvalues.shape[1]
    pairs = width // PAIR
    rows = pl.BlockSpec((1, block, width), lambda s, low, first: (s, 0, 0))
    full = pl.BlockSpec((1, length, 2 * width), lambda s, low, first: (s, 0, 0))
    return pl.pallas_call(
        functools.partial(attend_back_kernel, length - block),
        grid_spec=pltpu.PrefetchScalarGridSpec(
            num_scalar_prefetch=2,
            grid=(seqs,),
            in_specs=[
                rows,
                full,
                pl.BlockSpec((1, 1, block), lambda s, low, first: (s, 0, 0)),
                rows,
                rows,
                pl.BlockSpec((1, pairs, 2, block), lambda s, low, first: (s, 0, 0, 0)),
            ],
            out_specs=[rows, full],
            scratch_shapes=[
                pltpu.VMEM((pairs, PAIR, block), F32),
                pltpu.VMEM((pairs, 8, block), F32),
                pltpu.VMEM((pairs, 2 * KEY_TILE, PAIR), F32),
                pltpu.VMEM((pairs, 2 * KEY_TILE, PAIR), F32),
            ],
        ),
        out_shape=[
            jax.ShapeDtypeStruct((seqs, block, width), BF16),
            jax.ShapeDtypeStruct((seqs, length, 2 * width), BF16),
        ],
        compiler_params=pltpu.CompilerParams(vmem_limit_bytes=VMEM_LIMIT),
        cost_estimate=pl.CostEstimate(
            flops=40 << 30, bytes_accessed=28 << 20, transcendentals=8 << 20
        ),
        name="attend_back",
    )(low, first, query, keyvalues, starts, mixed, grad, logs)


def slab_copies(slab_ref, merge_ref, up_ref, down_ref, sems):
    owners = slab_ref.shape[0]
    width = slab_ref.shape[2]
    rows = width // owners
    chunks = up_ref.shape[1] // width
    groups = [[], [], []]
    for owner in range(owners):
        here = pl.ds(owner * rows, rows)
        groups[0].append((slab_ref.at[owner, pl.ds(0, rows), :], merge_ref.at[here, :]))
        for c in range(chunks):
            groups[1].append(
                (
                    slab_ref.at[owner, pl.ds((1 + c) * rows, rows), :],
                    up_ref.at[here, pl.ds(c * width, width)],
                )
            )
        groups[2].append(
            (
                slab_ref.at[owner, pl.ds((1 + chunks) * rows, chunks * rows), :],
                down_ref.at[pl.ds(owner * chunks * rows, chunks * rows), :],
            )
        )
    return [
        [pltpu.make_async_copy(*pair, sems.at[k, n]) for n, pair in enumerate(group)]
        for k, group in enumerate(groups)
    ]


def mlp_kernel(
    factor_ref,
    mixed_ref,
    token_ref,
    teacher_ref,
    weight_ref,
    outbias_ref,
    gain_ref,
    shift_ref,
    upbias_ref,
    downbias_ref,
    slab_ref,
    layer_ref,
    gresid_ref,
    gmixed_ref,
    sums_ref,
    upsums_ref,
    gslab_ref,
    merge_ref,
    up_ref,
    down_ref,
    slope_ref,
    normed_ref,
    active_ref,
    ghidden_ref,
    gmlp_ref,
    gbranch_ref,
    split_ref,
    block_ref,
    sems,
    split_sems,
    block_sems,
):
    width = token_ref.shape[-1]
    hidden = up_ref.shape[1]
    step = pl.program_id(0)
    here = pl.ds(pl.multiple_of(step * MLP_TILE, MLP_TILE), MLP_TILE)
    copies = slab_copies(slab_ref, merge_ref, up_ref, down_ref, sems)

    def arrive(k):
        @pl.when(step == 0)
        def _():
            for copy in copies[k]:
                copy.wait()

    @pl.when(step == 0)
    def _():
        for group in copies:
            for copy in group:
                copy.start()
        sums_ref[...] = jnp.zeros_like(sums_ref)
        upsums_ref[...] = jnp.zeros_like(upsums_ref)

    arrive(0)
    resid = (
        token_ref[...].astype(F32) + dot(mixed_ref[here, :], merge_ref[...]) + outbias_ref[...]
    )
    unit, scale = norm_parts(resid)
    normed = (unit * gain_ref[...] + shift_ref[...]).astype(BF16)
    normed_ref[here, :] = normed
    arrive(1)
    cuts = [slice(c, c + MLP_CHUNK) for c in range(0, hidden, MLP_CHUNK)]
    result = resid + downbias_ref[...]
    for n, cols in enumerate(cuts):
        inner = dot(normed, up_ref[:, cols]) + upbias_ref[:, cols]
        square = inner * inner
        curve = jnp.tanh(0.7978845608028654 * (inner + 0.044715 * square * inner))
        half = 0.5 * (1.0 + curve)
        active = (half * inner).astype(BF16)
        active_ref[here, cols] = active
        slope_ref[:, cols] = half + 0.5 * inner * (1.0 - curve * curve) * (
            0.7978845608028654 * (1.0 + 3.0 * 0.044715 * square)
        )
        if n == 0:
            arrive(2)
        result += dot(active_ref[here, cols], down_ref[cols, :])
    layer_ref[...] = result.astype(BF16)
    error = result - teacher_ref[...].astype(F32)
    weight = weight_ref[...]
    sums_ref[4:5, :] += jnp.sum(weight * (error * error), 0, keepdims=True)
    gresult = error * (weight * factor_ref[0])
    gmlp = gresult.astype(BF16)
    gmlp_ref[here, :] = gmlp
    sums_ref[3:4, :] += jnp.sum(gmlp.astype(F32), 0, keepdims=True)
    gnormed = jnp.zeros_like(result)
    for cols in cuts:
        gactive = dot(gmlp, down_ref[cols, :], NT)
        ghidden = (gactive * slope_ref[:, cols]).astype(BF16)
        ghidden_ref[here, cols] = ghidden
        upsums_ref[0:1, cols] += jnp.sum(ghidden.astype(F32), 0, keepdims=True)
        gnormed += dot(ghidden_ref[here, cols], up_ref[:, cols], NT)
    sums_ref[1:2, :] += jnp.sum(gnormed * unit, 0, keepdims=True)
    sums_ref[2:3, :] += jnp.sum(gnormed, 0, keepdims=True)
    gresid = gresult + norm_back(gnormed, gain_ref[...], unit, scale)
    gresid_ref[...] = gresid
    gbranch = gresid.astype(BF16)
    gbranch_ref[here, :] = gbranch
    sums_ref[0:1, :] += jnp.sum(gbranch.astype(F32), 0, keepdims=True)
    gmixed_ref[...] = dot(gbranch, merge_ref[...], NT).astype(BF16)

    owners, rows, _ = split_ref.shape[1:]
    chunks = hidden // width
    share = owners // chunks

    def split_copy(index):
        return pltpu.make_async_copy(
            split_ref.at[index % 2],
            gslab_ref.at[:, pl.ds(pl.multiple_of(index * rows, 16), rows), :],
            split_sems.at[index % 2],
        )

    def block_copy(index):
        return pltpu.make_async_copy(
            block_ref.at[index % 2],
            gslab_ref.at[
                pl.ds(index * share, share), pl.ds((1 + chunks) * rows, chunks * rows), :
            ],
            block_sems.at[index % 2],
        )

    @pl.when(step == pl.num_programs(0) - 1)
    def _():
        out = dot(mixed_ref[...], gbranch_ref[...], TN).astype(BF16)
        split_ref[0] = out.reshape(owners, rows, width)
        split_copy(0).start()

        def ups(index, nothing):
            @pl.when(index >= 2)
            def _():
                split_copy(index - 2).wait()

            cols = pl.ds(pl.multiple_of((index - 1) * width, 128), width)
            out = dot(normed_ref[...], ghidden_ref[:, cols], TN).astype(BF16)
            split_ref[index % 2] = out.reshape(owners, rows, width)
            split_copy(index).start()
            return nothing

        lax.fori_loop(1, chunks + 1, ups, 0)

        def downs(index, nothing):
            @pl.when(index >= 2)
            def _():
                block_copy(index - 2).wait()

            cols = pl.ds(pl.multiple_of(index * width, 128), width)
            out = dot(active_ref[:, cols], gmlp_ref[...], TN).astype(BF16)
            block_ref[index % 2] = out.reshape(share, chunks * rows, width)
            block_copy(index).start()
            return nothing

        lax.fori_loop(0, chunks, downs, 0)
        split_copy(chunks - 1).wait()
        split_copy(chunks).wait()
        block_copy(chunks - 2).wait()
        block_copy(chunks - 1).wait()


def mlp(factor, mixed, tokens, teacher, weight, vectors, slab, extra):
    rows, width = tokens.shape
    outbias, gain, shift, upbias, downbias = vectors
    hidden = upbias.shape[1]
    chunks = hidden // width
    owners = slab.shape[0]
    few = width // owners
    tile = lambda n: pl.BlockSpec((MLP_TILE, n), lambda i: (i, 0))
    fixed = lambda m, n: pl.BlockSpec((m, n), lambda i: (0, 0))
    anywhere = pl.BlockSpec(memory_space=pl.ANY)
    shape = jax.ShapeDtypeStruct
    return pl.pallas_call(
        mlp_kernel,
        grid=(rows // MLP_TILE,),
        in_specs=[
            pl.BlockSpec(memory_space=pltpu.SMEM),
            fixed(rows, width),
            tile(width),
            tile(width),
            tile(1),
            fixed(1, width),
            fixed(1, width),
            fixed(1, width),
            fixed(1, hidden),
            fixed(1, width),
            anywhere,
        ],
        out_specs=[
            tile(width),
            tile(width),
            tile(width),
            fixed(8, width),
            fixed(8, hidden),
            anywhere,
        ],
        out_shape=[
            shape((rows, width), BF16),
            shape((rows, width), F32),
            shape((rows, width), BF16),
            shape((8, width), F32),
            shape((8, hidden), F32),
            shape((owners, (1 + 2 * chunks) * few + extra, width), BF16),
        ],
        scratch_shapes=[
            pltpu.VMEM((width, width), BF16),
            pltpu.VMEM((width, hidden), BF16),
            pltpu.VMEM((hidden, width), BF16),
            pltpu.VMEM((MLP_TILE, hidden), F32),
            pltpu.VMEM((rows, width), BF16),
            pltpu.VMEM((rows, hidden), BF16),
            pltpu.VMEM((rows, hidden), BF16),
            pltpu.VMEM((rows, width), BF16),
            pltpu.VMEM((rows, width), BF16),
            pltpu.VMEM((2, owners, few, width), BF16),
            pltpu.VMEM((2, owners // chunks, chunks * few, width), BF16),
            pltpu.SemaphoreType.DMA((3, owners * chunks)),
            pltpu.SemaphoreType.DMA((2,)),
            pltpu.SemaphoreType.DMA((2,)),
        ],
        compiler_params=pltpu.CompilerParams(vmem_limit_bytes=VMEM_LIMIT),
        cost_estimate=pl.CostEstimate(
            flops=6 * rows * width * (width + 2 * hidden),
            bytes_accessed=40 << 20,
            transcendentals=rows * hidden,
        ),
        name="mlp",
    )(factor, mixed, tokens, teacher, weight, outbias, gain, shift, upbias, downbias, slab)


def halo_back_kernel(
    low_ref,
    halo_any,
    grad_any,
    whole_any,
    out_any,
    sums_ref,
    halo_ref,
    grad_ref,
    out_ref,
    weight_ref,
    halo_sems,
    grad_sems,
    out_sems,
    sem,
):
    seqs, rows, width = halo_ref.shape
    tiles = rows // ROW_TILE
    weight = pltpu.make_async_copy(whole_any.at[:, pl.ds(width, 2 * width)], weight_ref, sem)
    weight.start()

    def arrive(seq, tile, at):
        return (
            pltpu.make_async_copy(
                halo_any.at[seq, at], halo_ref.at[seq, at], halo_sems.at[seq, tile]
            ),
            pltpu.make_async_copy(
                grad_any.at[seq, at], grad_ref.at[seq, at], grad_sems.at[seq, tile]
            ),
        )

    def leave(seq, tile, at):
        return pltpu.make_async_copy(
            out_ref.at[seq, at], out_any.at[seq, at], out_sems.at[seq, tile]
        )

    def begin(seq, tile, at):
        @pl.when(tile >= low_ref[seq])
        def _():
            for copy in arrive(seq, tile, at):
                copy.start()

        @pl.when(tile < low_ref[seq])
        def _():
            out_ref[seq, at, :] = jnp.zeros((ROW_TILE, width), BF16)
            leave(seq, tile, at).start()

    def work(seq, tile, at):
        for copy in arrive(seq, tile, at):
            copy.wait()
        grad = dot(grad_ref[seq, at, :], weight_ref[...], NT)
        unit, _ = norm_parts(halo_ref[seq, at, :].astype(F32))
        out_ref[seq, at, :] = grad.astype(BF16)
        leave(seq, tile, at).start()
        sums_ref[0:1, :] += jnp.sum(grad * unit, 0, keepdims=True)
        sums_ref[1:2, :] += jnp.sum(grad, 0, keepdims=True)

    def end(seq, tile, at):
        leave(seq, tile, at).wait()

    every_tile(low_ref, seqs, tiles, begin, every=True)
    sums_ref[...] = jnp.zeros_like(sums_ref)
    weight.wait()
    every_tile(low_ref, seqs, tiles, work)
    every_tile(low_ref, seqs, tiles, end, every=True)


def halo_back(low, halo, gkeyvalues, whole):
    seqs, rows, width = halo.shape
    tiles = rows // ROW_TILE
    anywhere = pl.BlockSpec(memory_space=pl.ANY)
    return pl.pallas_call(
        halo_back_kernel,
        grid_spec=pltpu.PrefetchScalarGridSpec(
            num_scalar_prefetch=1,
            grid=(1,),
            in_specs=[anywhere, anywhere, anywhere],
            out_specs=[anywhere, pl.BlockSpec((8, width), lambda i, low: (0, 0))],
            scratch_shapes=[
                pltpu.VMEM((seqs, rows, width), BF16),
                pltpu.VMEM((seqs, rows, 2 * width), BF16),
                pltpu.VMEM((seqs, rows, width), BF16),
                pltpu.VMEM((width, 2 * width), BF16),
                pltpu.SemaphoreType.DMA((seqs, tiles)),
                pltpu.SemaphoreType.DMA((seqs, tiles)),
                pltpu.SemaphoreType.DMA((seqs, tiles)),
                pltpu.SemaphoreType.DMA,
            ],
        ),
        out_shape=[
            jax.ShapeDtypeStruct((seqs, rows, width), BF16),
            jax.ShapeDtypeStruct((8, width), F32),
        ],
        compiler_params=pltpu.CompilerParams(vmem_limit_bytes=VMEM_LIMIT),
        cost_estimate=pl.CostEstimate(
            flops=4 << 30, bytes_accessed=16 << 20, transcendentals=0
        ),
        name="halo_back",
    )(low, halo, gkeyvalues, whole)


def own_back_kernel(
    low_ref,
    own_any,
    normed_any,
    gquery_any,
    gkeyvalue_any,
    whole_any,
    gnormed_any,
    gweight_any,
    sums_ref,
    own_ref,
    normed_ref,
    gquery_ref,
    gkeyvalue_ref,
    weight_ref,
    total_ref,
    gnormed_ref,
    gweight_ref,
    sems,
    out_sems,
):
    seqs, block, width = own_ref.shape
    halo = normed_ref.shape[1] - block
    tiles = halo // ROW_TILE
    here = pl.ds(halo, block)
    before = pl.ds(0, halo)
    first = [
        pltpu.make_async_copy(normed_any.at[:, here], normed_ref.at[:, here], sems.at[0]),
        pltpu.make_async_copy(gkeyvalue_any.at[:, here], gkeyvalue_ref.at[:, here], sems.at[1]),
        pltpu.make_async_copy(gquery_any, gquery_ref, sems.at[2]),
    ]
    later = [
        pltpu.make_async_copy(normed_any.at[:, before], normed_ref.at[:, before], sems.at[3]),
        pltpu.make_async_copy(gkeyvalue_any.at[:, before], gkeyvalue_ref.at[:, before], sems.at[4]),
    ]
    last = [
        pltpu.make_async_copy(whole_any, weight_ref, sems.at[5]),
        pltpu.make_async_copy(own_any, own_ref, sems.at[6]),
    ]
    for copy in first + later + last:
        copy.start()
    for copy in first:
        copy.wait()
    rows = seqs * block
    gweight_ref[:, :width] = dot(
        normed_ref[:, halo:, :].reshape(rows, width), gquery_ref[...].reshape(rows, width), TN
    ).astype(BF16)

    def whole(k, nothing):
        cols = pl.ds(pl.multiple_of(k * width, 128), width)
        total_ref[:, cols] = dot(
            normed_ref[:, halo:, :].reshape(rows, width),
            gkeyvalue_ref[:, halo:, cols].reshape(rows, width),
            TN,
        )
        return nothing

    lax.fori_loop(0, 2, whole, 0)
    sums_ref[...] = jnp.zeros_like(sums_ref)
    sums_ref[2:3, :] = jnp.sum(
        gquery_ref[...].reshape(rows, width).astype(F32), 0, keepdims=True
    )
    sums_ref[3:4, :] = jnp.sum(
        gkeyvalue_ref[:, halo:, width:].reshape(rows, width).astype(F32), 0, keepdims=True
    )
    for copy in later:
        copy.wait()

    def add(seq, tile, at):
        total_ref[...] += dot(normed_ref[seq, at, :], gkeyvalue_ref[seq, at, :], TN)
        sums_ref[3:4, :] += jnp.sum(gkeyvalue_ref[seq, at, width:].astype(F32), 0, keepdims=True)

    every_tile(low_ref, seqs, tiles, add)
    gweight_ref[:, width:] = total_ref[...].astype(BF16)
    send = pltpu.make_async_copy(gweight_ref, gweight_any, out_sems.at[0])
    send.start()
    for copy in last:
        copy.wait()

    def lead(seq, nothing):
        grad = dot(gquery_ref[seq], weight_ref[:, :width], NT)
        grad += dot(gkeyvalue_ref[seq, halo:, :], weight_ref[:, width:], NT)
        gnormed_ref[seq] = grad
        unit, _ = norm_parts(own_ref[seq].astype(F32))
        sums_ref[0:1, :] += jnp.sum(grad * unit, 0, keepdims=True)
        sums_ref[1:2, :] += jnp.sum(grad, 0, keepdims=True)
        return nothing

    lax.fori_loop(0, seqs, lead, 0)
    back = pltpu.make_async_copy(gnormed_ref, gnormed_any, out_sems.at[1])
    back.start()
    send.wait()
    back.wait()


def own_back(low, own, normed, gquery, gkeyvalues, whole):
    seqs, block, width = own.shape
    length = normed.shape[1]
    anywhere = pl.BlockSpec(memory_space=pl.ANY)
    return pl.pallas_call(
        own_back_kernel,
        grid_spec=pltpu.PrefetchScalarGridSpec(
            num_scalar_prefetch=1,
            grid=(1,),
            in_specs=[anywhere] * 5,
            out_specs=[anywhere, anywhere, pl.BlockSpec((8, width), lambda i, low: (0, 0))],
            scratch_shapes=[
                pltpu.VMEM((seqs, block, width), BF16),
                pltpu.VMEM((seqs, length, width), BF16),
                pltpu.VMEM((seqs, block, width), BF16),
                pltpu.VMEM((seqs, length, 2 * width), BF16),
                pltpu.VMEM((width, 3 * width), BF16),
                pltpu.VMEM((width, 2 * width), F32),
                pltpu.VMEM((seqs, block, width), F32),
                pltpu.VMEM((width, 3 * width), BF16),
                pltpu.SemaphoreType.DMA((7,)),
                pltpu.SemaphoreType.DMA((2,)),
            ],
        ),
        out_shape=[
            jax.ShapeDtypeStruct((seqs, block, width), F32),
            jax.ShapeDtypeStruct((width, 3 * width), BF16),
            jax.ShapeDtypeStruct((8, width), F32),
        ],
        compiler_params=pltpu.CompilerParams(vmem_limit_bytes=VMEM_LIMIT),
        cost_estimate=pl.CostEstimate(
            flops=16 << 30, bytes_accessed=24 << 20, transcendentals=0
        ),
        name="own_back",
    )(low, own, normed, gquery, gkeyvalues, whole)


def finish_kernel(seqs, own_ref, gnormed_ref, gresid_ref, gain_ref, *rest):
    near_refs, far_refs = rest[:seqs], rest[seqs:-2]
    out_ref, total_ref = rest[-2:]
    unit, scale = norm_parts(own_ref[0].astype(F32))
    for seq, near_ref in enumerate(near_refs):

        @pl.when(pl.program_id(0) == seq)
        def _():
            total_ref[...] = gnormed_ref[0] + near_ref[...].astype(F32)

    for far_ref in far_refs:

        @pl.when(pl.program_id(1) == pl.num_programs(1) - 1)
        def _():
            total_ref[-HALO_CHUNK:, :] += far_ref[0].astype(F32)

    out_ref[0] = (gresid_ref[0] + norm_back(total_ref[...], gain_ref[...], unit, scale)).astype(BF16)


def finish(own, gnormed, near, far, gresid, gain):
    seqs, block, width = own.shape
    tile = pl.BlockSpec((1, ROW_TILE, width), lambda s, t: (s, t, 0))
    last = pl.BlockSpec((1, HALO_CHUNK, width), lambda s, t: (s, 0, 0))
    return pl.pallas_call(
        functools.partial(finish_kernel, seqs),
        grid=(seqs, block // ROW_TILE),
        in_specs=[tile, tile, tile, pl.BlockSpec((1, width), lambda s, t: (0, 0))]
        + [pl.BlockSpec((ROW_TILE, width), lambda s, t: (t, 0))] * seqs
        + [last] * len(far),
        out_specs=tile,
        out_shape=jax.ShapeDtypeStruct(own.shape, BF16),
        scratch_shapes=[pltpu.VMEM((ROW_TILE, width), F32)],
        cost_estimate=pl.CostEstimate(
            flops=20 * seqs * block * width,
            bytes_accessed=14 * seqs * block * width,
            transcendentals=0,
        ),
        name="finish",
    )(own, gnormed, gresid, gain, *near, *far)


def swap(x, axis, bit):
    size = lax.axis_size(axis)
    return lax.ppermute(x, axis, [(i, i ^ bit) for i in range(size)])


def shift(x, axis, step):
    size = lax.axis_size(axis)
    return lax.ppermute(
        x, axis, [(i, i + step) for i in range(size) if 0 <= i + step < size]
    )


def sum_over(x, axis):
    bit = 1
    while bit < lax.axis_size(axis):
        x = x + swap(x, axis, bit)
        bit *= 2
    return x


def max_over(x, axis):
    bit = 1
    while bit < lax.axis_size(axis):
        x = jnp.maximum(x, swap(x, axis, bit))
        bit *= 2
    return x


def gather_near(shard):
    size = lax.axis_size("fsdp")
    if size != 8:
        return [lax.all_gather(shard, "fsdp", axis=0, tiled=True)]
    return [shard] + [swap(shard, "fsdp", 2 * d) for d in range(1, size // 2)]


def gather_rest(near):
    if lax.axis_size("fsdp") != 8:
        return near
    return near + [swap(piece, "fsdp", 1) for piece in near]


def piece_order():
    size = lax.axis_size("fsdp")
    me = lax.axis_index("fsdp").astype(jnp.int32)
    if size != 8:
        return jnp.zeros((1,), jnp.int32)
    return jnp.stack(
        [me ^ (2 * d) for d in range(size // 2)] + [me ^ (2 * d) ^ 1 for d in range(size // 2)]
    )


def sum_seq(total):
    if lax.axis_size("seq") != 4:
        return lax.psum(total, "seq")
    return sum_seq_rest(sum_seq_first(total))


def sum_seq_first(total):
    rows, columns = total.shape
    odd = lax.axis_index("seq") % 2
    halves = total.reshape(2, rows // 2, columns)
    pick = lambda k: lax.dynamic_index_in_dim(halves, k, 0, keepdims=False)
    return (pick(odd).astype(F32) + swap(pick(1 - odd), "seq", 1).astype(F32)).astype(BF16)


def sum_seq_rest(half):
    odd = lax.axis_index("seq") % 2
    half = (half.astype(F32) + swap(half, "seq", 2).astype(F32)).astype(BF16)
    back = swap(half, "seq", 1)
    return jnp.where(
        odd == 0, jnp.concatenate([half, back], 0), jnp.concatenate([back, half], 0)
    )


def reduce_rows(parts, extra, *first):
    size = lax.axis_size("fsdp")
    me = lax.axis_index("fsdp")
    if size != 8:
        parts = jnp.concatenate([parts, extra], 1)
        total = lax.psum_scatter(parts, "fsdp", scatter_dimension=0, tiled=False)
        return lax.psum(total, "seq"), *first
    rows, columns = parts.shape[1:]
    few = extra.shape[1]
    core = me % 2
    chip = me // 2
    pick = lambda a, k, ax: lax.dynamic_index_in_dim(a, k, ax, keepdims=False)
    parts = parts.reshape(size // 2, 2, rows, columns)
    extra = extra.reshape(size // 2, 2, few, columns)
    half = lambda k: jnp.concatenate([pick(parts, k, 1), pick(extra, k, 1)], 1)
    other = swap(half(1 - core), "fsdp", 1)
    mine = (half(core).astype(F32) + other.astype(F32)).astype(BF16)
    arrived = [
        swap(pick(mine, chip ^ d, 0), "fsdp", 2 * d) for d in range(1, size // 2)
    ]
    arrived, *first = lax.optimization_barrier((arrived, *first))
    total = pick(mine, chip, 0).astype(F32)
    for part in arrived:
        total = total + part.astype(F32)
    return sum_seq(total.astype(BF16)), *first


def gather_slab(outweight, fcweight, projweight, *first):
    width = outweight.shape[1]
    cuts = fcweight.shape[1] // width

    def join(out, up, down, axis):
        ups = [lax.slice_in_dim(up, c * width, (c + 1) * width, axis=-1) for c in range(cuts)]
        return jnp.concatenate([out, *ups, down], axis)

    if lax.axis_size("fsdp") == SHARES:
        slab = join(outweight, fcweight, projweight, 0)
        slab, *first = lax.optimization_barrier((slab, *first))
        return lax.all_gather(slab, "fsdp", axis=0, tiled=False), *first
    whole = [
        lax.all_gather(w, "fsdp", axis=0, tiled=True) for w in (outweight, fcweight, projweight)
    ]
    return join(*(w.reshape(SHARES, -1, w.shape[1]) for w in whole), 1), *first


def reduce_slab(slab, width, hidden):
    owners = lax.axis_size("fsdp")
    cuts = hidden // width
    rows = width // SHARES

    def part(array, axis):
        at = lambda a, b: lax.slice_in_dim(array, a * rows, b * rows, axis=axis)
        ups = [at(1 + c, 2 + c) for c in range(cuts)]
        rest = lax.slice_in_dim(array, (1 + 2 * cuts) * rows, array.shape[axis], axis=axis)
        return at(0, 1), jnp.concatenate(ups, -1), at(1 + cuts, 1 + 2 * cuts), rest

    if owners == SHARES:
        return part(slab.astype(F32), 0)
    *grads, rest = part(slab, 1)
    grads = [
        lax.psum(
            lax.psum_scatter(
                g.reshape(-1, g.shape[-1]), "fsdp", scatter_dimension=0, tiled=True
            ),
            "seq",
        ).astype(F32)
        for g in grads
    ]
    rest = lax.psum(rest.astype(F32), ("fsdp", "seq"))
    return *grads, rest


def local(
    tokens,
    teacher,
    segment_ids,
    latent_flags,
    valid_mask,
    attngain,
    attnshift,
    qkvweight,
    qvbias,
    outweight,
    outbias,
    mlpgain,
    mlpshift,
    fcweight,
    fcbias,
    projweight,
    projbias,
):
    seqs, block, width = tokens.shape
    groups = lax.axis_size("seq")
    owners = lax.axis_size("fsdp")
    rows = seqs * block
    halo_rows = (groups - 1) * block
    far_rows = halo_rows - block
    me = lax.axis_index("fsdp")
    place = lax.axis_index("seq").astype(jnp.int32)
    hidden = fcweight.shape[1]

    order = piece_order()
    qkv_pieces = gather_near(qkvweight)

    weight = (valid_mask * (1 - latent_flags)).astype(F32)
    below = jnp.sum(
        (segment_ids[:, :, None] < jnp.arange(1, 4, dtype=jnp.int32)).astype(jnp.int32), 1
    )
    facts = jnp.concatenate([below.reshape(-1), jnp.sum(weight).astype(jnp.int32)[None]])
    facts = sum_over(facts, "seq")
    bounds = facts[:-1].reshape(seqs, 3)

    sent, facts = lax.optimization_barrier((tokens, facts))
    near = [shift(sent[s], "seq", 1) for s in range(seqs)]
    far = shift(sent[:, block - HALO_CHUNK :], "seq", 2) if far_rows > 0 else None

    def start_of(positions):
        found = jnp.zeros((seqs,) + positions.shape, jnp.int32)
        for d in range(3):
            bound = bounds[:, d].reshape((seqs,) + (1,) * positions.ndim)
            found = jnp.maximum(found, jnp.where(bound <= positions[None], bound, 0))
        return found

    firsts = jnp.arange(groups, dtype=jnp.int32) * block
    reach = jnp.max(firsts[None] - start_of(firsts)) - block
    chunks = jnp.maximum(reach + HALO_CHUNK - 1, 0) // HALO_CHUNK

    shards = [attngain, attnshift, qvbias, outbias, mlpgain, mlpshift, fcbias, projbias]
    packed = jnp.concatenate(shards).astype(F32)
    table = jnp.where(
        lax.broadcasted_iota(jnp.int32, (owners, packed.shape[0]), 0) == me,
        packed[None],
        0.0,
    )
    line = lax.broadcasted_iota(jnp.int32, (8, packed.shape[0]), 0)
    table = jnp.concatenate(
        [
            table,
            jnp.where(line == 0, facts[-1].astype(F32), jnp.where(line == 1, chunks.astype(F32), 0.0)),
        ],
        0,
    )
    is_reach = lax.broadcasted_iota(jnp.int32, table.shape, 0) == owners + 1
    bit = 1
    while bit < owners:
        other = swap(table, "fsdp", bit)
        table = jnp.where(is_reach, jnp.maximum(table, other), table + other)
        bit *= 2
    qkv_pieces = gather_rest(qkv_pieces)
    slab, qkv_pieces, table, near[0] = gather_slab(
        outweight, fcweight, projweight, qkv_pieces, table, near[0]
    )

    count = table[owners, 0]
    chunks = table[owners + 1, 0].astype(jnp.int32)
    vectors = []
    at = 0
    for shard in shards:
        size = shard.shape[0]
        vectors.append(table[:owners, at : at + size].reshape(1, size * owners))
        at += size
    gain1, shift1, bias1, outbias_v, gain2, shift2, upbias, downbias = vectors


    base = (place - (groups - 1)) * block
    starts = start_of(place * block + jnp.arange(block, dtype=jnp.int32)) - base
    low_rows = starts[:, ::QUERY_TILE]
    low = (low_rows // KEY_TILE).reshape(-1)
    low_tile = starts[:, 0] // ROW_TILE
    first = low_tile * (ROW_TILE // KEY_TILE)
    starts = starts[:, None, :]

    bias1 = jnp.concatenate([bias1[:, :width], jnp.zeros((1, width), F32), bias1[:, width:]], 1)
    normed, query, keyvalues, qkv = project_own(
        order, tokens, gain1, shift1, bias1, qkv_pieces, halo_rows + block
    )
    halo = jnp.stack(near)
    if far_rows > 0:
        blank = jnp.zeros((seqs, far_rows - HALO_CHUNK, width), BF16)
        halo = jnp.concatenate([blank, far, halo], 1)

    def fetch(state):
        j, halo = state
        sent = lax.dynamic_slice_in_dim(halo, halo_rows - HALO_CHUNK * (j + 1), HALO_CHUNK, 1)
        came = shift(sent, "seq", 1)
        return j + 1, lax.dynamic_update_slice_in_dim(
            halo, came, far_rows - HALO_CHUNK * (j + 1), 1
        )

    if far_rows > 0:
        _, halo = lax.while_loop(lambda state: state[0] < chunks, fetch, (jnp.int32(1), halo))

    normed, keyvalues = project_halo(
        low_tile, halo, gain1, shift1, bias1, qkv, normed, keyvalues
    )
    mixed, logs = attend(low, query, keyvalues, starts)

    factor = (rows * owners * groups) / count
    layer_out, gresid, gmixed, sums, upsums, outer = mlp(
        factor.reshape(1),
        mixed.reshape(rows, width),
        tokens.reshape(rows, width),
        teacher.reshape(rows, width),
        weight.reshape(rows, 1),
        (outbias_v, gain2, shift2, upbias, downbias),
        slab,
        SMALL_ROWS,
    )

    small = jnp.concatenate(
        [upsums[0].reshape(SHARES, -1)] + [sums[k].reshape(SHARES, -1) for k in range(4)], 1
    )
    line = lax.broadcasted_iota(jnp.int32, (SHARES, SMALL_ROWS, width), 1)
    small = jnp.where(line == 0, small[:, None, :], jnp.where(line == 1, sums[4], 0.0))
    outer = lax.dynamic_update_slice_in_dim(
        outer, small.astype(BF16), outer.shape[1] - SMALL_ROWS, 1
    )
    outer, gmixed = lax.optimization_barrier((outer, gmixed))
    staged = owners == SHARES and groups == 4
    if owners == SHARES:
        outer = lax.psum_scatter(outer, "fsdp", scatter_dimension=0, tiled=False)
        outer = sum_seq_first(outer) if staged else sum_seq(outer)

    gquery, gkeyvalues = attend_back(
        low, first, query, keyvalues, starts, mixed, gmixed.reshape(seqs, block, width), logs
    )
    ghalo, halo_sums = halo_back(low_tile, halo, gkeyvalues, qkv)

    def give(state):
        j, ghalo = state
        j = j - 1
        sent = lax.dynamic_slice_in_dim(ghalo, far_rows - HALO_CHUNK * (j + 1), HALO_CHUNK, 1)
        came = shift(sent, "seq", -1)
        spot = halo_rows - HALO_CHUNK * (j + 1)
        held = lax.dynamic_slice_in_dim(ghalo, spot, HALO_CHUNK, 1)
        total = (held.astype(F32) + came.astype(F32)).astype(BF16)
        return j, lax.dynamic_update_slice_in_dim(ghalo, total, spot, 1)

    if far_rows > 0:
        _, ghalo = lax.while_loop(lambda state: state[0] > 1, give, (chunks, ghalo))

    ghalo, gquery = lax.optimization_barrier((ghalo, gquery))
    near = [shift(ghalo[s, far_rows:], "seq", -1) for s in range(seqs)]
    far = []
    if far_rows > 0:
        far = [shift(ghalo[:, far_rows - HALO_CHUNK : far_rows], "seq", -2)]
    gnormed, gweight, own_sums = own_back(
        low_tile, tokens, normed, gquery, gkeyvalues, qkv
    )
    late = jnp.concatenate(
        [(own_sums[k] + halo_sums[k]).reshape(owners, -1) for k in range(2)]
        + [own_sums[2:4].reshape(owners, -1)],
        1,
    ).astype(BF16)
    late = jnp.pad(late, ((0, 0), (0, 2 * width + width - late.shape[1])))
    line = lax.broadcasted_iota(jnp.int32, (owners, 16, 3 * width), 1)
    late = jnp.where(line == 0, late[:, None, :], jnp.zeros((), BF16))
    gweight, near[0] = lax.optimization_barrier((gweight, near[0]))
    grad_tokens = finish(
        tokens,
        gnormed,
        near,
        far,
        gresid.reshape(tokens.shape),
        gain1,
    )

    joint, outer, grad_tokens = reduce_rows(
        gweight.reshape(owners, width // owners, 3 * width), late, outer, grad_tokens
    )
    joint = joint.astype(F32)
    if staged:
        outer = sum_seq_rest(outer)
    grad_merge, grad_up, grad_down, small = reduce_slab(outer, width, hidden)

    share = width // owners
    if owners == SHARES:
        at = hidden // owners
        cuts = [small[0, :at]] + [
            small[0, at + k * share : at + (k + 1) * share] for k in range(4)
        ]
        loss_row = small[1]
    else:
        at = hidden // SHARES
        wide = width // SHARES
        full = [small[:, 0, :at].reshape(-1)] + [
            small[:, 0, at + k * wide : at + (k + 1) * wide].reshape(-1) for k in range(4)
        ]
        cuts = [
            lax.dynamic_slice_in_dim(v, me * (v.shape[0] // owners), v.shape[0] // owners)
            for v in full
        ]
        loss_row = small[0, 1]
    loss = jnp.sum(loss_row) / (width * count)
    return (
        loss,
        layer_out.reshape(tokens.shape),
        grad_tokens,
        joint[share, :share],
        joint[share, share : 2 * share],
        joint[:share],
        joint[share, 2 * share : 4 * share],
        grad_merge,
        cuts[1],
        cuts[2],
        cuts[3],
        grad_up,
        cuts[0],
        grad_down,
        cuts[4],
    )


def solution(mesh):
    placed = (
        P("fsdp", "seq", None),
        P("fsdp", "seq", None),
        P("fsdp", "seq"),
        P("fsdp", "seq"),
        P("fsdp", "seq"),
        P("fsdp"),
        P("fsdp"),
        P("fsdp", None),
        P("fsdp"),
        P("fsdp", None),
        P("fsdp"),
        P("fsdp"),
        P("fsdp"),
        P("fsdp", None),
        P("fsdp"),
        P("fsdp", None),
        P("fsdp"),
    )
    return jax.shard_map(
        local,
        mesh=mesh,
        in_specs=placed,
        out_specs=(
            P(),
            P("fsdp", "seq", None),
            P("fsdp", "seq", None),
            P("fsdp"),
            P("fsdp"),
            P("fsdp", None),
            P("fsdp"),
            P("fsdp", None),
            P("fsdp"),
            P("fsdp"),
            P("fsdp"),
            P("fsdp", None),
            P("fsdp"),
            P("fsdp", None),
            P("fsdp"),
        ),
        check_vma=False,
    )
```

time: 503 us -> 431 us (0.86)
  Pallas kernels: 194 us -> 145 us
  starting transfers between devices: 66.2 us -> 45.9 us
    ppermute x22, starting transfers between devices: 50 us -> 29.4 us  [swap(): return lax.ppermute(x, axis, [(i, i ^ bit) for i in range(size)])]
    pallas_call x5, Pallas kernels: 110 us -> 90.8 us  [the longest x1 55.6 us: mlp(): pl.pallas_call(mlp_kernel, grid=(rows // MLP_TILE,), in_specs=[pl.BlockSp...]
    pallas_call x1, Pallas kernels: 35.7 us -> 19.5 us  [attend(): pl.pallas_call(functools.partial(attend_kernel, length - block), grid_spe...]
    pallas_call x1, Pallas kernels: 40.6 us -> 27.2 us  [attend_back(): pl.pallas_call(functools.partial(attend_back_kernel, length - block), gri...]
    ppermute x6, waiting for transfers between devices: 80.1 us -> 72 us  [shift(): lax.ppermute(x, axis, [(i, i + step) for i in range(size) if 0 <= i + ste...]
    all_gather x1, waiting for transfers between devices: 0.01 us -> 7.33 us  [gather_slab(): return (lax.all_gather(slab, 'fsdp', axis=0, tiled=False), *first)]
  transfers between devices with their start and end apart: 30 -> 30, of which waited for: 14 -> 15; matrix products, arithmetic and copies ran while one was open for 11% -> 12% of each run, Pallas kernels for 25% -> 21%
where the time goes in v3:
time: 431 us; the launch traced here: 428 us
  waiting for transfers between devices  150 us (35%)
  Pallas kernels  145 us (34%)
  starting transfers between devices  45.9 us (11%)
  local copies, waits for them, and re-layouts  42.3 us (10%)
  other arithmetic  24.5 us (6%)
  between operations  20.3 us (5%)
    ppermute x6, waiting for transfers between devices, shift(): lax.ppermute(x, axis, [(i, i + step) for i in range(size) if 0 <= i + ste...  72 us
    ppermute x22, waiting for transfers between devices, swap(): return lax.ppermute(x, axis, [(i, i ^ bit) for i in range(size)])  70.6 us
    pallas_call x1, Pallas kernels, mlp(): pl.pallas_call(mlp_kernel, grid=(rows // MLP_TILE,), in_specs=[pl.BlockSp...  55.6 us
    ppermute x22, starting transfers between devices, swap(): return lax.ppermute(x, axis, [(i, i ^ bit) for i in range(size)])  29.4 us
    pallas_call x1, Pallas kernels, attend_back(): pl.pallas_call(functools.partial(attend_back_kernel, length - block), gri...  27.2 us
    pallas_call x1, Pallas kernels, attend(): pl.pallas_call(functools.partial(attend_kernel, length - block), grid_spe...  19.5 us
    ppermute x6, starting transfers between devices, shift(): lax.ppermute(x, axis, [(i, i + step) for i in range(size) if 0 <= i + ste...  16.4 us
    pallas_call x1, Pallas kernels, own_back(): pl.pallas_call(own_back_kernel, grid_spec=pltpu.PrefetchScalarGridSpec(nu...  16.1 us
  transfers between devices with their start and end apart: 30, of which 15 were waited for; matrix products, arithmetic and copies ran while one was open for 12% of the time, Pallas kernels for 21%

profile of v3, /device:TPU:0, one launch (start us, length us, event | category | flops | bytes accessed | tf_op | source)
XLA Modules:
  0.0 427.6 jit_solution(9446452912507036284)
XLA Ops:
  22.7 5.5 %concatenate.52 = bf16[1152]{0:T(1024)(128)(2,1)S(1)} concatenate(bf16[96]{0:T(256)(128)(2,1)} %param.26, bf16[96]{0:T(256)(128)(2,1)} %param.27, bf16[192]{0:T(256)(128)(2,1)} %param.29, bf16[96]{0:T(256)(128)(2,1)} %param.31, bf16[96]{0:T(256)(128)(2,1)} %param.32, bf16[96]{0:T(256)(128)(2,1)} %param.33, bf16[384]{0:T(512)(128)(2,1)} %param.35, bf16[96]{0:T(256)(128)(2,1)} %param.37), dimensions={0} | concatenate | bytes 4608 | tf_op jit(solution)/shard_map/concatenate | solution.py:1205
  53.4 8.7 %collective-permute-done.14 = bf16[512,768]{1,0:T(8,128)(2,1)} collective-permute-done((bf16[512,768]{1,0:T(8,128)(2,1)}, bf16[512,768]{1,0:T(8,128)(2,1)}, u32[]{:S(2)}, u32[]{:S(2)}) %collective-permute-start.14) | collective-permute-done | bytes 786464 | tf_op jit(solution)/shard_map/ppermute | solution.py:1010
  64.0 4.7 %collective-permute-start.16 = (bf16[512,768]{1,0:T(8,128)(2,1)}, bf16[512,768]{1,0:T(8,128)(2,1)S(1)}, u32[]{:S(2)}, u32[]{:S(2)}) collective-permute-start(bf16[512,768]{1,0:T(8,128)(2,1)} %get-tuple-element.202), channel_id=1, source_target_pairs={{0,1},{1,2},{2,3},{4,5},{5,6},{6,7},{8,9},{9,10},{10,11},{12,13},{... | collective-permute-start | bytes 2359304 | tf_op jit(solution)/shard_map/ppermute | solution.py:1010
  68.7 4.3 collective-permute-start.15
  82.2 10.4 %project_own.1 = (bf16[2,2048,768]{2,1,0:T(8,128)(2,1)}, bf16[2,512,768]{2,1,0:T(8,128)(2,1)}, bf16[2,2048,1536]{2,1,0:T(8,128)(2,1)}, bf16[768,2304]{1,0:T(8,128)(2,1)}) custom-call(s32[8]{0:T(128)} %stack.47.order_ref, bf16[2,512,768]{2,1,0:T(8,128)(2,1)} %own_ref.3, f32[1,768]{1,0:T(1,128)} %reshape.422.gain_ref, f32[1,768]{1,0:T(1,128)} %reshape.423.shift_ref, ...), custom_call_target="tpu_custom_call" | custom-call | flops 3623878656 | bytes 16777216 | tf_op jit(solution)/shard_map/project_own/pallas_call | solution.py:95
  93.3 4.1 maximum_maximum_fusion
  97.4 3.4 project_halo.1
  100.7 19.5 %attend.1 = (bf16[2,512,768]{2,1,0:T(8,128)(2,1)}, f32[2,6,2,512]{3,2,1,0:T(2,128)}) custom-call(s32[8]{0:T(128)} %reshape.425.low_ref, bf16[2,512,768]{2,1,0:T(8,128)(2,1)} %get-tuple-element.134.query_ref, bf16[2,2048,1536]{2,1,0:T(8,128)(2,1)} %get-tuple-element.135.keyvalue_ref, s32[2,1,512]{2,1,0:T(1,128)} %fusion.19.start_ref), custom_call_target="tpu_custom_call" | custom-call | flops 17179869184 | bytes 16777216 | tf_op jit(solution)/shard_map/attend/pallas_call | solution.py:332
  120.2 7.3 %all-gather.3.cloned.1.call-done = bf16[6912,768]{1,0:T(8,128)(2,1)} async-done(((bf16[864,768]{1,0:T(8,128)(2,1)}), bf16[6912,768]{1,0:T(8,128)(2,1)}) %all-gather.3.cloned.1.call-update) | async-done | bytes 10616848 | tf_op jit(solution)/shard_map/all_gather | solution.py:1115
  127.5 55.6 %mlp.1 = (bf16[1024,768]{1,0:T(8,128)(2,1)}, f32[1024,768]{1,0:T(8,128)}, bf16[1024,768]{1,0:T(8,128)(2,1)}, f32[8,768]{1,0:T(8,128)}, f32[8,3072]{1,0:T(8,128)}, /*index=5*/bf16[8,880,768]{2,1,0:T(8,128)(2,1)}) custom-call(f32[1]{0:T(128)} %bitcast.15.factor_ref, bf16[1024,768]{1,0:T(8,128)(2,1)} %bitcast.98, bf16[1024,768]{1,0:T(8,128)(2,1)} %bitcast.83, ...), custom_call_target="tpu_custom_call" | custom-call | flops 32614907904 | bytes 41943040 | tf_op jit(solution)/shard_map/mlp/pallas_call | solution.py:671
  186.3 27.2 %attend_back.1 = (bf16[2,512,768]{2,1,0:T(8,128)(2,1)}, bf16[2,2048,1536]{2,1,0:T(8,128)(2,1)}) custom-call(s32[8]{0:T(128)} %reshape.425.low_ref, s32[2]{0:T(128)} %get-tuple-element.184.first_ref, bf16[2,512,768]{2,1,0:T(8,128)(2,1)} %get-tuple-element.134.query_ref, bf16[2,2048,1536]{2,1,0:T(8,128)(2,1)} %get-tuple-element.135.keyvalue_ref, ...), custom_call_target="tpu_custom_call" | custom-call | flops 42949672960 | bytes 29360128 | tf_op jit(solution)/shard_map/attend_back/pallas_call | solution.py:442
  213.6 5.3 %halo_back.1 = (bf16[2,1536,768]{2,1,0:T(8,128)(2,1)}, f32[8,768]{1,0:T(8,128)}) custom-call(s32[2]{0:T(128)} %get-tuple-element.185.low_ref, bf16[2,1536,768]{2,1,0:T(8,128)(2,1)} %get-tuple-element.121.halo_any, bf16[2,2048,1536]{2,1,0:T(8,128)(2,1)} %get-tuple-element.144.grad_any.gkeyvalue_any, bf16[768,2304]{1,0:T(8,128)(2,1)} %get-tuple-element.130.whole_any), custom_call_target="tpu_custom_call" | custom-call | flops 4294967296 | bytes 16777216 | tf_op jit(solution)/shard_map/halo_back/pallas_call | solution.py:800
  218.9 16.1 %own_back.1 = (f32[2,512,768]{2,1,0:T(8,128)}, bf16[768,2304]{1,0:T(8,128)(2,1)}, f32[8,768]{1,0:T(8,128)}) custom-call(s32[2]{0:T(128)} %get-tuple-element.185.low_ref, bf16[2,512,768]{2,1,0:T(8,128)(2,1)} %own_ref.3, bf16[2,2048,768]{2,1,0:T(8,128)(2,1)} %get-tuple-element.133.normed_any, bf16[2,512,768]{2,1,0:T(8,128)(2,1)} %get-tuple-element.148.gquery_any, ...), custom_call_target="tpu_custom_call" | custom-call | flops 17179869184 | bytes 25165824 | tf_op jit(solution)/shard_map/own_back/pallas_call | solution.py:929
  241.0 36.0 %collective-permute-done.17.rest_0_ = bf16[512,768]{1,0:T(8,128)(2,1)S(1)} collective-permute-done((bf16[512,768]{1,0:T(8,128)(2,1)S(1)}, bf16[512,768]{1,0:T(8,128)(2,1)S(1)}, u32[]{:S(2)}, u32[]{:S(2)}) %collective-permute-start.17) | collective-permute-done | bytes 786464 | tf_op jit(solution)/shard_map/ppermute | solution.py:1010
  280.8 3.5 collective-permute-start.18
  290.9 3.7 collective-permute-start.22
  300.5 26.6 %collective-permute-done.24.rest_2_ = bf16[2,128,768]{2,1,0:T(8,128)(2,1)S(1)} collective-permute-done((bf16[2,128,768]{2,1,0:T(8,128)(2,1)}, bf16[2,128,768]{2,1,0:T(8,128)(2,1)S(1)}, u32[]{:S(2)}, u32[]{:S(2)}) %collective-permute-start.24) | collective-permute-done | bytes 393248 | tf_op jit(solution)/shard_map/ppermute | solution.py:1010
  327.1 5.0 %collective-permute-start.21 = (bf16[112,2304]{1,0:T(8,128)(2,1)}, bf16[112,2304]{1,0:T(8,128)(2,1)}, u32[]{:S(2)}, u32[]{:S(2)}) collective-permute-start(bf16[112,2304]{1,0:T(8,128)(2,1)} %get-tuple-element.199), channel_id=1, source_target_pairs={{0,24},{4,28},{8,16},{12,20},{16,8},{20,12},{24,0},{28,4},{1,25},{... | collective-permute-start | bytes 1548296 | tf_op jit(solution)/shard_map/ppermute | solution.py:1005
  333.0 7.2 %finish.1 = bf16[2,512,768]{2,1,0:T(8,128)(2,1)} custom-call(bf16[2,512,768]{2,1,0:T(8,128)(2,1)} %own_ref.3, f32[2,512,768]{2,1,0:T(8,128)} %get-tuple-element.155.gnormed_ref, f32[2,512,768]{2,1,0:T(8,128)} %bitcast.85, f32[1,768]{1,0:T(1,128)} %reshape.422.gain_ref, bf16[512,768]{1,0:T(8,128)(2,1)} %copy-done.5, bf16[512,768]{1,0:T(8,128)(2,1)} %copy-done.6, ...), custom_call_target="tpu_custom_call" | custom-call | flops 15728640 | bytes 11010048 | tf_op jit(solution)/shard_map/finish/pallas_call | solution.py:985
  345.4 6.9 %collective-permute-done.27 = bf16[56,2304]{1,0:T(8,128)(2,1)S(1)} collective-permute-done((bf16[56,2304]{1,0:T(8,128)(2,1)S(1)}, bf16[56,2304]{1,0:T(8,128)(2,1)S(1)}, u32[]{:S(2)}, u32[]{:S(2)}) %collective-permute-start.27) | collective-permute-done | bytes 258080 | tf_op jit(solution)/shard_map/ppermute | solution.py:1005
  355.4 24.1 %collective-permute-done.28 = bf16[56,2304]{1,0:T(8,128)(2,1)S(1)} collective-permute-done((bf16[56,2304]{1,0:T(8,128)(2,1)S(1)}, bf16[56,2304]{1,0:T(8,128)(2,1)S(1)}, u32[]{:S(2)}, u32[]{:S(2)}) %collective-permute-start.28) | collective-permute-done | bytes 258080 | tf_op jit(solution)/shard_map/ppermute | solution.py:1005
  379.6 14.3 %collective-permute-done.25 = bf16[440,768]{1,0:T(8,128)(2,1)S(1)} collective-permute-done((bf16[440,768]{1,0:T(8,128)(2,1)S(1)}, bf16[440,768]{1,0:T(8,128)(2,1)S(1)}, u32[]{:S(2)}, u32[]{:S(2)}) %collective-permute-start.25) | collective-permute-done | bytes 675872 | tf_op jit(solution)/shard_map/ppermute | solution.py:1005
  394.9 4.6 %collective-permute-done.29 = bf16[56,2304]{1,0:T(8,128)(2,1)S(1)} collective-permute-done((bf16[56,2304]{1,0:T(8,128)(2,1)S(1)}, bf16[56,2304]{1,0:T(8,128)(2,1)S(1)}, u32[]{:S(2)}, u32[]{:S(2)}) %collective-permute-start.29) | collective-permute-done | bytes 258080 | tf_op jit(solution)/shard_map/ppermute | solution.py:1005
  401.7 12.1 %collective-permute-done.26 = bf16[440,768]{1,0:T(8,128)(2,1)S(1)} collective-permute-done((bf16[440,768]{1,0:T(8,128)(2,1)S(1)}, bf16[440,768]{1,0:T(8,128)(2,1)S(1)}, u32[]{:S(2)}, u32[]{:S(2)}) %collective-permute-start.26) | collective-permute-done | bytes 675872 | tf_op jit(solution)/shard_map/ppermute | solution.py:1005
  (179 shorter events, 91.2 us)
Async XLA Ops:
  7.2 120.3 %all-gather.3.cloned.1.call-start = ((), (), s32[]{:S(2)}) async-start(), calls=%async_computation.2 | async-start | bytes 11943936 | tf_op jit(solution)/shard_map/all_gather | solution.py:1115
  7.2 44.1 %collective-permute-start.4 = (bf16[96,2304]{1,0:T(8,128)(2,1)}, bf16[96,2304]{1,0:T(8,128)(2,1)}, u32[]{:S(2)}, u32[]{:S(2)}) collective-permute-start(bf16[96,2304]{1,0:T(8,128)(2,1)} %rest_0_), channel_id=1, source_target_pairs={{0,8},{4,12},{8,0},{12,4},{16,24},{20,28},{24,16},{28,20},{1,9},{5... | collective-permute-start | bytes 1327112 | tf_op jit(solution)/shard_map/ppermute | solution.py:1005
  10.2 41.6 %collective-permute-start.5 = (bf16[96,2304]{1,0:T(8,128)(2,1)}, bf16[96,2304]{1,0:T(8,128)(2,1)}, u32[]{:S(2)}, u32[]{:S(2)}) collective-permute-start(bf16[96,2304]{1,0:T(8,128)(2,1)} %rest_0_), channel_id=1, source_target_pairs={{0,16},{4,20},{8,24},{12,28},{16,0},{20,4},{24,8},{28,12},{1,17},{... | collective-permute-start | bytes 1327112 | tf_op jit(solution)/shard_map/ppermute | solution.py:1005
  11.8 40.1 %collective-permute-start.6 = (bf16[96,2304]{1,0:T(8,128)(2,1)}, bf16[96,2304]{1,0:T(8,128)(2,1)}, u32[]{:S(2)}, u32[]{:S(2)}) collective-permute-start(bf16[96,2304]{1,0:T(8,128)(2,1)} %rest_0_), channel_id=1, source_target_pairs={{0,24},{4,28},{8,16},{12,20},{16,8},{20,12},{24,0},{28,4},{1,25},{... | collective-permute-start | bytes 1327112 | tf_op jit(solution)/shard_map/ppermute | solution.py:1005
  14.9 13.3 %collective-permute-start.2 = (s32[7]{0:T(128)S(1)}, s32[7]{0:T(128)S(1)}, u32[]{:S(2)}, u32[]{:S(2)}) collective-permute-start(s32[7]{0:T(128)S(1)} %pad_add_fusion), channel_id=1, source_target_pairs={{0,1},{1,0},{2,3},{3,2},{4,5},{5,4},{6,7},{7,6},{8,9},{9,8},{10,11... | collective-permute-start | bytes 92 | tf_op jit(solution)/shard_map/ppermute | solution.py:1005
  42.5 19.6 %collective-permute-start.14 = (bf16[512,768]{1,0:T(8,128)(2,1)}, bf16[512,768]{1,0:T(8,128)(2,1)}, u32[]{:S(2)}, u32[]{:S(2)}) collective-permute-start(bf16[512,768]{1,0:T(8,128)(2,1)} %get-tuple-element.203), channel_id=1, source_target_pairs={{0,1},{1,2},{2,3},{4,5},{5,6},{6,7},{8,9},{9,10},{10,11},{12,13},{... | collective-permute-start | bytes 2359304 | tf_op jit(solution)/shard_map/ppermute | solution.py:1010
  51.3 10.9 %collective-permute-start.8 = (bf16[96,2304]{1,0:T(8,128)(2,1)}, bf16[96,2304]{1,0:T(8,128)(2,1)}, u32[]{:S(2)}, u32[]{:S(2)}) collective-permute-start(bf16[96,2304]{1,0:T(8,128)(2,1)} %collective-permute-done.4.rest_1_), channel_id=1, source_target_pairs={{0,4},{4,0},{8,12},{12,8},{16,20},{20,16},{24,28},{28,24},{1,5},{5... | collective-permute-start | bytes 1327112 | tf_op jit(solution)/shard_map/ppermute | solution.py:1005
  51.8 10.4 %collective-permute-start.9 = (bf16[96,2304]{1,0:T(8,128)(2,1)}, bf16[96,2304]{1,0:T(8,128)(2,1)}, u32[]{:S(2)}, u32[]{:S(2)}) collective-permute-start(bf16[96,2304]{1,0:T(8,128)(2,1)} %collective-permute-done.5.rest_2_), channel_id=1, source_target_pairs={{0,4},{4,0},{8,12},{12,8},{16,20},{20,16},{24,28},{28,24},{1,5},{5... | collective-permute-start | bytes 1327112 | tf_op jit(solution)/shard_map/ppermute | solution.py:1005
  51.9 10.3 %collective-permute-start.10 = (bf16[96,2304]{1,0:T(8,128)(2,1)}, bf16[96,2304]{1,0:T(8,128)(2,1)}, u32[]{:S(2)}, u32[]{:S(2)}) collective-permute-start(bf16[96,2304]{1,0:T(8,128)(2,1)} %collective-permute-done.6.rest_3_), channel_id=1, source_target_pairs={{0,4},{4,0},{8,12},{12,8},{16,20},{20,16},{24,28},{28,24},{1,5},{5... | collective-permute-start | bytes 1327112 | tf_op jit(solution)/shard_map/ppermute | solution.py:1005
  62.2 226.7 %reduce-scatter.2.cloned.1.call-start = ((), (), s32[]{:S(2)}) async-start(), calls=%async_computation.1 | async-start | bytes 12165120 | tf_op jit(solution)/shard_map/reduce_scatter | solution.py:1297
  64.0 29.3 %collective-permute-start.16 = (bf16[512,768]{1,0:T(8,128)(2,1)}, bf16[512,768]{1,0:T(8,128)(2,1)S(1)}, u32[]{:S(2)}, u32[]{:S(2)}) collective-permute-start(bf16[512,768]{1,0:T(8,128)(2,1)} %get-tuple-element.202), channel_id=1, source_target_pairs={{0,1},{1,2},{2,3},{4,5},{5,6},{6,7},{8,9},{9,10},{10,11},{12,13},{... | collective-permute-start | bytes 2359304 | tf_op jit(solution)/shard_map/ppermute | solution.py:1010
  68.7 24.6 %collective-permute-start.15 = (bf16[2,128,768]{2,1,0:T(8,128)(2,1)S(1)}, bf16[2,128,768]{2,1,0:T(8,128)(2,1)S(1)}, u32[]{:S(2)}, u32[]{:S(2)}) collective-permute-start(bf16[2,128,768]{2,1,0:T(8,128)(2,1)S(1)} %slice.195), channel_id=1, source_target_pairs={{0,2},{1,3},{4,6},{5,7},{8,10},{9,11},{12,14},{13,15},{16,18},{17,... | collective-permute-start | bytes 1179656 | tf_op jit(solution)/shard_map/ppermute | solution.py:1010
  239.5 37.5 %collective-permute-start.17 = (bf16[512,768]{1,0:T(8,128)(2,1)S(1)}, bf16[512,768]{1,0:T(8,128)(2,1)S(1)}, u32[]{:S(2)}, u32[]{:S(2)}) collective-permute-start(bf16[512,768]{1,0:T(8,128)(2,1)S(1)} %get-tuple-element.187), channel_id=1, source_target_pairs={{1,0},{2,1},{3,2},{5,4},{6,5},{7,6},{9,8},{10,9},{11,10},{13,12},{... | collective-permute-start | bytes 2359304 | tf_op jit(solution)/shard_map/ppermute | solution.py:1010
  280.8 13.9 %collective-permute-start.18 = (bf16[4,112,2304]{2,1,0:T(8,128)(2,1)}, bf16[4,112,2304]{2,1,0:T(8,128)(2,1)S(1)}, u32[]{:S(2)}, u32[]{:S(2)}) collective-permute-start(bf16[4,112,2304]{2,1,0:T(8,128)(2,1)} %pad_maximum_fusion), channel_id=1, source_target_pairs={{0,4},{4,0},{8,12},{12,8},{16,20},{20,16},{24,28},{28,24},{1,5},{5... | collective-permute-start | bytes 6193160 | tf_op jit(solution)/shard_map/ppermute | solution.py:1005
  286.1 46.0 %collective-permute-start.23 = (bf16[512,768]{1,0:T(8,128)(2,1)}, bf16[512,768]{1,0:T(8,128)(2,1)S(1)}, u32[]{:S(2)}, u32[]{:S(2)}) collective-permute-start(bf16[512,768]{1,0:T(8,128)(2,1)} %get-tuple-element.186), channel_id=1, source_target_pairs={{1,0},{2,1},{3,2},{5,4},{6,5},{7,6},{9,8},{10,9},{11,10},{13,12},{... | collective-permute-start | bytes 2359304 | tf_op jit(solution)/shard_map/ppermute | solution.py:1010
  287.4 39.8 %collective-permute-start.24 = (bf16[2,128,768]{2,1,0:T(8,128)(2,1)}, bf16[2,128,768]{2,1,0:T(8,128)(2,1)S(1)}, u32[]{:S(2)}, u32[]{:S(2)}) collective-permute-start(bf16[2,128,768]{2,1,0:T(8,128)(2,1)} %slice.218), channel_id=1, source_target_pairs={{2,0},{3,1},{6,4},{7,5},{10,8},{11,9},{14,12},{15,13},{18,16},{19,... | collective-permute-start | bytes 1179656 | tf_op jit(solution)/shard_map/ppermute | solution.py:1010
  290.9 49.3 %collective-permute-start.22 = (bf16[440,768]{1,0:T(8,128)(2,1)}, bf16[440,768]{1,0:T(8,128)(2,1)}, u32[]{:S(2)}, u32[]{:S(2)}) collective-permute-start(bf16[440,768]{1,0:T(8,128)(2,1)} %dynamic-slice_bitcast_fusion.2), channel_id=1, source_target_pairs={{0,1},{1,0},{2,3},{3,2},{4,5},{5,4},{6,7},{7,6},{8,9},{9,8},{10,11... | collective-permute-start | bytes 2027528 | tf_op jit(solution)/shard_map/ppermute | solution.py:1005
  299.8 41.7 %collective-permute-start.19 = (bf16[112,2304]{1,0:T(8,128)(2,1)}, bf16[112,2304]{1,0:T(8,128)(2,1)}, u32[]{:S(2)}, u32[]{:S(2)}) collective-permute-start(bf16[112,2304]{1,0:T(8,128)(2,1)} %get-tuple-element.201), channel_id=1, source_target_pairs={{0,8},{4,12},{8,0},{12,4},{16,24},{20,28},{24,16},{28,20},{1,9},{5... | collective-permute-start | bytes 1548296 | tf_op jit(solution)/shard_map/ppermute | solution.py:1005
  299.8 41.7 %collective-permute-start.20 = (bf16[112,2304]{1,0:T(8,128)(2,1)}, bf16[112,2304]{1,0:T(8,128)(2,1)}, u32[]{:S(2)}, u32[]{:S(2)}) collective-permute-start(bf16[112,2304]{1,0:T(8,128)(2,1)} %get-tuple-element.200), channel_id=1, source_target_pairs={{0,16},{4,20},{8,24},{12,28},{16,0},{20,4},{24,8},{28,12},{1,17},{... | collective-permute-start | bytes 1548296 | tf_op jit(solution)/shard_map/ppermute | solution.py:1005
  327.1 16.6 %collective-permute-start.21 = (bf16[112,2304]{1,0:T(8,128)(2,1)}, bf16[112,2304]{1,0:T(8,128)(2,1)}, u32[]{:S(2)}, u32[]{:S(2)}) collective-permute-start(bf16[112,2304]{1,0:T(8,128)(2,1)} %get-tuple-element.199), channel_id=1, source_target_pairs={{0,24},{4,28},{8,16},{12,20},{16,8},{20,12},{24,0},{28,4},{1,25},{... | collective-permute-start | bytes 1548296 | tf_op jit(solution)/shard_map/ppermute | solution.py:1005
  352.4 27.1 %collective-permute-start.28 = (bf16[56,2304]{1,0:T(8,128)(2,1)S(1)}, bf16[56,2304]{1,0:T(8,128)(2,1)S(1)}, u32[]{:S(2)}, u32[]{:S(2)}) collective-permute-start(bf16[56,2304]{1,0:T(8,128)(2,1)S(1)} %fusion.7), channel_id=1, source_target_pairs={{0,2},{1,3},{2,0},{3,1},{4,6},{5,7},{6,4},{7,5},{8,10},{9,11},{10,... | collective-permute-start | bytes 774152 | tf_op jit(solution)/shard_map/ppermute | solution.py:1005
  352.5 41.5 %collective-permute-start.25 = (bf16[440,768]{1,0:T(8,128)(2,1)S(1)}, bf16[440,768]{1,0:T(8,128)(2,1)S(1)}, u32[]{:S(2)}, u32[]{:S(2)}) collective-permute-start(bf16[440,768]{1,0:T(8,128)(2,1)S(1)} %fusion.2), channel_id=1, source_target_pairs={{0,2},{1,3},{2,0},{3,1},{4,6},{5,7},{6,4},{7,5},{8,10},{9,11},{10,... | collective-permute-start | bytes 2027528 | tf_op jit(solution)/shard_map/ppermute | solution.py:1005
  379.5 19.9 %collective-permute-start.29 = (bf16[56,2304]{1,0:T(8,128)(2,1)S(1)}, bf16[56,2304]{1,0:T(8,128)(2,1)S(1)}, u32[]{:S(2)}, u32[]{:S(2)}) collective-permute-start(bf16[56,2304]{1,0:T(8,128)(2,1)S(1)} %add_convert_fusion.3), channel_id=1, source_target_pairs={{0,1},{1,0},{2,3},{3,2},{4,5},{5,4},{6,7},{7,6},{8,9},{9,8},{10,11... | collective-permute-start | bytes 774152 | tf_op jit(solution)/shard_map/ppermute | solution.py:1005
  394.1 19.7 %collective-permute-start.26 = (bf16[440,768]{1,0:T(8,128)(2,1)S(1)}, bf16[440,768]{1,0:T(8,128)(2,1)S(1)}, u32[]{:S(2)}, u32[]{:S(2)}) collective-permute-start(bf16[440,768]{1,0:T(8,128)(2,1)S(1)} %add_convert_fusion.2), channel_id=1, source_target_pairs={{0,1},{1,0},{2,3},{3,2},{4,5},{5,4},{6,7},{7,6},{8,9},{9,8},{10,11... | collective-permute-start | bytes 2027528 | tf_op jit(solution)/shard_map/ppermute | solution.py:1005
  (18 other events, 196.4 us)
Sparse Core Ops, SparseCore 0:
  62.3 65.1 all-gather.2
  186.4 97.0 reduce-scatter.1

commit v4 on v3

--- a/solution.py
+++ b/solution.py
@@ -829,13 +829,15 @@
 
 def own_back_kernel(
     low_ref,
+    order_ref,
     own_any,
     normed_any,
     gquery_any,
     gkeyvalue_any,
     whole_any,
     gnormed_any,
-    gweight_any,
+    keep_any,
+    give_any,
     sums_ref,
     own_ref,
     normed_ref,
@@ -901,8 +903,18 @@
 
     every_tile(low_ref, seqs, tiles, add)
     gweight_ref[:, width:] = total_ref[...].astype(BF16)
-    send = pltpu.make_async_copy(gweight_ref, gweight_any, out_sems.at[0])
-    send.start()
+    slots = keep_any.shape[0]
+    share = width // (2 * slots)
+    sends = [
+        pltpu.make_async_copy(
+            gweight_ref.at[pl.ds(pl.multiple_of(order_ref[k] * share, 16), share), :],
+            (keep_any, give_any)[k // slots].at[k % slots, pl.ds(0, share), :],
+            out_sems.at[1 + k],
+        )
+        for k in range(2 * slots)
+    ]
+    for copy in sends:
+        copy.start()
     for copy in last:
         copy.wait()
 
@@ -916,23 +928,29 @@
         return nothing
 
     lax.fori_loop(0, seqs, lead, 0)
-    back = pltpu.make_async_copy(gnormed_ref, gnormed_any, out_sems.at[1])
+    back = pltpu.make_async_copy(gnormed_ref, gnormed_any, out_sems.at[0])
     back.start()
-    send.wait()
+    for copy in sends:
+        copy.wait()
     back.wait()
 
 
-def own_back(low, own, normed, gquery, gkeyvalues, whole):
+def own_back(low, order, own, normed, gquery, gkeyvalues, whole):
     seqs, block, width = own.shape
     length = normed.shape[1]
     anywhere = pl.BlockSpec(memory_space=pl.ANY)
     return pl.pallas_call(
         own_back_kernel,
         grid_spec=pltpu.PrefetchScalarGridSpec(
-            num_scalar_prefetch=1,
+            num_scalar_prefetch=2,
             grid=(1,),
             in_specs=[anywhere] * 5,
-            out_specs=[anywhere, anywhere, pl.BlockSpec((8, width), lambda i, low: (0, 0))],
+            out_specs=[
+                anywhere,
+                anywhere,
+                anywhere,
+                pl.BlockSpec((8, width), lambda i, low, order: (0, 0)),
+            ],
             scratch_shapes=[
                 pltpu.VMEM((seqs, block, width), BF16),
                 pltpu.VMEM((seqs, length, width), BF16),
@@ -943,12 +961,13 @@
                 pltpu.VMEM((seqs, block, width), F32),
                 pltpu.VMEM((width, 3 * width), BF16),
                 pltpu.SemaphoreType.DMA((7,)),
-                pltpu.SemaphoreType.DMA((2,)),
+                pltpu.SemaphoreType.DMA((1 + SHARES,)),
             ],
         ),
         out_shape=[
             jax.ShapeDtypeStruct((seqs, block, width), F32),
-            jax.ShapeDtypeStruct((width, 3 * width), BF16),
+            jax.ShapeDtypeStruct((SHARES // 2, width // SHARES + SMALL_ROWS, 3 * width), BF16),
+            jax.ShapeDtypeStruct((SHARES // 2, width // SHARES + SMALL_ROWS, 3 * width), BF16),
             jax.ShapeDtypeStruct((8, width), F32),
         ],
         compiler_params=pltpu.CompilerParams(vmem_limit_bytes=VMEM_LIMIT),
@@ -956,7 +975,7 @@
             flops=16 << 30, bytes_accessed=24 << 20, transcendentals=0
         ),
         name="own_back",
-    )(low, own, normed, gquery, gkeyvalues, whole)
+    )(low, order, own, normed, gquery, gkeyvalues, whole)
 
 
 def finish_kernel(seqs, own_ref, gnormed_ref, gresid_ref, gain_ref, *rest):
@@ -1054,7 +1073,7 @@
 def sum_seq(total):
     if lax.axis_size("seq") != 4:
         return lax.psum(total, "seq")
-    return sum_seq_rest(sum_seq_first(total))
+    return sum_seq_rest(sum_seq_second(sum_seq_first(total)))
 
 
 def sum_seq_first(total):
@@ -1065,40 +1084,34 @@
     return (pick(odd).astype(F32) + swap(pick(1 - odd), "seq", 1).astype(F32)).astype(BF16)
 
 
+def sum_seq_second(half):
+    return (half.astype(F32) + swap(half, "seq", 2).astype(F32)).astype(BF16)
+
+
 def sum_seq_rest(half):
     odd = lax.axis_index("seq") % 2
-    half = (half.astype(F32) + swap(half, "seq", 2).astype(F32)).astype(BF16)
     back = swap(half, "seq", 1)
     return jnp.where(
         odd == 0, jnp.concatenate([half, back], 0), jnp.concatenate([back, half], 0)
     )
 
 
-def reduce_rows(parts, extra, *first):
-    size = lax.axis_size("fsdp")
-    me = lax.axis_index("fsdp")
-    if size != 8:
-        parts = jnp.concatenate([parts, extra], 1)
-        total = lax.psum_scatter(parts, "fsdp", scatter_dimension=0, tiled=False)
-        return lax.psum(total, "seq"), *first
-    rows, columns = parts.shape[1:]
-    few = extra.shape[1]
-    core = me % 2
-    chip = me // 2
-    pick = lambda a, k, ax: lax.dynamic_index_in_dim(a, k, ax, keepdims=False)
-    parts = parts.reshape(size // 2, 2, rows, columns)
-    extra = extra.reshape(size // 2, 2, few, columns)
-    half = lambda k: jnp.concatenate([pick(parts, k, 1), pick(extra, k, 1)], 1)
-    other = swap(half(1 - core), "fsdp", 1)
-    mine = (half(core).astype(F32) + other.astype(F32)).astype(BF16)
-    arrived = [
-        swap(pick(mine, chip ^ d, 0), "fsdp", 2 * d) for d in range(1, size // 2)
+def reduce_rows(keep, give, half, *first):
+    other = swap(give, "fsdp", 1)
+    staged = lax.axis_size("seq") == 4
+    if staged:
+        half = sum_seq_first(half)
+    mine = [
+        (keep[d].astype(F32) + other[d].astype(F32)).astype(BF16) for d in range(keep.shape[0])
     ]
-    arrived, *first = lax.optimization_barrier((arrived, *first))
-    total = pick(mine, chip, 0).astype(F32)
+    arrived = [swap(part, "fsdp", 2 * d) for d, part in enumerate(mine) if d > 0]
+    arrived, half, *first = lax.optimization_barrier((arrived, half, *first))
+    if staged:
+        half = sum_seq_rest(sum_seq_second(half))
+    total = mine[0].astype(F32)
     for part in arrived:
         total = total + part.astype(F32)
-    return sum_seq(total.astype(BF16)), *first
+    return sum_seq(total.astype(BF16)), half, *first
 
 
 def gather_slab(outweight, fcweight, projweight, *first):
@@ -1183,12 +1196,20 @@
         (segment_ids[:, :, None] < jnp.arange(1, 4, dtype=jnp.int32)).astype(jnp.int32), 1
     )
     facts = jnp.concatenate([below.reshape(-1), jnp.sum(weight).astype(jnp.int32)[None]])
-    facts = sum_over(facts, "seq")
+
+    shards = [attngain, attnshift, qvbias, outbias, mlpgain, mlpshift, fcbias, projbias]
+    sent = [tokens[k] for k in range(seqs)] + [tokens[:, block - HALO_CHUNK :]]
+    bit = 1
+    while bit < groups:
+        facts = facts + swap(facts, "seq", bit)
+        if bit == 1:
+            facts, shards = lax.optimization_barrier((facts, shards))
+        bit *= 2
+
+    sent, facts = lax.optimization_barrier((sent, facts))
+    near = [shift(sent[k], "seq", 1) for k in range(seqs)]
+    far = shift(sent[seqs], "seq", 2) if far_rows > 0 else None
     bounds = facts[:-1].reshape(seqs, 3)
-
-    sent, facts = lax.optimization_barrier((tokens, facts))
-    near = [shift(sent[s], "seq", 1) for s in range(seqs)]
-    far = shift(sent[:, block - HALO_CHUNK :], "seq", 2) if far_rows > 0 else None
 
     def start_of(positions):
         found = jnp.zeros((seqs,) + positions.shape, jnp.int32)
@@ -1201,40 +1222,36 @@
     reach = jnp.max(firsts[None] - start_of(firsts)) - block
     chunks = jnp.maximum(reach + HALO_CHUNK - 1, 0) // HALO_CHUNK
 
-    shards = [attngain, attnshift, qvbias, outbias, mlpgain, mlpshift, fcbias, projbias]
-    packed = jnp.concatenate(shards).astype(F32)
-    table = jnp.where(
-        lax.broadcasted_iota(jnp.int32, (owners, packed.shape[0]), 0) == me,
-        packed[None],
-        0.0,
-    )
-    line = lax.broadcasted_iota(jnp.int32, (8, packed.shape[0]), 0)
-    table = jnp.concatenate(
-        [
-            table,
-            jnp.where(line == 0, facts[-1].astype(F32), jnp.where(line == 1, chunks.astype(F32), 0.0)),
-        ],
-        0,
-    )
-    is_reach = lax.broadcasted_iota(jnp.int32, table.shape, 0) == owners + 1
+    facts = jnp.stack([facts[-1], chunks])
     bit = 1
     while bit < owners:
-        other = swap(table, "fsdp", bit)
-        table = jnp.where(is_reach, jnp.maximum(table, other), table + other)
+        other = swap(facts, "fsdp", bit)
+        facts = jnp.where(jnp.arange(2) == 1, jnp.maximum(facts, other), facts + other)
         bit *= 2
+
+    packed = jnp.concatenate(
+        [jnp.pad(v[None], ((0, 0), (0, -v.shape[0] % 128))) for v in shards], 1
+    )
+    table = jnp.where(
+        lax.broadcasted_iota(jnp.int32, (owners, packed.shape[1]), 0) == me,
+        packed,
+        jnp.zeros((), BF16),
+    )
+    table = sum_over(table, "fsdp")
+
     qkv_pieces = gather_rest(qkv_pieces)
-    slab, qkv_pieces, table, near[0] = gather_slab(
-        outweight, fcweight, projweight, qkv_pieces, table, near[0]
-    )
-
-    count = table[owners, 0]
-    chunks = table[owners + 1, 0].astype(jnp.int32)
+    slab, qkv_pieces, table, facts, near[0] = gather_slab(
+        outweight, fcweight, projweight, qkv_pieces, table, facts, near[0]
+    )
+    count = facts[0].astype(F32)
+    chunks = facts[1]
+
     vectors = []
     at = 0
     for shard in shards:
         size = shard.shape[0]
-        vectors.append(table[:owners, at : at + size].reshape(1, size * owners))
-        at += size
+        vectors.append(table[:, at : at + size].reshape(1, size * owners).astype(F32))
+        at += size + -size % 128
     gain1, shift1, bias1, outbias_v, gain2, shift2, upbias, downbias = vectors
 
 
@@ -1250,6 +1267,7 @@
     normed, query, keyvalues, qkv = project_own(
         order, tokens, gain1, shift1, bias1, qkv_pieces, halo_rows + block
     )
+    near[-1], query = lax.optimization_barrier((near[-1], query))
     halo = jnp.stack(near)
     if far_rows > 0:
         blank = jnp.zeros((seqs, far_rows - HALO_CHUNK, width), BF16)
@@ -1295,7 +1313,7 @@
     staged = owners == SHARES and groups == 4
     if owners == SHARES:
         outer = lax.psum_scatter(outer, "fsdp", scatter_dimension=0, tiled=False)
-        outer = sum_seq_first(outer) if staged else sum_seq(outer)
+        outer = outer if staged else sum_seq(outer)
 
     gquery, gkeyvalues = attend_back(
         low, first, query, keyvalues, starts, mixed, gmixed.reshape(seqs, block, width), logs
@@ -1316,22 +1334,30 @@
         _, ghalo = lax.while_loop(lambda state: state[0] > 1, give, (chunks, ghalo))
 
     ghalo, gquery = lax.optimization_barrier((ghalo, gquery))
-    near = [shift(ghalo[s, far_rows:], "seq", -1) for s in range(seqs)]
+    near = [shift(ghalo[k, far_rows:], "seq", -1) for k in range(seqs)]
     far = []
     if far_rows > 0:
         far = [shift(ghalo[:, far_rows - HALO_CHUNK : far_rows], "seq", -2)]
-    gnormed, gweight, own_sums = own_back(
-        low_tile, tokens, normed, gquery, gkeyvalues, qkv
+    sort = order if owners == SHARES else jnp.arange(SHARES, dtype=jnp.int32)
+    gnormed, keep, give, own_sums = own_back(
+        low_tile, sort, tokens, normed, gquery, gkeyvalues, qkv
+    )
+    keep, give, own_sums, halo_sums, near[0] = lax.optimization_barrier(
+        (keep, give, own_sums, halo_sums, near[0])
     )
     late = jnp.concatenate(
-        [(own_sums[k] + halo_sums[k]).reshape(owners, -1) for k in range(2)]
-        + [own_sums[2:4].reshape(owners, -1)],
+        [(own_sums[k] + halo_sums[k]).reshape(SHARES, -1) for k in range(2)]
+        + [own_sums[2:4].reshape(SHARES, -1)],
         1,
     ).astype(BF16)
-    late = jnp.pad(late, ((0, 0), (0, 2 * width + width - late.shape[1])))
-    line = lax.broadcasted_iota(jnp.int32, (owners, 16, 3 * width), 1)
-    late = jnp.where(line == 0, late[:, None, :], jnp.zeros((), BF16))
-    gweight, near[0] = lax.optimization_barrier((gweight, near[0]))
+    late = jnp.pad(late, ((0, 0), (0, 3 * width - late.shape[1])))
+    slots = SHARES // 2
+    late = jnp.stack([lax.dynamic_index_in_dim(late, sort[k], 0) for k in range(SHARES)])
+    late = jnp.pad(late, ((0, 0), (0, SMALL_ROWS - 1), (0, 0)))
+    share = width // SHARES
+    keep = lax.dynamic_update_slice_in_dim(keep, late[:slots], share, 1)
+    give = lax.dynamic_update_slice_in_dim(give, late[slots:], share, 1)
+
     grad_tokens = finish(
         tokens,
         gnormed,
@@ -1341,12 +1367,15 @@
         gain1,
     )
 
-    joint, outer, grad_tokens = reduce_rows(
-        gweight.reshape(owners, width // owners, 3 * width), late, outer, grad_tokens
-    )
+    if owners == SHARES:
+        joint, outer, grad_tokens = reduce_rows(keep, give, outer, grad_tokens)
+    else:
+        joint = jnp.concatenate([keep, give])
+        small_late = lax.psum(joint[:, share].astype(F32), ("fsdp", "seq"))
+        joint = joint[:, :share].reshape(width, 3 * width)
+        joint = lax.psum_scatter(joint, "fsdp", scatter_dimension=0, tiled=True)
+        joint = lax.psum(joint, "seq")
     joint = joint.astype(F32)
-    if staged:
-        outer = sum_seq_rest(outer)
     grad_merge, grad_up, grad_down, small = reduce_slab(outer, width, hidden)
 
     share = width // owners
@@ -1368,14 +1397,27 @@
         ]
         loss_row = small[0, 1]
     loss = jnp.sum(loss_row) / (width * count)
+    share = width // owners
+    if owners == SHARES:
+        late = [joint[share, k * share : (k + 1) * share] for k in range(2)]
+        late.append(joint[share, 2 * share : 4 * share])
+    else:
+        late = []
+        for vector in (small_late[:, : width // SHARES], small_late[:, width // SHARES : 2 * width // SHARES], small_late[:, 2 * width // SHARES : 4 * width // SHARES]):
+            vector = vector.reshape(-1)
+            late.append(
+                lax.dynamic_slice_in_dim(
+                    vector, me * (vector.shape[0] // owners), vector.shape[0] // owners
+                )
+            )
     return (
         loss,
         layer_out.reshape(tokens.shape),
         grad_tokens,
-        joint[share, :share],
-        joint[share, share : 2 * share],
+        late[0],
+        late[1],
         joint[:share],
-        joint[share, 2 * share : 4 * share],
+        late[2],
         grad_merge,
         cuts[1],
         cuts[2],

time: 431 us -> 405 us (0.940)
  local copies, waits for them, and re-layouts: 42.3 us -> 30 us
  waiting for transfers between devices: 150 us -> 143 us
    ppermute x6, waiting for transfers between devices: 72 us -> 44.1 us  [shift(): lax.ppermute(x, axis, [(i, i + step) for i in range(size) if 0 <= i + ste...]
    reduce_scatter x1, waiting for transfers between devices: 0.02 us -> 15.9 us  [local(): outer = lax.psum_scatter(outer, 'fsdp', scatter_dimension=0, tiled=False)]
    unnamed x33 -> x58, local copies, waits for them, and re-layouts: 10 us -> 2.93 us
    concatenate x1, local copies, waits for them, and re-layouts: 5.45 us -> 0.01 us  [local(): jnp.concatenate([jnp.pad(v[None], ((0, 0), (0, -v.shape[0] % 128))) for v...]
    ppermute x22 -> x25, waiting for transfers between devices: 70.6 us -> 73.6 us  [swap(): return lax.ppermute(x, axis, [(i, i ^ bit) for i in range(size)])]
    ppermute x22 -> x25, starting transfers between devices: 29.4 us -> 26.4 us  [swap(): return lax.ppermute(x, axis, [(i, i ^ bit) for i in range(size)])]
  transfers between devices with their start and end apart: 30 -> 33, of which waited for: 15 -> 18; matrix products, arithmetic and copies ran while one was open for 12% -> 10% of each run, Pallas kernels for 21% -> 22%
where the time goes in v4:
time: 405 us; the launch traced here: 401 us
  Pallas kernels  146 us (36%)
  waiting for transfers between devices  143 us (35%)
  starting transfers between devices  42.6 us (11%)
  local copies, waits for them, and re-layouts  30 us (7%)
  other arithmetic  20.2 us (5%)
  between operations  18.5 us (5%)
    ppermute x25, waiting for transfers between devices, swap(): return lax.ppermute(x, axis, [(i, i ^ bit) for i in range(size)])  73.6 us
    pallas_call x1, Pallas kernels, mlp(): pl.pallas_call(mlp_kernel, grid=(rows // MLP_TILE,), in_specs=[pl.BlockSp...  55.7 us
    ppermute x6, waiting for transfers between devices, shift(): lax.ppermute(x, axis, [(i, i + step) for i in range(size) if 0 <= i + ste...  44.1 us
    pallas_call x1, Pallas kernels, attend_back(): pl.pallas_call(functools.partial(attend_back_kernel, length - block), gri...  27.2 us
    ppermute x25, starting transfers between devices, swap(): return lax.ppermute(x, axis, [(i, i ^ bit) for i in range(size)])  26.4 us
    pallas_call x1, Pallas kernels, attend(): pl.pallas_call(functools.partial(attend_kernel, length - block), grid_spe...  19.5 us
    pallas_call x1, Pallas kernels, own_back(): pl.pallas_call(own_back_kernel, grid_spec=pltpu.PrefetchScalarGridSpec(nu...  16.7 us
    ppermute x6, starting transfers between devices, shift(): lax.ppermute(x, axis, [(i, i + step) for i in range(size) if 0 <= i + ste...  16 us
  transfers between devices with their start and end apart: 33, of which 18 were waited for; matrix products, arithmetic and copies ran while one was open for 10% of the time, Pallas kernels for 22%

profile of v4, /device:TPU:0, one launch (start us, length us, event | category | flops | bytes accessed | tf_op | source)
XLA Modules:
  0.0 400.9 jit_solution(9668660414561797749)
XLA Ops:
  7.2 3.0 collective-permute-start.4
  34.2 2.9 collective-permute-start.17
  46.7 5.6 %collective-permute-done.17 = bf16[512,768]{1,0:T(8,128)(2,1)} collective-permute-done((bf16[512,768]{1,0:T(8,128)(2,1)S(1)}, bf16[512,768]{1,0:T(8,128)(2,1)}, u32[]{:S(2)}, u32[]{:S(2)}) %collective-permute-start.17) | collective-permute-done | bytes 786464 | tf_op jit(solution)/shard_map/ppermute | solution.py:1029
  54.2 4.9 %collective-permute-start.19 = (bf16[512,768]{1,0:T(8,128)(2,1)}, bf16[512,768]{1,0:T(8,128)(2,1)S(1)}, u32[]{:S(2)}, u32[]{:S(2)}) collective-permute-start(bf16[512,768]{1,0:T(8,128)(2,1)} %get-tuple-element.149), channel_id=1, source_target_pairs={{0,1},{1,2},{2,3},{4,5},{5,6},{6,7},{8,9},{9,10},{10,11},{12,13},{... | collective-permute-start | bytes 2359304 | tf_op jit(solution)/shard_map/ppermute | solution.py:1029
  59.1 4.4 %collective-permute-start.18 = (bf16[2,128,768]{2,1,0:T(8,128)(2,1)}, bf16[2,128,768]{2,1,0:T(8,128)(2,1)S(1)}, u32[]{:S(2)}, u32[]{:S(2)}) collective-permute-start(bf16[2,128,768]{2,1,0:T(8,128)(2,1)} %slice.211), channel_id=1, source_target_pairs={{0,2},{1,3},{4,6},{5,7},{8,10},{9,11},{12,14},{13,15},{16,18},{17,... | collective-permute-start | bytes 1179656 | tf_op jit(solution)/shard_map/ppermute | solution.py:1029
  67.7 10.4 %project_own.1 = (bf16[2,2048,768]{2,1,0:T(8,128)(2,1)}, bf16[2,512,768]{2,1,0:T(8,128)(2,1)}, bf16[2,2048,1536]{2,1,0:T(8,128)(2,1)}, bf16[768,2304]{1,0:T(8,128)(2,1)}) custom-call(s32[8]{0:T(128)} %stack.77.order_ref, bf16[2,512,768]{2,1,0:T(8,128)(2,1)} %own_ref.3, f32[1,768]{1,0:T(1,128)} %reshape.480.gain_ref, f32[1,768]{1,0:T(1,128)} %reshape.481.shift_ref, ...), custom_call_target="tpu_custom_call" | custom-call | flops 3623878656 | bytes 16777216 | tf_op jit(solution)/shard_map/project_own/pallas_call | solution.py:95
  82.9 3.5 maximum_maximum_fusion
  87.1 3.4 project_halo.1
  90.5 19.5 %attend.1 = (bf16[2,512,768]{2,1,0:T(8,128)(2,1)}, f32[2,6,2,512]{3,2,1,0:T(2,128)}) custom-call(s32[8]{0:T(128)} %reshape.470.low_ref, bf16[2,512,768]{2,1,0:T(8,128)(2,1)} %get-tuple-element.166.query_ref, bf16[2,2048,1536]{2,1,0:T(8,128)(2,1)} %get-tuple-element.167.keyvalue_ref, s32[2,1,512]{2,1,0:T(1,128)} %fusion.25.start_ref), custom_call_target="tpu_custom_call" | custom-call | flops 17179869184 | bytes 16777216 | tf_op jit(solution)/shard_map/attend/pallas_call | solution.py:332
  110.0 9.0 %all-gather.3.cloned.1.call-done = bf16[6912,768]{1,0:T(8,128)(2,1)} async-done(((bf16[864,768]{1,0:T(8,128)(2,1)}), bf16[6912,768]{1,0:T(8,128)(2,1)}) %all-gather.3.cloned.1.call-update) | async-done | bytes 10616848 | tf_op jit(solution)/shard_map/all_gather | solution.py:1128
  119.0 55.7 %mlp.1 = (bf16[1024,768]{1,0:T(8,128)(2,1)}, f32[1024,768]{1,0:T(8,128)}, bf16[1024,768]{1,0:T(8,128)(2,1)}, f32[8,768]{1,0:T(8,128)}, f32[8,3072]{1,0:T(8,128)}, /*index=5*/bf16[8,880,768]{2,1,0:T(8,128)(2,1)}) custom-call(f32[1]{0:T(128)S(6)} %div.44.factor_ref, bf16[1024,768]{1,0:T(8,128)(2,1)} %bitcast.117, bf16[1024,768]{1,0:T(8,128)(2,1)} %bitcast.97, ...), custom_call_target="tpu_custom_call" | custom-call | flops 32614907904 | bytes 41943040 | tf_op jit(solution)/shard_map/mlp/pallas_call | solution.py:671
  177.9 27.2 %attend_back.1 = (bf16[2,512,768]{2,1,0:T(8,128)(2,1)}, bf16[2,2048,1536]{2,1,0:T(8,128)(2,1)}) custom-call(s32[8]{0:T(128)} %reshape.470.low_ref, s32[2]{0:T(128)} %get-tuple-element.220.first_ref, bf16[2,512,768]{2,1,0:T(8,128)(2,1)} %get-tuple-element.166.query_ref, bf16[2,2048,1536]{2,1,0:T(8,128)(2,1)} %get-tuple-element.167.keyvalue_ref, ...), custom_call_target="tpu_custom_call" | custom-call | flops 42949672960 | bytes 29360128 | tf_op jit(solution)/shard_map/attend_back/pallas_call | solution.py:442
  205.1 5.2 %halo_back.1 = (bf16[2,1536,768]{2,1,0:T(8,128)(2,1)}, f32[8,768]{1,0:T(8,128)}) custom-call(s32[2]{0:T(128)} %get-tuple-element.221.low_ref, bf16[2,1536,768]{2,1,0:T(8,128)(2,1)} %get-tuple-element.161.halo_any, bf16[2,2048,1536]{2,1,0:T(8,128)(2,1)} %get-tuple-element.176.grad_any.gkeyvalue_any, bf16[768,2304]{1,0:T(8,128)(2,1)} %get-tuple-element.162.whole_any), custom_call_target="tpu_custom_call" | custom-call | flops 4294967296 | bytes 16777216 | tf_op jit(solution)/shard_map/halo_back/pallas_call | solution.py:800
  214.6 16.7 %own_back.1 = (f32[2,512,768]{2,1,0:T(8,128)}, bf16[4,112,2304]{2,1,0:T(8,128)(2,1)}, bf16[4,112,2304]{2,1,0:T(8,128)(2,1)}, f32[8,768]{1,0:T(8,128)}) custom-call(s32[2]{0:T(128)} %get-tuple-element.221.low_ref, s32[8]{0:T(128)} %stack.77.order_ref, bf16[2,512,768]{2,1,0:T(8,128)(2,1)} %own_ref.3, bf16[2,2048,768]{2,1,0:T(8,128)(2,1)} %get-tuple-element.165.normed_any, ...), custom_call_target="tpu_custom_call" | custom-call | flops 17179869184 | bytes 25165824 | tf_op jit(solution)/shard_map/own_back/pallas_call | solution.py:942
  231.3 19.7 %collective-permute-done.20.rest_0_ = bf16[512,768]{1,0:T(8,128)(2,1)S(1)} collective-permute-done((bf16[512,768]{1,0:T(8,128)(2,1)S(1)}, bf16[512,768]{1,0:T(8,128)(2,1)S(1)}, u32[]{:S(2)}, u32[]{:S(2)}) %collective-permute-start.20) | collective-permute-done | bytes 786464 | tf_op jit(solution)/shard_map/ppermute | solution.py:1029
  258.4 15.9 %reduce-scatter.2.cloned.1.call-done = bf16[1,880,768]{2,1,0:T(8,128)(2,1)} async-done(((bf16[8,880,768]{2,1,0:T(8,128)(2,1)}), bf16[1,880,768]{2,1,0:T(8,128)(2,1)}) %reduce-scatter.2.cloned.1.call-update) | async-done | bytes 1351696 | tf_op jit(solution)/shard_map/reduce_scatter | solution.py:1315
  282.5 18.6 %collective-permute-done.27.rest_2_ = bf16[2,128,768]{2,1,0:T(8,128)(2,1)S(1)} collective-permute-done((bf16[2,128,768]{2,1,0:T(8,128)(2,1)}, bf16[2,128,768]{2,1,0:T(8,128)(2,1)S(1)}, u32[]{:S(2)}, u32[]{:S(2)}) %collective-permute-start.27) | collective-permute-done | bytes 393248 | tf_op jit(solution)/shard_map/ppermute | solution.py:1029
  301.1 3.8 collective-permute-start.24
  305.8 7.5 %finish.1 = bf16[2,512,768]{2,1,0:T(8,128)(2,1)} custom-call(bf16[2,512,768]{2,1,0:T(8,128)(2,1)} %own_ref.3, f32[2,512,768]{2,1,0:T(8,128)} %get-tuple-element.191.gnormed_ref, f32[2,512,768]{2,1,0:T(8,128)} %bitcast.98, f32[1,768]{1,0:T(1,128)} %reshape.480.gain_ref, bf16[512,768]{1,0:T(8,128)(2,1)} %copy-done.2, bf16[512,768]{1,0:T(8,128)(2,1)} %copy-done.3, ...), custom_call_target="tpu_custom_call" | custom-call | flops 15728640 | bytes 11010048 | tf_op jit(solution)/shard_map/finish/pallas_call | solution.py:1004
  318.5 7.0 %collective-permute-done.30 = bf16[56,2304]{1,0:T(8,128)(2,1)S(1)} collective-permute-done((bf16[56,2304]{1,0:T(8,128)(2,1)S(1)}, bf16[56,2304]{1,0:T(8,128)(2,1)S(1)}, u32[]{:S(2)}, u32[]{:S(2)}) %collective-permute-start.30) | collective-permute-done | bytes 258080 | tf_op jit(solution)/shard_map/ppermute | solution.py:1024
  328.6 24.2 %collective-permute-done.31 = bf16[56,2304]{1,0:T(8,128)(2,1)S(1)} collective-permute-done((bf16[56,2304]{1,0:T(8,128)(2,1)S(1)}, bf16[56,2304]{1,0:T(8,128)(2,1)S(1)}, u32[]{:S(2)}, u32[]{:S(2)}) %collective-permute-start.31) | collective-permute-done | bytes 258080 | tf_op jit(solution)/shard_map/ppermute | solution.py:1024
  352.9 14.3 %collective-permute-done.28 = bf16[440,768]{1,0:T(8,128)(2,1)S(1)} collective-permute-done((bf16[440,768]{1,0:T(8,128)(2,1)S(1)}, bf16[440,768]{1,0:T(8,128)(2,1)S(1)}, u32[]{:S(2)}, u32[]{:S(2)}) %collective-permute-start.28) | collective-permute-done | bytes 675872 | tf_op jit(solution)/shard_map/ppermute | solution.py:1024
  367.5 5.2 %collective-permute-done.32 = bf16[56,2304]{1,0:T(8,128)(2,1)S(1)} collective-permute-done((bf16[56,2304]{1,0:T(8,128)(2,1)S(1)}, bf16[56,2304]{1,0:T(8,128)(2,1)S(1)}, u32[]{:S(2)}, u32[]{:S(2)}) %collective-permute-start.32) | collective-permute-done | bytes 258080 | tf_op jit(solution)/shard_map/ppermute | solution.py:1024
  375.0 12.1 %collective-permute-done.29 = bf16[440,768]{1,0:T(8,128)(2,1)S(1)} collective-permute-done((bf16[440,768]{1,0:T(8,128)(2,1)S(1)}, bf16[440,768]{1,0:T(8,128)(2,1)S(1)}, u32[]{:S(2)}, u32[]{:S(2)}) %collective-permute-start.29) | collective-permute-done | bytes 675872 | tf_op jit(solution)/shard_map/ppermute | solution.py:1024
  (207 shorter events, 82.7 us)
Async XLA Ops:
  7.2 111.8 %all-gather.3.cloned.1.call-start = ((), (), s32[]{:S(2)}) async-start(), calls=%async_computation.2 | async-start | bytes 11943936 | tf_op jit(solution)/shard_map/all_gather | solution.py:1128
  7.2 37.4 %collective-permute-start.4 = (bf16[96,2304]{1,0:T(8,128)(2,1)}, bf16[96,2304]{1,0:T(8,128)(2,1)}, u32[]{:S(2)}, u32[]{:S(2)}) collective-permute-start(bf16[96,2304]{1,0:T(8,128)(2,1)} %rest_0_), channel_id=1, source_target_pairs={{0,8},{4,12},{8,0},{12,4},{16,24},{20,28},{24,16},{28,20},{1,9},{5... | collective-permute-start | bytes 1327112 | tf_op jit(solution)/shard_map/ppermute | solution.py:1024
  10.2 34.9 %collective-permute-start.5 = (bf16[96,2304]{1,0:T(8,128)(2,1)}, bf16[96,2304]{1,0:T(8,128)(2,1)}, u32[]{:S(2)}, u32[]{:S(2)}) collective-permute-start(bf16[96,2304]{1,0:T(8,128)(2,1)} %rest_0_), channel_id=1, source_target_pairs={{0,16},{4,20},{8,24},{12,28},{16,0},{20,4},{24,8},{28,12},{1,17},{... | collective-permute-start | bytes 1327112 | tf_op jit(solution)/shard_map/ppermute | solution.py:1024
  11.8 33.4 %collective-permute-start.6 = (bf16[96,2304]{1,0:T(8,128)(2,1)}, bf16[96,2304]{1,0:T(8,128)(2,1)}, u32[]{:S(2)}, u32[]{:S(2)}) collective-permute-start(bf16[96,2304]{1,0:T(8,128)(2,1)} %rest_0_), channel_id=1, source_target_pairs={{0,24},{4,28},{8,16},{12,20},{16,8},{20,12},{24,0},{28,4},{1,25},{... | collective-permute-start | bytes 1327112 | tf_op jit(solution)/shard_map/ppermute | solution.py:1024
  24.3 7.9 %collective-permute-start.11 = (bf16[8,1408]{1,0:T(8,128)(2,1)S(1)}, bf16[8,1408]{1,0:T(8,128)(2,1)S(1)}, u32[]{:S(2)}, u32[]{:S(2)}) collective-permute-start(bf16[8,1408]{1,0:T(8,128)(2,1)S(1)} %broadcast_select_fusion), channel_id=1, source_target_pairs={{0,4},{4,0},{8,12},{12,8},{16,20},{20,16},{24,28},{28,24},{1,5},{5... | collective-permute-start | bytes 67592 | tf_op jit(solution)/shard_map/ppermute | solution.py:1024
  34.2 18.1 %collective-permute-start.17 = (bf16[512,768]{1,0:T(8,128)(2,1)S(1)}, bf16[512,768]{1,0:T(8,128)(2,1)}, u32[]{:S(2)}, u32[]{:S(2)}) collective-permute-start(bf16[512,768]{1,0:T(8,128)(2,1)S(1)} %get-tuple-element.145), channel_id=1, source_target_pairs={{0,1},{1,2},{2,3},{4,5},{5,6},{6,7},{8,9},{9,10},{10,11},{12,13},{... | collective-permute-start | bytes 2359304 | tf_op jit(solution)/shard_map/ppermute | solution.py:1029
  44.6 7.7 %collective-permute-start.8 = (bf16[96,2304]{1,0:T(8,128)(2,1)}, bf16[96,2304]{1,0:T(8,128)(2,1)}, u32[]{:S(2)}, u32[]{:S(2)}) collective-permute-start(bf16[96,2304]{1,0:T(8,128)(2,1)} %collective-permute-done.4.rest_1_), channel_id=1, source_target_pairs={{0,4},{4,0},{8,12},{12,8},{16,20},{20,16},{24,28},{28,24},{1,5},{5... | collective-permute-start | bytes 1327112 | tf_op jit(solution)/shard_map/ppermute | solution.py:1024
  45.1 7.2 %collective-permute-start.9 = (bf16[96,2304]{1,0:T(8,128)(2,1)}, bf16[96,2304]{1,0:T(8,128)(2,1)}, u32[]{:S(2)}, u32[]{:S(2)}) collective-permute-start(bf16[96,2304]{1,0:T(8,128)(2,1)} %collective-permute-done.5.rest_2_), channel_id=1, source_target_pairs={{0,4},{4,0},{8,12},{12,8},{16,20},{20,16},{24,28},{28,24},{1,5},{5... | collective-permute-start | bytes 1327112 | tf_op jit(solution)/shard_map/ppermute | solution.py:1024
  45.2 7.2 %collective-permute-start.10 = (bf16[96,2304]{1,0:T(8,128)(2,1)}, bf16[96,2304]{1,0:T(8,128)(2,1)}, u32[]{:S(2)}, u32[]{:S(2)}) collective-permute-start(bf16[96,2304]{1,0:T(8,128)(2,1)} %collective-permute-done.6.rest_3_), channel_id=1, source_target_pairs={{0,4},{4,0},{8,12},{12,8},{16,20},{20,16},{24,28},{28,24},{1,5},{5... | collective-permute-start | bytes 1327112 | tf_op jit(solution)/shard_map/ppermute | solution.py:1024
  52.4 221.9 %reduce-scatter.2.cloned.1.call-start = ((), (), s32[]{:S(2)}) async-start(), calls=%async_computation.1 | async-start | bytes 12165120 | tf_op jit(solution)/shard_map/reduce_scatter | solution.py:1315
  54.2 23.9 %collective-permute-start.19 = (bf16[512,768]{1,0:T(8,128)(2,1)}, bf16[512,768]{1,0:T(8,128)(2,1)S(1)}, u32[]{:S(2)}, u32[]{:S(2)}) collective-permute-start(bf16[512,768]{1,0:T(8,128)(2,1)} %get-tuple-element.149), channel_id=1, source_target_pairs={{0,1},{1,2},{2,3},{4,5},{5,6},{6,7},{8,9},{9,10},{10,11},{12,13},{... | collective-permute-start | bytes 2359304 | tf_op jit(solution)/shard_map/ppermute | solution.py:1029
  59.1 23.8 %collective-permute-start.18 = (bf16[2,128,768]{2,1,0:T(8,128)(2,1)}, bf16[2,128,768]{2,1,0:T(8,128)(2,1)S(1)}, u32[]{:S(2)}, u32[]{:S(2)}) collective-permute-start(bf16[2,128,768]{2,1,0:T(8,128)(2,1)} %slice.211), channel_id=1, source_target_pairs={{0,2},{1,3},{4,6},{5,7},{8,10},{9,11},{12,14},{13,15},{16,18},{17,... | collective-permute-start | bytes 1179656 | tf_op jit(solution)/shard_map/ppermute | solution.py:1029
  213.4 37.6 %collective-permute-start.20 = (bf16[512,768]{1,0:T(8,128)(2,1)S(1)}, bf16[512,768]{1,0:T(8,128)(2,1)S(1)}, u32[]{:S(2)}, u32[]{:S(2)}) collective-permute-start(bf16[512,768]{1,0:T(8,128)(2,1)S(1)} %get-tuple-element.223), channel_id=1, source_target_pairs={{1,0},{2,1},{3,2},{5,4},{6,5},{7,6},{9,8},{10,9},{11,10},{13,12},{... | collective-permute-start | bytes 2359304 | tf_op jit(solution)/shard_map/ppermute | solution.py:1029
  254.1 23.7 %collective-permute-start.21 = (bf16[4,112,2304]{2,1,0:T(8,128)(2,1)}, bf16[4,112,2304]{2,1,0:T(8,128)(2,1)S(1)}, u32[]{:S(2)}, u32[]{:S(2)}) collective-permute-start(bf16[4,112,2304]{2,1,0:T(8,128)(2,1)} %get-tuple-element.241), channel_id=1, source_target_pairs={{0,4},{4,0},{8,12},{12,8},{16,20},{20,16},{24,28},{28,24},{1,5},{5... | collective-permute-start | bytes 6193160 | tf_op jit(solution)/shard_map/ppermute | solution.py:1024
  255.9 49.0 %collective-permute-start.26 = (bf16[512,768]{1,0:T(8,128)(2,1)}, bf16[512,768]{1,0:T(8,128)(2,1)S(1)}, u32[]{:S(2)}, u32[]{:S(2)}) collective-permute-start(bf16[512,768]{1,0:T(8,128)(2,1)} %get-tuple-element.222), channel_id=1, source_target_pairs={{1,0},{2,1},{3,2},{5,4},{6,5},{7,6},{9,8},{10,9},{11,10},{13,12},{... | collective-permute-start | bytes 2359304 | tf_op jit(solution)/shard_map/ppermute | solution.py:1029
  257.1 43.9 %collective-permute-start.27 = (bf16[2,128,768]{2,1,0:T(8,128)(2,1)}, bf16[2,128,768]{2,1,0:T(8,128)(2,1)S(1)}, u32[]{:S(2)}, u32[]{:S(2)}) collective-permute-start(bf16[2,128,768]{2,1,0:T(8,128)(2,1)} %slice.256), channel_id=1, source_target_pairs={{2,0},{3,1},{6,4},{7,5},{10,8},{11,9},{14,12},{15,13},{18,16},{19,... | collective-permute-start | bytes 1179656 | tf_op jit(solution)/shard_map/ppermute | solution.py:1029
  276.3 37.0 %collective-permute-start.25 = (bf16[440,768]{1,0:T(8,128)(2,1)}, bf16[440,768]{1,0:T(8,128)(2,1)}, u32[]{:S(2)}, u32[]{:S(2)}) collective-permute-start(bf16[440,768]{1,0:T(8,128)(2,1)} %dynamic-slice_bitcast_fusion), channel_id=1, source_target_pairs={{0,1},{1,0},{2,3},{3,2},{4,5},{5,4},{6,7},{7,6},{8,9},{9,8},{10,11... | collective-permute-start | bytes 2027528 | tf_op jit(solution)/shard_map/ppermute | solution.py:1024
  280.5 34.1 %collective-permute-start.22 = (bf16[112,2304]{1,0:T(8,128)(2,1)}, bf16[112,2304]{1,0:T(8,128)(2,1)}, u32[]{:S(2)}, u32[]{:S(2)}) collective-permute-start(bf16[112,2304]{1,0:T(8,128)(2,1)} %get-tuple-element.226), channel_id=1, source_target_pairs={{0,8},{4,12},{8,0},{12,4},{16,24},{20,28},{24,16},{28,20},{1,9},{5... | collective-permute-start | bytes 1548296 | tf_op jit(solution)/shard_map/ppermute | solution.py:1024
  281.8 32.8 %collective-permute-start.23 = (bf16[112,2304]{1,0:T(8,128)(2,1)}, bf16[112,2304]{1,0:T(8,128)(2,1)}, u32[]{:S(2)}, u32[]{:S(2)}) collective-permute-start(bf16[112,2304]{1,0:T(8,128)(2,1)} %get-tuple-element.225), channel_id=1, source_target_pairs={{0,16},{4,20},{8,24},{12,28},{16,0},{20,4},{24,8},{28,12},{1,17},{... | collective-permute-start | bytes 1548296 | tf_op jit(solution)/shard_map/ppermute | solution.py:1024
  301.1 15.5 %collective-permute-start.24 = (bf16[112,2304]{1,0:T(8,128)(2,1)}, bf16[112,2304]{1,0:T(8,128)(2,1)}, u32[]{:S(2)}, u32[]{:S(2)}) collective-permute-start(bf16[112,2304]{1,0:T(8,128)(2,1)} %get-tuple-element.224), channel_id=1, source_target_pairs={{0,24},{4,28},{8,16},{12,20},{16,8},{20,12},{24,0},{28,4},{1,25},{... | collective-permute-start | bytes 1548296 | tf_op jit(solution)/shard_map/ppermute | solution.py:1024
  325.6 27.2 %collective-permute-start.31 = (bf16[56,2304]{1,0:T(8,128)(2,1)S(1)}, bf16[56,2304]{1,0:T(8,128)(2,1)S(1)}, u32[]{:S(2)}, u32[]{:S(2)}) collective-permute-start(bf16[56,2304]{1,0:T(8,128)(2,1)S(1)} %fusion.11), channel_id=1, source_target_pairs={{0,2},{1,3},{2,0},{3,1},{4,6},{5,7},{6,4},{7,5},{8,10},{9,11},{10,... | collective-permute-start | bytes 774152 | tf_op jit(solution)/shard_map/ppermute | solution.py:1024
  325.7 41.6 %collective-permute-start.28 = (bf16[440,768]{1,0:T(8,128)(2,1)S(1)}, bf16[440,768]{1,0:T(8,128)(2,1)S(1)}, u32[]{:S(2)}, u32[]{:S(2)}) collective-permute-start(bf16[440,768]{1,0:T(8,128)(2,1)S(1)} %fusion.2), channel_id=1, source_target_pairs={{0,2},{1,3},{2,0},{3,1},{4,6},{5,7},{6,4},{7,5},{8,10},{9,11},{10,... | collective-permute-start | bytes 2027528 | tf_op jit(solution)/shard_map/ppermute | solution.py:1024
  352.8 19.9 %collective-permute-start.32 = (bf16[56,2304]{1,0:T(8,128)(2,1)S(1)}, bf16[56,2304]{1,0:T(8,128)(2,1)S(1)}, u32[]{:S(2)}, u32[]{:S(2)}) collective-permute-start(bf16[56,2304]{1,0:T(8,128)(2,1)S(1)} %add_convert_fusion.6), channel_id=1, source_target_pairs={{0,1},{1,0},{2,3},{3,2},{4,5},{5,4},{6,7},{7,6},{8,9},{9,8},{10,11... | collective-permute-start | bytes 774152 | tf_op jit(solution)/shard_map/ppermute | solution.py:1024
  367.4 19.7 %collective-permute-start.29 = (bf16[440,768]{1,0:T(8,128)(2,1)S(1)}, bf16[440,768]{1,0:T(8,128)(2,1)S(1)}, u32[]{:S(2)}, u32[]{:S(2)}) collective-permute-start(bf16[440,768]{1,0:T(8,128)(2,1)S(1)} %add_convert_fusion.1), channel_id=1, source_target_pairs={{0,1},{1,0},{2,3},{3,2},{4,5},{5,4},{6,7},{7,6},{8,9},{9,8},{10,11... | collective-permute-start | bytes 2027528 | tf_op jit(solution)/shard_map/ppermute | solution.py:1024
  (27 other events, 225.5 us)
Sparse Core Ops, SparseCore 0:
  52.5 66.4 all-gather.2
  178.0 96.2 reduce-scatter.1

commit v5 on v4

--- a/solution.py
+++ b/solution.py
@@ -657,7 +657,7 @@
         block_copy(chunks - 1).wait()
 
 
-def mlp(factor, mixed, tokens, teacher, weight, vectors, slab, extra):
+def mlp(factor, mixed, tokens, teacher, weight, vectors, slab):
     rows, width = tokens.shape
     outbias, gain, shift, upbias, downbias = vectors
     hidden = upbias.shape[1]
@@ -698,7 +698,7 @@
             shape((rows, width), BF16),
             shape((8, width), F32),
             shape((8, hidden), F32),
-            shape((owners, (1 + 2 * chunks) * few + extra, width), BF16),
+            shape((owners, (1 + 2 * chunks) * few, width), BF16),
         ],
         scratch_shapes=[
             pltpu.VMEM((width, width), BF16),
@@ -978,45 +978,44 @@
     )(low, order, own, normed, gquery, gkeyvalues, whole)
 
 
-def finish_kernel(seqs, own_ref, gnormed_ref, gresid_ref, gain_ref, *rest):
-    near_refs, far_refs = rest[:seqs], rest[seqs:-2]
-    out_ref, total_ref = rest[-2:]
-    unit, scale = norm_parts(own_ref[0].astype(F32))
-    for seq, near_ref in enumerate(near_refs):
-
-        @pl.when(pl.program_id(0) == seq)
-        def _():
-            total_ref[...] = gnormed_ref[0] + near_ref[...].astype(F32)
-
-    for far_ref in far_refs:
-
-        @pl.when(pl.program_id(1) == pl.num_programs(1) - 1)
-        def _():
-            total_ref[-HALO_CHUNK:, :] += far_ref[0].astype(F32)
-
-    out_ref[0] = (gresid_ref[0] + norm_back(total_ref[...], gain_ref[...], unit, scale)).astype(BF16)
-
-
-def finish(own, gnormed, near, far, gresid, gain):
+def finish_kernel(own_ref, gnormed_ref, gresid_ref, gain_ref, *rest):
+    more_refs, (out_ref, total_ref) = rest[:-2], rest[-2:]
+    start = 0
+    for more_ref in more_refs:
+        end = start + more_ref.shape[1]
+        total_ref[start:end, :] = gnormed_ref[0, start:end, :] + more_ref[0].astype(F32)
+        start = end
+
+    def one(t, nothing):
+        at = pl.ds(pl.multiple_of(t * HALO_CHUNK, HALO_CHUNK), HALO_CHUNK)
+        unit, scale = norm_parts(own_ref[0, at, :].astype(F32))
+        out_ref[0, at, :] = (
+            gresid_ref[0, at, :] + norm_back(total_ref[at, :], gain_ref[...], unit, scale)
+        ).astype(BF16)
+        return nothing
+
+    lax.fori_loop(0, own_ref.shape[1] // HALO_CHUNK, one, 0)
+
+
+def finish(own, gnormed, more, gresid, gain):
     seqs, block, width = own.shape
-    tile = pl.BlockSpec((1, ROW_TILE, width), lambda s, t: (s, t, 0))
-    last = pl.BlockSpec((1, HALO_CHUNK, width), lambda s, t: (s, 0, 0))
+    whole = lambda rows: pl.BlockSpec((1, rows, width), lambda s: (s, 0, 0))
+    tile = whole(block)
     return pl.pallas_call(
-        functools.partial(finish_kernel, seqs),
-        grid=(seqs, block // ROW_TILE),
-        in_specs=[tile, tile, tile, pl.BlockSpec((1, width), lambda s, t: (0, 0))]
-        + [pl.BlockSpec((ROW_TILE, width), lambda s, t: (t, 0))] * seqs
-        + [last] * len(far),
+        finish_kernel,
+        grid=(seqs,),
+        in_specs=[tile, tile, tile, pl.BlockSpec((1, width), lambda s: (0, 0))]
+        + [whole(part.shape[1]) for part in more],
         out_specs=tile,
         out_shape=jax.ShapeDtypeStruct(own.shape, BF16),
-        scratch_shapes=[pltpu.VMEM((ROW_TILE, width), F32)],
+        scratch_shapes=[pltpu.VMEM((block, width), F32)],
         cost_estimate=pl.CostEstimate(
             flops=20 * seqs * block * width,
             bytes_accessed=14 * seqs * block * width,
             transcendentals=0,
         ),
         name="finish",
-    )(own, gnormed, gresid, gain, *near, *far)
+    )(own, gnormed, gresid, gain, *more)
 
 
 def swap(x, axis, bit):
@@ -1106,12 +1105,15 @@
     ]
     arrived = [swap(part, "fsdp", 2 * d) for d, part in enumerate(mine) if d > 0]
     arrived, half, *first = lax.optimization_barrier((arrived, half, *first))
-    if staged:
-        half = sum_seq_rest(sum_seq_second(half))
     total = mine[0].astype(F32)
     for part in arrived:
         total = total + part.astype(F32)
-    return sum_seq(total.astype(BF16)), half, *first
+    total = total.astype(BF16)
+    if not staged:
+        return lax.psum(total, "seq"), half, *first
+    total, half = sum_seq_first(total), sum_seq_second(half)
+    total, half = lax.optimization_barrier((total, half))
+    return sum_seq_rest(sum_seq_second(total)), sum_seq_rest(half), *first
 
 
 def gather_slab(outweight, fcweight, projweight, *first):
@@ -1140,23 +1142,19 @@
     def part(array, axis):
         at = lambda a, b: lax.slice_in_dim(array, a * rows, b * rows, axis=axis)
         ups = [at(1 + c, 2 + c) for c in range(cuts)]
-        rest = lax.slice_in_dim(array, (1 + 2 * cuts) * rows, array.shape[axis], axis=axis)
-        return at(0, 1), jnp.concatenate(ups, -1), at(1 + cuts, 1 + 2 * cuts), rest
+        return at(0, 1), jnp.concatenate(ups, -1), at(1 + cuts, 1 + 2 * cuts)
 
     if owners == SHARES:
         return part(slab.astype(F32), 0)
-    *grads, rest = part(slab, 1)
-    grads = [
+    return [
         lax.psum(
             lax.psum_scatter(
                 g.reshape(-1, g.shape[-1]), "fsdp", scatter_dimension=0, tiled=True
             ),
             "seq",
         ).astype(F32)
-        for g in grads
+        for g in part(slab, 1)
     ]
-    rest = lax.psum(rest.astype(F32), ("fsdp", "seq"))
-    return *grads, rest
 
 
 def local(
@@ -1298,16 +1296,10 @@
         weight.reshape(rows, 1),
         (outbias_v, gain2, shift2, upbias, downbias),
         slab,
-        SMALL_ROWS,
     )
 
     small = jnp.concatenate(
         [upsums[0].reshape(SHARES, -1)] + [sums[k].reshape(SHARES, -1) for k in range(4)], 1
-    )
-    line = lax.broadcasted_iota(jnp.int32, (SHARES, SMALL_ROWS, width), 1)
-    small = jnp.where(line == 0, small[:, None, :], jnp.where(line == 1, sums[4], 0.0))
-    outer = lax.dynamic_update_slice_in_dim(
-        outer, small.astype(BF16), outer.shape[1] - SMALL_ROWS, 1
     )
     outer, gmixed = lax.optimization_barrier((outer, gmixed))
     staged = owners == SHARES and groups == 4
@@ -1334,23 +1326,29 @@
         _, ghalo = lax.while_loop(lambda state: state[0] > 1, give, (chunks, ghalo))
 
     ghalo, gquery = lax.optimization_barrier((ghalo, gquery))
-    near = [shift(ghalo[k, far_rows:], "seq", -1) for k in range(seqs)]
-    far = []
-    if far_rows > 0:
-        far = [shift(ghalo[:, far_rows - HALO_CHUNK : far_rows], "seq", -2)]
+    ends = far_rows + block - HALO_CHUNK
+    cut = far_rows + (block - HALO_CHUNK) // 2
+    closing = ghalo[:, ends:]
+    came = shift(ghalo[:, far_rows - HALO_CHUNK : far_rows], "seq", -1) if far_rows > 0 else closing
+    near = [shift(ghalo[:, far_rows:cut], "seq", -1), shift(ghalo[:, cut:ends], "seq", -1)]
     sort = order if owners == SHARES else jnp.arange(SHARES, dtype=jnp.int32)
     gnormed, keep, give, own_sums = own_back(
         low_tile, sort, tokens, normed, gquery, gkeyvalues, qkv
     )
-    keep, give, own_sums, halo_sums, near[0] = lax.optimization_barrier(
-        (keep, give, own_sums, halo_sums, near[0])
-    )
+    keep, give, own_sums, halo_sums, near[0], came = lax.optimization_barrier(
+        (keep, give, own_sums, halo_sums, near[0], came)
+    )
+    if far_rows > 0:
+        closing = (closing.astype(F32) + came.astype(F32)).astype(BF16)
+    near.append(shift(closing, "seq", -1))
     late = jnp.concatenate(
         [(own_sums[k] + halo_sums[k]).reshape(SHARES, -1) for k in range(2)]
         + [own_sums[2:4].reshape(SHARES, -1)],
         1,
     ).astype(BF16)
-    late = jnp.pad(late, ((0, 0), (0, 3 * width - late.shape[1])))
+    late = jnp.pad(late, ((0, 0), (0, width - late.shape[1])))
+    loss_row = jnp.broadcast_to(sums[4:5].astype(BF16), (SHARES, width))
+    late = jnp.concatenate([late, small.astype(BF16), loss_row], 1)
     slots = SHARES // 2
     late = jnp.stack([lax.dynamic_index_in_dim(late, sort[k], 0) for k in range(SHARES)])
     late = jnp.pad(late, ((0, 0), (0, SMALL_ROWS - 1), (0, 0)))
@@ -1362,7 +1360,6 @@
         tokens,
         gnormed,
         near,
-        far,
         gresid.reshape(tokens.shape),
         gain1,
     )
@@ -1376,56 +1373,40 @@
         joint = lax.psum_scatter(joint, "fsdp", scatter_dimension=0, tiled=True)
         joint = lax.psum(joint, "seq")
     joint = joint.astype(F32)
-    grad_merge, grad_up, grad_down, small = reduce_slab(outer, width, hidden)
+    grad_merge, grad_up, grad_down = reduce_slab(outer, width, hidden)
 
     share = width // owners
+    at = hidden // SHARES
+    wide = width // SHARES
+    spots = [(0, wide), (wide, wide), (2 * wide, 2 * wide), (width, at)]
+    spots += [(width + at + k * wide, wide) for k in range(4)]
     if owners == SHARES:
-        at = hidden // owners
-        cuts = [small[0, :at]] + [
-            small[0, at + k * share : at + (k + 1) * share] for k in range(4)
-        ]
-        loss_row = small[1]
+        cuts = [joint[share, start : start + size] for start, size in spots]
+        loss_row = joint[share, 2 * width :]
     else:
-        at = hidden // SHARES
-        wide = width // SHARES
-        full = [small[:, 0, :at].reshape(-1)] + [
-            small[:, 0, at + k * wide : at + (k + 1) * wide].reshape(-1) for k in range(4)
-        ]
+        full = [small_late[:, start : start + size].reshape(-1) for start, size in spots]
         cuts = [
             lax.dynamic_slice_in_dim(v, me * (v.shape[0] // owners), v.shape[0] // owners)
             for v in full
         ]
-        loss_row = small[0, 1]
+        loss_row = small_late[0, 2 * width :]
     loss = jnp.sum(loss_row) / (width * count)
-    share = width // owners
-    if owners == SHARES:
-        late = [joint[share, k * share : (k + 1) * share] for k in range(2)]
-        late.append(joint[share, 2 * share : 4 * share])
-    else:
-        late = []
-        for vector in (small_late[:, : width // SHARES], small_late[:, width // SHARES : 2 * width // SHARES], small_late[:, 2 * width // SHARES : 4 * width // SHARES]):
-            vector = vector.reshape(-1)
-            late.append(
-                lax.dynamic_slice_in_dim(
-                    vector, me * (vector.shape[0] // owners), vector.shape[0] // owners
-                )
-            )
     return (
         loss,
         layer_out.reshape(tokens.shape),
         grad_tokens,
-        late[0],
-        late[1],
+        cuts[0],
+        cuts[1],
         joint[:share],
-        late[2],
+        cuts[2],
         grad_merge,
-        cuts[1],
-        cuts[2],
+        cuts[4],
+        cuts[5],
+        cuts[6],
+        grad_up,
         cuts[3],
-        grad_up,
-        cuts[0],
         grad_down,
-        cuts[4],
+        cuts[7],
     )
 
 

time: 405 us -> 385 us (0.951)
  waiting for transfers between devices: 143 us -> 118 us
  starting transfers between devices: 42.6 us -> 48.3 us
    ppermute x6 -> x7, waiting for transfers between devices: 44.1 us -> 32.2 us  [shift(): lax.ppermute(x, axis, [(i, i + step) for i in range(size) if 0 <= i + ste...]
    reduce_scatter x1, waiting for transfers between devices: 15.9 us -> 7.9 us  [local(): outer = lax.psum_scatter(outer, 'fsdp', scatter_dimension=0, tiled=False)]
    ppermute x25, waiting for transfers between devices: 73.6 us -> 69.3 us  [swap(): return lax.ppermute(x, axis, [(i, i ^ bit) for i in range(size)])]
    ppermute x25, starting transfers between devices: 26.4 us -> 30.6 us  [swap(): return lax.ppermute(x, axis, [(i, i ^ bit) for i in range(size)])]
    ppermute x6 -> x7, starting transfers between devices: 16 us -> 17.6 us  [shift(): lax.ppermute(x, axis, [(i, i + step) for i in range(size) if 0 <= i + ste...]
  transfers between devices with their start and end apart: 33 -> 34, of which waited for: 18 -> 19; matrix products, arithmetic and copies ran while one was open for 10% -> 11% of each run, Pallas kernels for 22% -> 23%
where the time goes in v5:
time: 385 us; the launch traced here: 379 us
  Pallas kernels  144 us (37%)
  waiting for transfers between devices  118 us (31%)
  starting transfers between devices  48.3 us (13%)
  local copies, waits for them, and re-layouts  26.9 us (7%)
  other arithmetic  21.3 us (6%)
  between operations  18.5 us (5%)
    ppermute x25, waiting for transfers between devices, swap(): return lax.ppermute(x, axis, [(i, i ^ bit) for i in range(size)])  69.3 us
    pallas_call x1, Pallas kernels, mlp(): pl.pallas_call(mlp_kernel, grid=(rows // MLP_TILE,), in_specs=[pl.BlockSp...  55.7 us
    ppermute x7, waiting for transfers between devices, shift(): lax.ppermute(x, axis, [(i, i + step) for i in range(size) if 0 <= i + ste...  32.2 us
    ppermute x25, starting transfers between devices, swap(): return lax.ppermute(x, axis, [(i, i ^ bit) for i in range(size)])  30.6 us
    pallas_call x1, Pallas kernels, attend_back(): pl.pallas_call(functools.partial(attend_back_kernel, length - block), gri...  27.2 us
    pallas_call x1, Pallas kernels, attend(): pl.pallas_call(functools.partial(attend_kernel, length - block), grid_spe...  19.5 us
    ppermute x7, starting transfers between devices, shift(): lax.ppermute(x, axis, [(i, i + step) for i in range(size) if 0 <= i + ste...  17.6 us
    pallas_call x1, Pallas kernels, own_back(): pl.pallas_call(own_back_kernel, grid_spec=pltpu.PrefetchScalarGridSpec(nu...  16.1 us
  transfers between devices with their start and end apart: 34, of which 19 were waited for; matrix products, arithmetic and copies ran while one was open for 11% of the time, Pallas kernels for 23%

profile of v5, /device:TPU:0, one launch (start us, length us, event | category | flops | bytes accessed | tf_op | source)
XLA Modules:
  0.0 378.6 jit_solution(18063172671599621926)
XLA Ops:
  46.7 5.6 %collective-permute-done.17 = bf16[512,768]{1,0:T(8,128)(2,1)} collective-permute-done((bf16[512,768]{1,0:T(8,128)(2,1)S(1)}, bf16[512,768]{1,0:T(8,128)(2,1)}, u32[]{:S(2)}, u32[]{:S(2)}) %collective-permute-start.17) | collective-permute-done | bytes 786464 | tf_op jit(solution)/shard_map/ppermute | solution.py:1028
  54.2 4.9 %collective-permute-start.19 = (bf16[512,768]{1,0:T(8,128)(2,1)}, bf16[512,768]{1,0:T(8,128)(2,1)S(1)}, u32[]{:S(2)}, u32[]{:S(2)}) collective-permute-start(bf16[512,768]{1,0:T(8,128)(2,1)} %get-tuple-element.152), channel_id=1, source_target_pairs={{0,1},{1,2},{2,3},{4,5},{5,6},{6,7},{8,9},{9,10},{10,11},{12,13},{... | collective-permute-start | bytes 2359304 | tf_op jit(solution)/shard_map/ppermute | solution.py:1028
  59.1 4.4 %collective-permute-start.18 = (bf16[2,128,768]{2,1,0:T(8,128)(2,1)}, bf16[2,128,768]{2,1,0:T(8,128)(2,1)S(1)}, u32[]{:S(2)}, u32[]{:S(2)}) collective-permute-start(bf16[2,128,768]{2,1,0:T(8,128)(2,1)} %slice.213), channel_id=1, source_target_pairs={{0,2},{1,3},{4,6},{5,7},{8,10},{9,11},{12,14},{13,15},{16,18},{17,... | collective-permute-start | bytes 1179656 | tf_op jit(solution)/shard_map/ppermute | solution.py:1028
  67.7 10.4 %project_own.1 = (bf16[2,2048,768]{2,1,0:T(8,128)(2,1)}, bf16[2,512,768]{2,1,0:T(8,128)(2,1)}, bf16[2,2048,1536]{2,1,0:T(8,128)(2,1)}, bf16[768,2304]{1,0:T(8,128)(2,1)}) custom-call(s32[8]{0:T(128)} %stack.77.order_ref, bf16[2,512,768]{2,1,0:T(8,128)(2,1)} %own_ref.3, f32[1,768]{1,0:T(1,128)} %reshape.479.gain_ref, f32[1,768]{1,0:T(1,128)} %reshape.480.shift_ref, ...), custom_call_target="tpu_custom_call" | custom-call | flops 3623878656 | bytes 16777216 | tf_op jit(solution)/shard_map/project_own/pallas_call | solution.py:95
  82.9 3.5 maximum_maximum_fusion
  87.0 3.4 project_halo.1
  90.4 19.5 %attend.1 = (bf16[2,512,768]{2,1,0:T(8,128)(2,1)}, f32[2,6,2,512]{3,2,1,0:T(2,128)}) custom-call(s32[8]{0:T(128)} %reshape.469.low_ref, bf16[2,512,768]{2,1,0:T(8,128)(2,1)} %get-tuple-element.169.query_ref, bf16[2,2048,1536]{2,1,0:T(8,128)(2,1)} %get-tuple-element.170.keyvalue_ref, s32[2,1,512]{2,1,0:T(1,128)} %fusion.25.start_ref), custom_call_target="tpu_custom_call" | custom-call | flops 17179869184 | bytes 16777216 | tf_op jit(solution)/shard_map/attend/pallas_call | solution.py:332
  109.9 9.1 %all-gather.3.cloned.1.call-done = bf16[6912,768]{1,0:T(8,128)(2,1)} async-done(((bf16[864,768]{1,0:T(8,128)(2,1)}), bf16[6912,768]{1,0:T(8,128)(2,1)}) %all-gather.3.cloned.1.call-update) | async-done | bytes 10616848 | tf_op jit(solution)/shard_map/all_gather | solution.py:1130
  119.0 55.7 %mlp.1 = (bf16[1024,768]{1,0:T(8,128)(2,1)}, f32[1024,768]{1,0:T(8,128)}, bf16[1024,768]{1,0:T(8,128)(2,1)}, f32[8,768]{1,0:T(8,128)}, f32[8,3072]{1,0:T(8,128)}, /*index=5*/bf16[8,864,768]{2,1,0:T(8,128)(2,1)}) custom-call(f32[1]{0:T(128)S(6)} %div.44.factor_ref, bf16[1024,768]{1,0:T(8,128)(2,1)} %bitcast.113, bf16[1024,768]{1,0:T(8,128)(2,1)} %bitcast.93, ...), custom_call_target="tpu_custom_call" | custom-call | flops 32614907904 | bytes 41943040 | tf_op jit(solution)/shard_map/mlp/pallas_call | solution.py:671
  174.7 27.2 %attend_back.1 = (bf16[2,512,768]{2,1,0:T(8,128)(2,1)}, bf16[2,2048,1536]{2,1,0:T(8,128)(2,1)}) custom-call(s32[8]{0:T(128)} %reshape.469.low_ref, s32[2]{0:T(128)} %get-tuple-element.226.first_ref, bf16[2,512,768]{2,1,0:T(8,128)(2,1)} %get-tuple-element.169.query_ref, bf16[2,2048,1536]{2,1,0:T(8,128)(2,1)} %get-tuple-element.170.keyvalue_ref, ...), custom_call_target="tpu_custom_call" | custom-call | flops 42949672960 | bytes 29360128 | tf_op jit(solution)/shard_map/attend_back/pallas_call | solution.py:442
  201.9 5.1 %halo_back.1 = (bf16[2,1536,768]{2,1,0:T(8,128)(2,1)}, f32[8,768]{1,0:T(8,128)}) custom-call(s32[2]{0:T(128)} %get-tuple-element.227.low_ref, bf16[2,1536,768]{2,1,0:T(8,128)(2,1)} %get-tuple-element.164.halo_any, bf16[2,2048,1536]{2,1,0:T(8,128)(2,1)} %get-tuple-element.177.grad_any.gkeyvalue_any, bf16[768,2304]{1,0:T(8,128)(2,1)} %get-tuple-element.165.whole_any), custom_call_target="tpu_custom_call" | custom-call | flops 4294967296 | bytes 16777216 | tf_op jit(solution)/shard_map/halo_back/pallas_call | solution.py:800
  213.4 16.1 %own_back.1 = (f32[2,512,768]{2,1,0:T(8,128)}, bf16[4,112,2304]{2,1,0:T(8,128)(2,1)}, bf16[4,112,2304]{2,1,0:T(8,128)(2,1)}, f32[8,768]{1,0:T(8,128)}) custom-call(s32[2]{0:T(128)} %get-tuple-element.227.low_ref, s32[8]{0:T(128)} %stack.77.order_ref, bf16[2,512,768]{2,1,0:T(8,128)(2,1)} %own_ref.3, bf16[2,2048,768]{2,1,0:T(8,128)(2,1)} %get-tuple-element.168.normed_any, ...), custom_call_target="tpu_custom_call" | custom-call | flops 17179869184 | bytes 25165824 | tf_op jit(solution)/shard_map/own_back/pallas_call | solution.py:942
  230.9 22.4 %collective-permute-done.21 = bf16[2,128,768]{2,1,0:T(8,128)(2,1)} collective-permute-done((bf16[2,128,768]{2,1,0:T(8,128)(2,1)S(1)}, bf16[2,128,768]{2,1,0:T(8,128)(2,1)}, u32[]{:S(2)}, u32[]{:S(2)}) %collective-permute-start.21) | collective-permute-done | bytes 393248 | tf_op jit(solution)/shard_map/ppermute | solution.py:1028
  261.3 7.9 %reduce-scatter.2.cloned.1.call-done = bf16[1,864,768]{2,1,0:T(8,128)(2,1)} async-done(((bf16[8,864,768]{2,1,0:T(8,128)(2,1)}), bf16[1,864,768]{2,1,0:T(8,128)(2,1)}) %reduce-scatter.2.cloned.1.call-update) | async-done | bytes 1327120 | tf_op jit(solution)/shard_map/reduce_scatter | solution.py:1307
  278.9 4.1 %collective-permute-done.28.rest_2_ = bf16[2,128,768]{2,1,0:T(8,128)(2,1)} collective-permute-done((bf16[2,128,768]{2,1,0:T(8,128)(2,1)}, bf16[2,128,768]{2,1,0:T(8,128)(2,1)}, u32[]{:S(2)}, u32[]{:S(2)}) %collective-permute-start.28) | collective-permute-done | bytes 393248 | tf_op jit(solution)/shard_map/ppermute | solution.py:1028
  283.0 6.6 %finish.1 = bf16[2,512,768]{2,1,0:T(8,128)(2,1)} custom-call(bf16[2,512,768]{2,1,0:T(8,128)(2,1)} %own_ref.3, f32[2,512,768]{2,1,0:T(8,128)} %get-tuple-element.194.gnormed_ref, f32[2,512,768]{2,1,0:T(8,128)} %bitcast.94, f32[1,768]{1,0:T(1,128)} %reshape.479.gain_ref, bf16[2,192,768]{2,1,0:T(8,128)(2,1)} %copy-done.2, bf16[2,192,768]{2,1,0:T(8,128)(2,1)} %copy-done.3, ...), custom_call_target="tpu_custom_call" | custom-call | flops 15728640 | bytes 11010048 | tf_op jit(solution)/shard_map/finish/pallas_call | solution.py:1004
  289.5 7.3 %collective-permute-done.26 = bf16[432,768]{1,0:T(8,128)(2,1)} collective-permute-done((bf16[432,768]{1,0:T(8,128)(2,1)}, bf16[432,768]{1,0:T(8,128)(2,1)}, u32[]{:S(2)}, u32[]{:S(2)}) %collective-permute-start.26) | collective-permute-done | bytes 663584 | tf_op jit(solution)/shard_map/ppermute | solution.py:1023
  303.4 4.3 %collective-permute-start.30 = (bf16[432,768]{1,0:T(8,128)(2,1)S(1)}, bf16[432,768]{1,0:T(8,128)(2,1)S(1)}, u32[]{:S(2)}, u32[]{:S(2)}) collective-permute-start(bf16[432,768]{1,0:T(8,128)(2,1)S(1)} %fusion.2), channel_id=1, source_target_pairs={{0,2},{1,3},{2,0},{3,1},{4,6},{5,7},{6,4},{7,5},{8,10},{9,11},{10,... | collective-permute-start | bytes 1990664 | tf_op jit(solution)/shard_map/ppermute | solution.py:1023
  307.7 7.6 %collective-permute-done.29 = bf16[56,2304]{1,0:T(8,128)(2,1)S(1)} collective-permute-done((bf16[56,2304]{1,0:T(8,128)(2,1)S(1)}, bf16[56,2304]{1,0:T(8,128)(2,1)S(1)}, u32[]{:S(2)}, u32[]{:S(2)}) %collective-permute-start.29) | collective-permute-done | bytes 258080 | tf_op jit(solution)/shard_map/ppermute | solution.py:1023
  315.4 20.7 %collective-permute-done.30 = bf16[432,768]{1,0:T(8,128)(2,1)S(1)} collective-permute-done((bf16[432,768]{1,0:T(8,128)(2,1)S(1)}, bf16[432,768]{1,0:T(8,128)(2,1)S(1)}, u32[]{:S(2)}, u32[]{:S(2)}) %collective-permute-start.30) | collective-permute-done | bytes 663584 | tf_op jit(solution)/shard_map/ppermute | solution.py:1023
  336.4 10.2 %collective-permute-done.31 = bf16[56,2304]{1,0:T(8,128)(2,1)S(1)} collective-permute-done((bf16[56,2304]{1,0:T(8,128)(2,1)S(1)}, bf16[56,2304]{1,0:T(8,128)(2,1)S(1)}, u32[]{:S(2)}, u32[]{:S(2)}) %collective-permute-start.31) | collective-permute-done | bytes 258080 | tf_op jit(solution)/shard_map/ppermute | solution.py:1023
  346.7 4.6 %collective-permute-start.32 = (bf16[56,2304]{1,0:T(8,128)(2,1)S(1)}, bf16[56,2304]{1,0:T(8,128)(2,1)S(1)}, u32[]{:S(2)}, u32[]{:S(2)}) collective-permute-start(bf16[56,2304]{1,0:T(8,128)(2,1)S(1)} %add_convert_fusion.7), channel_id=1, source_target_pairs={{0,1},{1,0},{2,3},{3,2},{4,5},{5,4},{6,7},{7,6},{8,9},{9,8},{10,11... | collective-permute-start | bytes 774152 | tf_op jit(solution)/shard_map/ppermute | solution.py:1023
  351.3 7.0 %collective-permute-done.32 = bf16[56,2304]{1,0:T(8,128)(2,1)S(1)} collective-permute-done((bf16[56,2304]{1,0:T(8,128)(2,1)S(1)}, bf16[56,2304]{1,0:T(8,128)(2,1)S(1)}, u32[]{:S(2)}, u32[]{:S(2)}) %collective-permute-start.32) | collective-permute-done | bytes 258080 | tf_op jit(solution)/shard_map/ppermute | solution.py:1023
  362.5 4.8 %collective-permute-done.33 = bf16[432,768]{1,0:T(8,128)(2,1)S(1)} collective-permute-done((bf16[432,768]{1,0:T(8,128)(2,1)S(1)}, bf16[432,768]{1,0:T(8,128)(2,1)S(1)}, u32[]{:S(2)}, u32[]{:S(2)}) %collective-permute-start.33) | collective-permute-done | bytes 663584 | tf_op jit(solution)/shard_map/ppermute | solution.py:1023
  (209 shorter events, 88.0 us)
Async XLA Ops:
  7.2 111.8 %all-gather.3.cloned.1.call-start = ((), (), s32[]{:S(2)}) async-start(), calls=%async_computation.2 | async-start | bytes 11943936 | tf_op jit(solution)/shard_map/all_gather | solution.py:1130
  7.2 37.4 %collective-permute-start.4 = (bf16[96,2304]{1,0:T(8,128)(2,1)}, bf16[96,2304]{1,0:T(8,128)(2,1)}, u32[]{:S(2)}, u32[]{:S(2)}) collective-permute-start(bf16[96,2304]{1,0:T(8,128)(2,1)} %rest_0_), channel_id=1, source_target_pairs={{0,8},{4,12},{8,0},{12,4},{16,24},{20,28},{24,16},{28,20},{1,9},{5... | collective-permute-start | bytes 1327112 | tf_op jit(solution)/shard_map/ppermute | solution.py:1023
  10.2 34.9 %collective-permute-start.5 = (bf16[96,2304]{1,0:T(8,128)(2,1)}, bf16[96,2304]{1,0:T(8,128)(2,1)}, u32[]{:S(2)}, u32[]{:S(2)}) collective-permute-start(bf16[96,2304]{1,0:T(8,128)(2,1)} %rest_0_), channel_id=1, source_target_pairs={{0,16},{4,20},{8,24},{12,28},{16,0},{20,4},{24,8},{28,12},{1,17},{... | collective-permute-start | bytes 1327112 | tf_op jit(solution)/shard_map/ppermute | solution.py:1023
  11.8 33.4 %collective-permute-start.6 = (bf16[96,2304]{1,0:T(8,128)(2,1)}, bf16[96,2304]{1,0:T(8,128)(2,1)}, u32[]{:S(2)}, u32[]{:S(2)}) collective-permute-start(bf16[96,2304]{1,0:T(8,128)(2,1)} %rest_0_), channel_id=1, source_target_pairs={{0,24},{4,28},{8,16},{12,20},{16,8},{20,12},{24,0},{28,4},{1,25},{... | collective-permute-start | bytes 1327112 | tf_op jit(solution)/shard_map/ppermute | solution.py:1023
  24.3 7.9 %collective-permute-start.11 = (bf16[8,1408]{1,0:T(8,128)(2,1)S(1)}, bf16[8,1408]{1,0:T(8,128)(2,1)S(1)}, u32[]{:S(2)}, u32[]{:S(2)}) collective-permute-start(bf16[8,1408]{1,0:T(8,128)(2,1)S(1)} %broadcast_select_fusion), channel_id=1, source_target_pairs={{0,4},{4,0},{8,12},{12,8},{16,20},{20,16},{24,28},{28,24},{1,5},{5... | collective-permute-start | bytes 67592 | tf_op jit(solution)/shard_map/ppermute | solution.py:1023
  34.2 18.1 %collective-permute-start.17 = (bf16[512,768]{1,0:T(8,128)(2,1)S(1)}, bf16[512,768]{1,0:T(8,128)(2,1)}, u32[]{:S(2)}, u32[]{:S(2)}) collective-permute-start(bf16[512,768]{1,0:T(8,128)(2,1)S(1)} %get-tuple-element.148), channel_id=1, source_target_pairs={{0,1},{1,2},{2,3},{4,5},{5,6},{6,7},{8,9},{9,10},{10,11},{12,13},{... | collective-permute-start | bytes 2359304 | tf_op jit(solution)/shard_map/ppermute | solution.py:1028
  44.6 7.7 %collective-permute-start.8 = (bf16[96,2304]{1,0:T(8,128)(2,1)}, bf16[96,2304]{1,0:T(8,128)(2,1)}, u32[]{:S(2)}, u32[]{:S(2)}) collective-permute-start(bf16[96,2304]{1,0:T(8,128)(2,1)} %collective-permute-done.4.rest_1_), channel_id=1, source_target_pairs={{0,4},{4,0},{8,12},{12,8},{16,20},{20,16},{24,28},{28,24},{1,5},{5... | collective-permute-start | bytes 1327112 | tf_op jit(solution)/shard_map/ppermute | solution.py:1023
  52.4 216.8 %reduce-scatter.2.cloned.1.call-start = ((), (), s32[]{:S(2)}) async-start(), calls=%async_computation.1 | async-start | bytes 11943936 | tf_op jit(solution)/shard_map/reduce_scatter | solution.py:1307
  54.2 23.9 %collective-permute-start.19 = (bf16[512,768]{1,0:T(8,128)(2,1)}, bf16[512,768]{1,0:T(8,128)(2,1)S(1)}, u32[]{:S(2)}, u32[]{:S(2)}) collective-permute-start(bf16[512,768]{1,0:T(8,128)(2,1)} %get-tuple-element.152), channel_id=1, source_target_pairs={{0,1},{1,2},{2,3},{4,5},{5,6},{6,7},{8,9},{9,10},{10,11},{12,13},{... | collective-permute-start | bytes 2359304 | tf_op jit(solution)/shard_map/ppermute | solution.py:1028
  59.1 23.8 %collective-permute-start.18 = (bf16[2,128,768]{2,1,0:T(8,128)(2,1)}, bf16[2,128,768]{2,1,0:T(8,128)(2,1)S(1)}, u32[]{:S(2)}, u32[]{:S(2)}) collective-permute-start(bf16[2,128,768]{2,1,0:T(8,128)(2,1)} %slice.213), channel_id=1, source_target_pairs={{0,2},{1,3},{4,6},{5,7},{8,10},{9,11},{12,14},{13,15},{16,18},{17,... | collective-permute-start | bytes 1179656 | tf_op jit(solution)/shard_map/ppermute | solution.py:1028
  210.8 42.4 %collective-permute-start.20 = (bf16[2,192,768]{2,1,0:T(8,128)(2,1)}, bf16[2,192,768]{2,1,0:T(8,128)(2,1)S(1)}, u32[]{:S(2)}, u32[]{:S(2)}) collective-permute-start(bf16[2,192,768]{2,1,0:T(8,128)(2,1)} %get-tuple-element.229), channel_id=1, source_target_pairs={{1,0},{2,1},{3,2},{5,4},{6,5},{7,6},{9,8},{10,9},{11,10},{13,12},{... | collective-permute-start | bytes 1769480 | tf_op jit(solution)/shard_map/ppermute | solution.py:1028
  212.1 41.1 %collective-permute-start.21 = (bf16[2,128,768]{2,1,0:T(8,128)(2,1)S(1)}, bf16[2,128,768]{2,1,0:T(8,128)(2,1)}, u32[]{:S(2)}, u32[]{:S(2)}) collective-permute-start(bf16[2,128,768]{2,1,0:T(8,128)(2,1)S(1)} %slice.238), channel_id=1, source_target_pairs={{1,0},{2,1},{3,2},{5,4},{6,5},{7,6},{9,8},{10,9},{11,10},{13,12},{... | collective-permute-start | bytes 1179656 | tf_op jit(solution)/shard_map/ppermute | solution.py:1028
  256.4 16.2 %collective-permute-start.22 = (bf16[4,112,2304]{2,1,0:T(8,128)(2,1)}, bf16[4,112,2304]{2,1,0:T(8,128)(2,1)S(1)}, u32[]{:S(2)}, u32[]{:S(2)}) collective-permute-start(bf16[4,112,2304]{2,1,0:T(8,128)(2,1)} %get-tuple-element.247), channel_id=1, source_target_pairs={{0,4},{4,0},{8,12},{12,8},{16,20},{20,16},{24,28},{28,24},{1,5},{5... | collective-permute-start | bytes 6193160 | tf_op jit(solution)/shard_map/ppermute | solution.py:1023
  256.4 20.9 %collective-permute-start.27 = (bf16[2,192,768]{2,1,0:T(8,128)(2,1)S(1)}, bf16[2,192,768]{2,1,0:T(8,128)(2,1)S(1)}, u32[]{:S(2)}, u32[]{:S(2)}) collective-permute-start(bf16[2,192,768]{2,1,0:T(8,128)(2,1)S(1)} %get-tuple-element.228), channel_id=1, source_target_pairs={{1,0},{2,1},{3,2},{5,4},{6,5},{7,6},{9,8},{10,9},{11,10},{13,12},{... | collective-permute-start | bytes 1769480 | tf_op jit(solution)/shard_map/ppermute | solution.py:1028
  259.7 23.3 %collective-permute-start.28 = (bf16[2,128,768]{2,1,0:T(8,128)(2,1)}, bf16[2,128,768]{2,1,0:T(8,128)(2,1)}, u32[]{:S(2)}, u32[]{:S(2)}) collective-permute-start(bf16[2,128,768]{2,1,0:T(8,128)(2,1)} %add_convert_fusion.6), channel_id=1, source_target_pairs={{1,0},{2,1},{3,2},{5,4},{6,5},{7,6},{9,8},{10,9},{11,10},{13,12},{... | collective-permute-start | bytes 1179656 | tf_op jit(solution)/shard_map/ppermute | solution.py:1028
  271.1 25.7 %collective-permute-start.26 = (bf16[432,768]{1,0:T(8,128)(2,1)}, bf16[432,768]{1,0:T(8,128)(2,1)}, u32[]{:S(2)}, u32[]{:S(2)}) collective-permute-start(bf16[432,768]{1,0:T(8,128)(2,1)} %dynamic-slice_bitcast_fusion), channel_id=1, source_target_pairs={{0,1},{1,0},{2,3},{3,2},{4,5},{5,4},{6,7},{7,6},{8,9},{9,8},{10,11... | collective-permute-start | bytes 1990664 | tf_op jit(solution)/shard_map/ppermute | solution.py:1023
  275.3 22.8 %collective-permute-start.23 = (bf16[112,2304]{1,0:T(8,128)(2,1)}, bf16[112,2304]{1,0:T(8,128)(2,1)}, u32[]{:S(2)}, u32[]{:S(2)}) collective-permute-start(bf16[112,2304]{1,0:T(8,128)(2,1)} %get-tuple-element.232), channel_id=1, source_target_pairs={{0,8},{4,12},{8,0},{12,4},{16,24},{20,28},{24,16},{28,20},{1,9},{5... | collective-permute-start | bytes 1548296 | tf_op jit(solution)/shard_map/ppermute | solution.py:1023
  276.7 24.3 %collective-permute-start.24 = (bf16[112,2304]{1,0:T(8,128)(2,1)}, bf16[112,2304]{1,0:T(8,128)(2,1)}, u32[]{:S(2)}, u32[]{:S(2)}) collective-permute-start(bf16[112,2304]{1,0:T(8,128)(2,1)} %get-tuple-element.231), channel_id=1, source_target_pairs={{0,16},{4,20},{8,24},{12,28},{16,0},{20,4},{24,8},{28,12},{1,17},{... | collective-permute-start | bytes 1548296 | tf_op jit(solution)/shard_map/ppermute | solution.py:1023
  277.3 23.6 %collective-permute-start.25 = (bf16[112,2304]{1,0:T(8,128)(2,1)}, bf16[112,2304]{1,0:T(8,128)(2,1)}, u32[]{:S(2)}, u32[]{:S(2)}) collective-permute-start(bf16[112,2304]{1,0:T(8,128)(2,1)} %get-tuple-element.230), channel_id=1, source_target_pairs={{0,24},{4,28},{8,16},{12,20},{16,8},{20,12},{24,0},{28,4},{1,25},{... | collective-permute-start | bytes 1548296 | tf_op jit(solution)/shard_map/ppermute | solution.py:1023
  302.8 12.5 %collective-permute-start.29 = (bf16[56,2304]{1,0:T(8,128)(2,1)S(1)}, bf16[56,2304]{1,0:T(8,128)(2,1)S(1)}, u32[]{:S(2)}, u32[]{:S(2)}) collective-permute-start(bf16[56,2304]{1,0:T(8,128)(2,1)S(1)} %dynamic-slice_bitcast_fusion.1), channel_id=1, source_target_pairs={{0,1},{1,0},{2,3},{3,2},{4,5},{5,4},{6,7},{7,6},{8,9},{9,8},{10,11... | collective-permute-start | bytes 774152 | tf_op jit(solution)/shard_map/ppermute | solution.py:1023
  303.4 32.7 %collective-permute-start.30 = (bf16[432,768]{1,0:T(8,128)(2,1)S(1)}, bf16[432,768]{1,0:T(8,128)(2,1)S(1)}, u32[]{:S(2)}, u32[]{:S(2)}) collective-permute-start(bf16[432,768]{1,0:T(8,128)(2,1)S(1)} %fusion.2), channel_id=1, source_target_pairs={{0,2},{1,3},{2,0},{3,1},{4,6},{5,7},{6,4},{7,5},{8,10},{9,11},{10,... | collective-permute-start | bytes 1990664 | tf_op jit(solution)/shard_map/ppermute | solution.py:1023
  336.3 10.3 %collective-permute-start.31 = (bf16[56,2304]{1,0:T(8,128)(2,1)S(1)}, bf16[56,2304]{1,0:T(8,128)(2,1)S(1)}, u32[]{:S(2)}, u32[]{:S(2)}) collective-permute-start(bf16[56,2304]{1,0:T(8,128)(2,1)S(1)} %fusion.11), channel_id=1, source_target_pairs={{0,2},{1,3},{2,0},{3,1},{4,6},{5,7},{6,4},{7,5},{8,10},{9,11},{10,... | collective-permute-start | bytes 774152 | tf_op jit(solution)/shard_map/ppermute | solution.py:1023
  346.7 11.7 %collective-permute-start.32 = (bf16[56,2304]{1,0:T(8,128)(2,1)S(1)}, bf16[56,2304]{1,0:T(8,128)(2,1)S(1)}, u32[]{:S(2)}, u32[]{:S(2)}) collective-permute-start(bf16[56,2304]{1,0:T(8,128)(2,1)S(1)} %add_convert_fusion.7), channel_id=1, source_target_pairs={{0,1},{1,0},{2,3},{3,2},{4,5},{5,4},{6,7},{7,6},{8,9},{9,8},{10,11... | collective-permute-start | bytes 774152 | tf_op jit(solution)/shard_map/ppermute | solution.py:1023
  351.2 16.0 %collective-permute-start.33 = (bf16[432,768]{1,0:T(8,128)(2,1)S(1)}, bf16[432,768]{1,0:T(8,128)(2,1)S(1)}, u32[]{:S(2)}, u32[]{:S(2)}) collective-permute-start(bf16[432,768]{1,0:T(8,128)(2,1)S(1)} %add_convert_fusion.1), channel_id=1, source_target_pairs={{0,1},{1,0},{2,3},{3,2},{4,5},{5,4},{6,7},{7,6},{8,9},{9,8},{10,11... | collective-permute-start | bytes 1990664 | tf_op jit(solution)/shard_map/ppermute | solution.py:1023
  (28 other events, 257.2 us)
Sparse Core Ops, SparseCore 0:
  52.5 66.4 all-gather.2
  174.8 94.3 reduce-scatter.1

commit v6 on v5

--- a/solution.py
+++ b/solution.py
@@ -1145,7 +1145,7 @@
         return at(0, 1), jnp.concatenate(ups, -1), at(1 + cuts, 1 + 2 * cuts)
 
     if owners == SHARES:
-        return part(slab.astype(F32), 0)
+        return [g.astype(F32) for g in part(slab, 0)]
     return [
         lax.psum(
             lax.psum_scatter(
@@ -1237,6 +1237,7 @@
     )
     table = sum_over(table, "fsdp")
 
+    qkv_pieces, near[0] = lax.optimization_barrier((qkv_pieces, near[0]))
     qkv_pieces = gather_rest(qkv_pieces)
     slab, qkv_pieces, table, facts, near[0] = gather_slab(
         outweight, fcweight, projweight, qkv_pieces, table, facts, near[0]
@@ -1250,6 +1251,7 @@
         size = shard.shape[0]
         vectors.append(table[:, at : at + size].reshape(1, size * owners).astype(F32))
         at += size + -size % 128
+    vectors, held = lax.optimization_barrier((vectors, order))
     gain1, shift1, bias1, outbias_v, gain2, shift2, upbias, downbias = vectors
 
 
@@ -1263,13 +1265,15 @@
 
     bias1 = jnp.concatenate([bias1[:, :width], jnp.zeros((1, width), F32), bias1[:, width:]], 1)
     normed, query, keyvalues, qkv = project_own(
-        order, tokens, gain1, shift1, bias1, qkv_pieces, halo_rows + block
-    )
-    near[-1], query = lax.optimization_barrier((near[-1], query))
-    halo = jnp.stack(near)
+        held, tokens, gain1, shift1, bias1, qkv_pieces, halo_rows + block
+    )
+    halo = jnp.zeros((seqs, halo_rows, width), BF16)
+    for k in range(seqs):
+        if k == seqs - 1:
+            halo, near[k], query = lax.optimization_barrier((halo, near[k], query))
+        halo = lax.dynamic_update_slice(halo, near[k][None], (k, far_rows, 0))
     if far_rows > 0:
-        blank = jnp.zeros((seqs, far_rows - HALO_CHUNK, width), BF16)
-        halo = jnp.concatenate([blank, far, halo], 1)
+        halo = lax.dynamic_update_slice(halo, far, (0, far_rows - HALO_CHUNK, 0))
 
     def fetch(state):
         j, halo = state
@@ -1372,7 +1376,6 @@
         joint = joint[:, :share].reshape(width, 3 * width)
         joint = lax.psum_scatter(joint, "fsdp", scatter_dimension=0, tiled=True)
         joint = lax.psum(joint, "seq")
-    joint = joint.astype(F32)
     grad_merge, grad_up, grad_down = reduce_slab(outer, width, hidden)
 
     share = width // owners
@@ -1381,8 +1384,9 @@
     spots = [(0, wide), (wide, wide), (2 * wide, 2 * wide), (width, at)]
     spots += [(width + at + k * wide, wide) for k in range(4)]
     if owners == SHARES:
-        cuts = [joint[share, start : start + size] for start, size in spots]
-        loss_row = joint[share, 2 * width :]
+        tail = joint[share].astype(F32)
+        cuts = [tail[start : start + size] for start, size in spots]
+        loss_row = tail[2 * width :]
     else:
         full = [small_late[:, start : start + size].reshape(-1) for start, size in spots]
         cuts = [
@@ -1397,7 +1401,7 @@
         grad_tokens,
         cuts[0],
         cuts[1],
-        joint[:share],
+        joint[:share].astype(F32),
         cuts[2],
         grad_merge,
         cuts[4],

time: 385 us -> 388 us (level)
  waiting for transfers between devices: 118 us -> 129 us
  starting transfers between devices: 48.3 us -> 41.8 us
    ppermute x25, waiting for transfers between devices: 69.3 us -> 89.2 us  [swap(): return lax.ppermute(x, axis, [(i, i ^ bit) for i in range(size)])]
    ppermute x7, waiting for transfers between devices: 32.2 us -> 16.8 us  [shift(): lax.ppermute(x, axis, [(i, i + step) for i in range(size) if 0 <= i + ste...]
    reduce_scatter x1, waiting for transfers between devices: 7.9 us -> 15 us  [local(): outer = lax.psum_scatter(outer, 'fsdp', scatter_dimension=0, tiled=False)]
    concatenate x2 -> x0, other arithmetic: 4.62 us -> none  [the longest x1 3.49 us: local(): halo = jnp.concatenate([blank, far, halo], 1)]
  transfers between devices with their start and end apart: 34 -> 34, of which waited for: 19 -> 18; matrix products, arithmetic and copies ran while one was open for 11% -> 11% of each run, Pallas kernels for 23% -> 23%
where the time goes in v6:
time: 388 us; the launch traced here: 384 us
  Pallas kernels  144 us (37%)
  waiting for transfers between devices  129 us (33%)
  starting transfers between devices  41.8 us (11%)
  local copies, waits for them, and re-layouts  28.8 us (7%)
  other arithmetic  21.1 us (5%)
  between operations  18.6 us (5%)
    ppermute x25, waiting for transfers between devices, swap(): return lax.ppermute(x, axis, [(i, i ^ bit) for i in range(size)])  89.2 us
    pallas_call x1, Pallas kernels, mlp(): pl.pallas_call(mlp_kernel, grid=(rows // MLP_TILE,), in_specs=[pl.BlockSp...  55.6 us
    ppermute x25, starting transfers between devices, swap(): return lax.ppermute(x, axis, [(i, i ^ bit) for i in range(size)])  27.5 us
    pallas_call x1, Pallas kernels, attend_back(): pl.pallas_call(functools.partial(attend_back_kernel, length - block), gri...  27.2 us
    pallas_call x1, Pallas kernels, attend(): pl.pallas_call(functools.partial(attend_kernel, length - block), grid_spe...  19.4 us
    ppermute x7, waiting for transfers between devices, shift(): lax.ppermute(x, axis, [(i, i + step) for i in range(size) if 0 <= i + ste...  16.8 us
    pallas_call x1, Pallas kernels, own_back(): pl.pallas_call(own_back_kernel, grid_spec=pltpu.PrefetchScalarGridSpec(nu...  16.2 us
    reduce_scatter x1, waiting for transfers between devices, local(): outer = lax.psum_scatter(outer, 'fsdp', scatter_dimension=0, tiled=False)  15 us
  transfers between devices with their start and end apart: 34, of which 18 were waited for; matrix products, arithmetic and copies ran while one was open for 11% of the time, Pallas kernels for 23%

profile of v6, /device:TPU:0, one launch (start us, length us, event | category | flops | bytes accessed | tf_op | source)
XLA Modules:
  0.0 384.2 jit_solution(6355110383811869552)
XLA Ops:
  7.2 3.0 collective-permute-start.4
  26.4 3.2 collective-permute-start.7
  35.6 10.4 %collective-permute-done.16 = s32[2]{0:T(128)S(1)} collective-permute-done((s32[2]{0:T(128)S(1)}, s32[2]{0:T(128)S(1)}, u32[]{:S(2)}, u32[]{:S(2)}) %collective-permute-start.16) | collective-permute-done | bytes 40 | tf_op jit(solution)/shard_map/ppermute | solution.py:1023
  59.7 3.8 collective-permute-start.18
  72.7 10.5 %project_own.1 = (bf16[2,2048,768]{2,1,0:T(8,128)(2,1)}, bf16[2,512,768]{2,1,0:T(8,128)(2,1)}, bf16[2,2048,1536]{2,1,0:T(8,128)(2,1)}, bf16[768,2304]{1,0:T(8,128)(2,1)}) custom-call(s32[8]{0:T(128)} %stack.68.order_ref, bf16[2,512,768]{2,1,0:T(8,128)(2,1)} %own_ref.3, f32[1,768]{1,0:T(1,128)} %reshape.489.gain_ref, f32[1,768]{1,0:T(1,128)} %reshape.490.shift_ref, ...), custom_call_target="tpu_custom_call" | custom-call | flops 3623878656 | bytes 16777216 | tf_op jit(solution)/shard_map/project_own/pallas_call | solution.py:95
  86.0 2.8 copy-done
  89.5 3.4 project_halo.1
  92.8 19.4 %attend.1 = (bf16[2,512,768]{2,1,0:T(8,128)(2,1)}, f32[2,6,2,512]{3,2,1,0:T(2,128)}) custom-call(s32[8]{0:T(128)} %reshape.479.low_ref, bf16[2,512,768]{2,1,0:T(8,128)(2,1)} %get-tuple-element.194.query_ref, bf16[2,2048,1536]{2,1,0:T(8,128)(2,1)} %get-tuple-element.195.keyvalue_ref, s32[2,1,512]{2,1,0:T(1,128)} %fusion.23.start_ref), custom_call_target="tpu_custom_call" | custom-call | flops 17179869184 | bytes 16777216 | tf_op jit(solution)/shard_map/attend/pallas_call | solution.py:332
  112.3 7.6 %all-gather.3.cloned.1.call-done = bf16[6912,768]{1,0:T(8,128)(2,1)} async-done(((bf16[864,768]{1,0:T(8,128)(2,1)}), bf16[6912,768]{1,0:T(8,128)(2,1)}) %all-gather.3.cloned.1.call-update) | async-done | bytes 10616848 | tf_op jit(solution)/shard_map/all_gather | solution.py:1130
  119.9 55.6 %mlp.1 = (bf16[1024,768]{1,0:T(8,128)(2,1)}, f32[1024,768]{1,0:T(8,128)}, bf16[1024,768]{1,0:T(8,128)(2,1)}, f32[8,768]{1,0:T(8,128)}, f32[8,3072]{1,0:T(8,128)}, /*index=5*/bf16[8,864,768]{2,1,0:T(8,128)(2,1)}) custom-call(f32[1]{0:T(128)S(6)} %div.44.factor_ref, bf16[1024,768]{1,0:T(8,128)(2,1)} %bitcast.113, bf16[1024,768]{1,0:T(8,128)(2,1)} %bitcast.94, ...), custom_call_target="tpu_custom_call" | custom-call | flops 32614907904 | bytes 41943040 | tf_op jit(solution)/shard_map/mlp/pallas_call | solution.py:671
  175.6 27.2 %attend_back.1 = (bf16[2,512,768]{2,1,0:T(8,128)(2,1)}, bf16[2,2048,1536]{2,1,0:T(8,128)(2,1)}) custom-call(s32[8]{0:T(128)} %reshape.479.low_ref, s32[2]{0:T(128)} %get-tuple-element.256.first_ref, bf16[2,512,768]{2,1,0:T(8,128)(2,1)} %get-tuple-element.194.query_ref, bf16[2,2048,1536]{2,1,0:T(8,128)(2,1)} %get-tuple-element.195.keyvalue_ref, ...), custom_call_target="tpu_custom_call" | custom-call | flops 42949672960 | bytes 29360128 | tf_op jit(solution)/shard_map/attend_back/pallas_call | solution.py:442
  202.8 5.2 %halo_back.1 = (bf16[2,1536,768]{2,1,0:T(8,128)(2,1)}, f32[8,768]{1,0:T(8,128)}) custom-call(s32[2]{0:T(128)} %get-tuple-element.257.low_ref, bf16[2,1536,768]{2,1,0:T(8,128)(2,1)} %get-tuple-element.189.halo_any, bf16[2,2048,1536]{2,1,0:T(8,128)(2,1)} %get-tuple-element.207.grad_any.gkeyvalue_any, bf16[768,2304]{1,0:T(8,128)(2,1)} %get-tuple-element.190.whole_any), custom_call_target="tpu_custom_call" | custom-call | flops 4294967296 | bytes 16777216 | tf_op jit(solution)/shard_map/halo_back/pallas_call | solution.py:800
  214.4 16.2 %own_back.1 = (f32[2,512,768]{2,1,0:T(8,128)}, bf16[4,112,2304]{2,1,0:T(8,128)(2,1)}, bf16[4,112,2304]{2,1,0:T(8,128)(2,1)}, f32[8,768]{1,0:T(8,128)}) custom-call(s32[2]{0:T(128)} %get-tuple-element.257.low_ref, s32[8]{0:T(128)} %stack.68.order_ref, bf16[2,512,768]{2,1,0:T(8,128)(2,1)} %own_ref.3, bf16[2,2048,768]{2,1,0:T(8,128)(2,1)} %get-tuple-element.193.normed_any, ...), custom_call_target="tpu_custom_call" | custom-call | flops 17179869184 | bytes 25165824 | tf_op jit(solution)/shard_map/own_back/pallas_call | solution.py:942
  232.0 15.5 %collective-permute-done.21 = bf16[2,128,768]{2,1,0:T(8,128)(2,1)} collective-permute-done((bf16[2,128,768]{2,1,0:T(8,128)(2,1)S(1)}, bf16[2,128,768]{2,1,0:T(8,128)(2,1)}, u32[]{:S(2)}, u32[]{:S(2)}) %collective-permute-start.21) | collective-permute-done | bytes 393248 | tf_op jit(solution)/shard_map/ppermute | solution.py:1028
  255.7 15.0 %reduce-scatter.2.cloned.1.call-done = bf16[1,864,768]{2,1,0:T(8,128)(2,1)} async-done(((bf16[8,864,768]{2,1,0:T(8,128)(2,1)}), bf16[1,864,768]{2,1,0:T(8,128)(2,1)}) %reduce-scatter.2.cloned.1.call-update) | async-done | bytes 1327120 | tf_op jit(solution)/shard_map/reduce_scatter | solution.py:1311
  281.7 6.5 %finish.1 = bf16[2,512,768]{2,1,0:T(8,128)(2,1)} custom-call(bf16[2,512,768]{2,1,0:T(8,128)(2,1)} %own_ref.3, f32[2,512,768]{2,1,0:T(8,128)} %get-tuple-element.224.gnormed_ref, f32[2,512,768]{2,1,0:T(8,128)} %bitcast.95, f32[1,768]{1,0:T(1,128)} %reshape.489.gain_ref, bf16[2,192,768]{2,1,0:T(8,128)(2,1)} %copy-done.3, bf16[2,192,768]{2,1,0:T(8,128)(2,1)} %copy-done.4, ...), custom_call_target="tpu_custom_call" | custom-call | flops 15728640 | bytes 11010048 | tf_op jit(solution)/shard_map/finish/pallas_call | solution.py:1004
  288.2 7.5 %collective-permute-done.26 = bf16[432,768]{1,0:T(8,128)(2,1)} collective-permute-done((bf16[432,768]{1,0:T(8,128)(2,1)}, bf16[432,768]{1,0:T(8,128)(2,1)}, u32[]{:S(2)}, u32[]{:S(2)}) %collective-permute-start.26) | collective-permute-done | bytes 663584 | tf_op jit(solution)/shard_map/ppermute | solution.py:1023
  297.0 5.5 %collective-permute-done.24 = bf16[112,2304]{1,0:T(8,128)(2,1)} collective-permute-done((bf16[112,2304]{1,0:T(8,128)(2,1)}, bf16[112,2304]{1,0:T(8,128)(2,1)}, u32[]{:S(2)}, u32[]{:S(2)}) %collective-permute-start.24) | collective-permute-done | bytes 516128 | tf_op jit(solution)/shard_map/ppermute | solution.py:1023
  304.9 4.7 %collective-permute-start.30 = (bf16[432,768]{1,0:T(8,128)(2,1)S(1)}, bf16[432,768]{1,0:T(8,128)(2,1)S(1)}, u32[]{:S(2)}, u32[]{:S(2)}) collective-permute-start(bf16[432,768]{1,0:T(8,128)(2,1)S(1)} %fusion.1), channel_id=1, source_target_pairs={{0,2},{1,3},{2,0},{3,1},{4,6},{5,7},{6,4},{7,5},{8,10},{9,11},{10,... | collective-permute-start | bytes 1990664 | tf_op jit(solution)/shard_map/ppermute | solution.py:1023
  309.6 7.1 %collective-permute-done.29 = bf16[56,2304]{1,0:T(8,128)(2,1)S(1)} collective-permute-done((bf16[56,2304]{1,0:T(8,128)(2,1)S(1)}, bf16[56,2304]{1,0:T(8,128)(2,1)S(1)}, u32[]{:S(2)}, u32[]{:S(2)}) %collective-permute-start.29) | collective-permute-done | bytes 258080 | tf_op jit(solution)/shard_map/ppermute | solution.py:1023
  316.8 21.7 %collective-permute-done.30 = bf16[432,768]{1,0:T(8,128)(2,1)S(1)} collective-permute-done((bf16[432,768]{1,0:T(8,128)(2,1)S(1)}, bf16[432,768]{1,0:T(8,128)(2,1)S(1)}, u32[]{:S(2)}, u32[]{:S(2)}) %collective-permute-start.30) | collective-permute-done | bytes 663584 | tf_op jit(solution)/shard_map/ppermute | solution.py:1023
  338.7 13.4 %collective-permute-done.31 = bf16[56,2304]{1,0:T(8,128)(2,1)S(1)} collective-permute-done((bf16[56,2304]{1,0:T(8,128)(2,1)S(1)}, bf16[56,2304]{1,0:T(8,128)(2,1)S(1)}, u32[]{:S(2)}, u32[]{:S(2)}) %collective-permute-start.31) | collective-permute-done | bytes 258080 | tf_op jit(solution)/shard_map/ppermute | solution.py:1023
  354.3 7.1 %collective-permute-done.32 = bf16[56,2304]{1,0:T(8,128)(2,1)S(1)} collective-permute-done((bf16[56,2304]{1,0:T(8,128)(2,1)S(1)}, bf16[56,2304]{1,0:T(8,128)(2,1)S(1)}, u32[]{:S(2)}, u32[]{:S(2)}) %collective-permute-start.32) | collective-permute-done | bytes 258080 | tf_op jit(solution)/shard_map/ppermute | solution.py:1023
  365.6 7.1 %collective-permute-done.33 = bf16[432,768]{1,0:T(8,128)(2,1)S(1)} collective-permute-done((bf16[432,768]{1,0:T(8,128)(2,1)S(1)}, bf16[432,768]{1,0:T(8,128)(2,1)S(1)}, u32[]{:S(2)}, u32[]{:S(2)}) %collective-permute-start.33) | collective-permute-done | bytes 663584 | tf_op jit(solution)/shard_map/ppermute | solution.py:1023
  (218 shorter events, 86.2 us)
Async XLA Ops:
  7.2 112.7 %all-gather.3.cloned.1.call-start = ((), (), s32[]{:S(2)}) async-start(), calls=%async_computation.2 | async-start | bytes 11943936 | tf_op jit(solution)/shard_map/all_gather | solution.py:1130
  7.2 39.1 %collective-permute-start.4 = (bf16[96,2304]{1,0:T(8,128)(2,1)}, bf16[96,2304]{1,0:T(8,128)(2,1)}, u32[]{:S(2)}, u32[]{:S(2)}) collective-permute-start(bf16[96,2304]{1,0:T(8,128)(2,1)} %rest_0_), channel_id=1, source_target_pairs={{0,8},{4,12},{8,0},{12,4},{16,24},{20,28},{24,16},{28,20},{1,9},{5... | collective-permute-start | bytes 1327112 | tf_op jit(solution)/shard_map/ppermute | solution.py:1023
  10.2 36.1 %collective-permute-start.5 = (bf16[96,2304]{1,0:T(8,128)(2,1)}, bf16[96,2304]{1,0:T(8,128)(2,1)}, u32[]{:S(2)}, u32[]{:S(2)}) collective-permute-start(bf16[96,2304]{1,0:T(8,128)(2,1)} %rest_0_), channel_id=1, source_target_pairs={{0,16},{4,20},{8,24},{12,28},{16,0},{20,4},{24,8},{28,12},{1,17},{... | collective-permute-start | bytes 1327112 | tf_op jit(solution)/shard_map/ppermute | solution.py:1023
  26.4 20.6 %collective-permute-start.7 = (bf16[512,768]{1,0:T(8,128)(2,1)S(1)}, bf16[512,768]{1,0:T(8,128)(2,1)}, u32[]{:S(2)}, u32[]{:S(2)}) collective-permute-start(bf16[512,768]{1,0:T(8,128)(2,1)S(1)} %get-tuple-element.155), channel_id=1, source_target_pairs={{0,1},{1,2},{2,3},{4,5},{5,6},{6,7},{8,9},{9,10},{10,11},{12,13},{... | collective-permute-start | bytes 2359304 | tf_op jit(solution)/shard_map/ppermute | solution.py:1028
  33.6 13.4 %collective-permute-start.6 = (bf16[96,2304]{1,0:T(8,128)(2,1)}, bf16[96,2304]{1,0:T(8,128)(2,1)S(1)}, u32[]{:S(2)}, u32[]{:S(2)}) collective-permute-start(bf16[96,2304]{1,0:T(8,128)(2,1)} %rest_0_), channel_id=1, source_target_pairs={{0,24},{4,28},{8,16},{12,20},{16,8},{20,12},{24,0},{28,4},{1,25},{... | collective-permute-start | bytes 1327112 | tf_op jit(solution)/shard_map/ppermute | solution.py:1023
  33.8 12.2 %collective-permute-start.16 = (s32[2]{0:T(128)S(1)}, s32[2]{0:T(128)S(1)}, u32[]{:S(2)}, u32[]{:S(2)}) collective-permute-start(s32[2]{0:T(128)S(1)} %add_select_fusion.2), channel_id=1, source_target_pairs={{0,8},{4,12},{8,0},{12,4},{16,24},{20,28},{24,16},{28,20},{1,9},{5... | collective-permute-start | bytes 32 | tf_op jit(solution)/shard_map/ppermute | solution.py:1023
  47.0 10.3 %collective-permute-start.8 = (bf16[96,2304]{1,0:T(8,128)(2,1)}, bf16[96,2304]{1,0:T(8,128)(2,1)S(1)}, u32[]{:S(2)}, u32[]{:S(2)}) collective-permute-start(bf16[96,2304]{1,0:T(8,128)(2,1)} %rest_0_), channel_id=1, source_target_pairs={{0,4},{4,0},{8,12},{12,8},{16,20},{20,16},{24,28},{28,24},{1,5},{5... | collective-permute-start | bytes 1327112 | tf_op jit(solution)/shard_map/ppermute | solution.py:1023
  47.0 10.3 %collective-permute-start.9 = (bf16[96,2304]{1,0:T(8,128)(2,1)}, bf16[96,2304]{1,0:T(8,128)(2,1)S(1)}, u32[]{:S(2)}, u32[]{:S(2)}) collective-permute-start(bf16[96,2304]{1,0:T(8,128)(2,1)} %collective-permute-done.4.rest_1_), channel_id=1, source_target_pairs={{0,4},{4,0},{8,12},{12,8},{16,20},{20,16},{24,28},{28,24},{1,5},{5... | collective-permute-start | bytes 1327112 | tf_op jit(solution)/shard_map/ppermute | solution.py:1023
  57.3 213.4 %reduce-scatter.2.cloned.1.call-start = ((), (), s32[]{:S(2)}) async-start(), calls=%async_computation.1 | async-start | bytes 11943936 | tf_op jit(solution)/shard_map/reduce_scatter | solution.py:1311
  59.7 24.9 %collective-permute-start.18 = (bf16[512,768]{1,0:T(8,128)(2,1)}, bf16[512,768]{1,0:T(8,128)(2,1)S(1)}, u32[]{:S(2)}, u32[]{:S(2)}) collective-permute-start(bf16[512,768]{1,0:T(8,128)(2,1)} %get-tuple-element.174), channel_id=1, source_target_pairs={{0,1},{1,2},{2,3},{4,5},{5,6},{6,7},{8,9},{9,10},{10,11},{12,13},{... | collective-permute-start | bytes 2359304 | tf_op jit(solution)/shard_map/ppermute | solution.py:1028
  63.5 22.5 %collective-permute-start.19 = (bf16[2,128,768]{2,1,0:T(8,128)(2,1)}, bf16[2,128,768]{2,1,0:T(8,128)(2,1)S(1)}, u32[]{:S(2)}, u32[]{:S(2)}) collective-permute-start(bf16[2,128,768]{2,1,0:T(8,128)(2,1)} %slice.241), channel_id=1, source_target_pairs={{0,2},{1,3},{4,6},{5,7},{8,10},{9,11},{12,14},{13,15},{16,18},{17,... | collective-permute-start | bytes 1179656 | tf_op jit(solution)/shard_map/ppermute | solution.py:1028
  211.8 35.7 %collective-permute-start.20 = (bf16[2,192,768]{2,1,0:T(8,128)(2,1)}, bf16[2,192,768]{2,1,0:T(8,128)(2,1)S(1)}, u32[]{:S(2)}, u32[]{:S(2)}) collective-permute-start(bf16[2,192,768]{2,1,0:T(8,128)(2,1)} %get-tuple-element.259), channel_id=1, source_target_pairs={{1,0},{2,1},{3,2},{5,4},{6,5},{7,6},{9,8},{10,9},{11,10},{13,12},{... | collective-permute-start | bytes 1769480 | tf_op jit(solution)/shard_map/ppermute | solution.py:1028
  213.1 34.4 %collective-permute-start.21 = (bf16[2,128,768]{2,1,0:T(8,128)(2,1)S(1)}, bf16[2,128,768]{2,1,0:T(8,128)(2,1)}, u32[]{:S(2)}, u32[]{:S(2)}) collective-permute-start(bf16[2,128,768]{2,1,0:T(8,128)(2,1)S(1)} %slice.266), channel_id=1, source_target_pairs={{1,0},{2,1},{3,2},{5,4},{6,5},{7,6},{9,8},{10,9},{11,10},{13,12},{... | collective-permute-start | bytes 1179656 | tf_op jit(solution)/shard_map/ppermute | solution.py:1028
  250.6 23.5 %collective-permute-start.22 = (bf16[4,112,2304]{2,1,0:T(8,128)(2,1)}, bf16[4,112,2304]{2,1,0:T(8,128)(2,1)S(1)}, u32[]{:S(2)}, u32[]{:S(2)}) collective-permute-start(bf16[4,112,2304]{2,1,0:T(8,128)(2,1)} %get-tuple-element.271), channel_id=1, source_target_pairs={{0,4},{4,0},{8,12},{12,8},{16,20},{20,16},{24,28},{28,24},{1,5},{5... | collective-permute-start | bytes 6193160 | tf_op jit(solution)/shard_map/ppermute | solution.py:1023
  250.6 28.2 %collective-permute-start.27 = (bf16[2,192,768]{2,1,0:T(8,128)(2,1)S(1)}, bf16[2,192,768]{2,1,0:T(8,128)(2,1)S(1)}, u32[]{:S(2)}, u32[]{:S(2)}) collective-permute-start(bf16[2,192,768]{2,1,0:T(8,128)(2,1)S(1)} %get-tuple-element.258), channel_id=1, source_target_pairs={{1,0},{2,1},{3,2},{5,4},{6,5},{7,6},{9,8},{10,9},{11,10},{13,12},{... | collective-permute-start | bytes 1769480 | tf_op jit(solution)/shard_map/ppermute | solution.py:1028
  254.1 27.5 %collective-permute-start.28 = (bf16[2,128,768]{2,1,0:T(8,128)(2,1)}, bf16[2,128,768]{2,1,0:T(8,128)(2,1)}, u32[]{:S(2)}, u32[]{:S(2)}) collective-permute-start(bf16[2,128,768]{2,1,0:T(8,128)(2,1)} %add_convert_fusion.6), channel_id=1, source_target_pairs={{1,0},{2,1},{3,2},{5,4},{6,5},{7,6},{9,8},{10,9},{11,10},{13,12},{... | collective-permute-start | bytes 1179656 | tf_op jit(solution)/shard_map/ppermute | solution.py:1028
  272.7 23.0 %collective-permute-start.26 = (bf16[432,768]{1,0:T(8,128)(2,1)}, bf16[432,768]{1,0:T(8,128)(2,1)}, u32[]{:S(2)}, u32[]{:S(2)}) collective-permute-start(bf16[432,768]{1,0:T(8,128)(2,1)} %dynamic-slice_bitcast_fusion), channel_id=1, source_target_pairs={{0,1},{1,0},{2,3},{3,2},{4,5},{5,4},{6,7},{7,6},{8,9},{9,8},{10,11... | collective-permute-start | bytes 1990664 | tf_op jit(solution)/shard_map/ppermute | solution.py:1023
  276.9 20.1 %collective-permute-start.23 = (bf16[112,2304]{1,0:T(8,128)(2,1)}, bf16[112,2304]{1,0:T(8,128)(2,1)}, u32[]{:S(2)}, u32[]{:S(2)}) collective-permute-start(bf16[112,2304]{1,0:T(8,128)(2,1)} %get-tuple-element.262), channel_id=1, source_target_pairs={{0,8},{4,12},{8,0},{12,4},{16,24},{20,28},{24,16},{28,20},{1,9},{5... | collective-permute-start | bytes 1548296 | tf_op jit(solution)/shard_map/ppermute | solution.py:1023
  278.2 24.3 %collective-permute-start.24 = (bf16[112,2304]{1,0:T(8,128)(2,1)}, bf16[112,2304]{1,0:T(8,128)(2,1)}, u32[]{:S(2)}, u32[]{:S(2)}) collective-permute-start(bf16[112,2304]{1,0:T(8,128)(2,1)} %get-tuple-element.261), channel_id=1, source_target_pairs={{0,16},{4,20},{8,24},{12,28},{16,0},{20,4},{24,8},{28,12},{1,17},{... | collective-permute-start | bytes 1548296 | tf_op jit(solution)/shard_map/ppermute | solution.py:1023
  278.9 23.6 %collective-permute-start.25 = (bf16[112,2304]{1,0:T(8,128)(2,1)}, bf16[112,2304]{1,0:T(8,128)(2,1)}, u32[]{:S(2)}, u32[]{:S(2)}) collective-permute-start(bf16[112,2304]{1,0:T(8,128)(2,1)} %get-tuple-element.260), channel_id=1, source_target_pairs={{0,24},{4,28},{8,16},{12,20},{16,8},{20,12},{24,0},{28,4},{1,25},{... | collective-permute-start | bytes 1548296 | tf_op jit(solution)/shard_map/ppermute | solution.py:1023
  304.4 12.3 %collective-permute-start.29 = (bf16[56,2304]{1,0:T(8,128)(2,1)S(1)}, bf16[56,2304]{1,0:T(8,128)(2,1)S(1)}, u32[]{:S(2)}, u32[]{:S(2)}) collective-permute-start(bf16[56,2304]{1,0:T(8,128)(2,1)S(1)} %dynamic-slice_bitcast_fusion.1), channel_id=1, source_target_pairs={{0,1},{1,0},{2,3},{3,2},{4,5},{5,4},{6,7},{7,6},{8,9},{9,8},{10,11... | collective-permute-start | bytes 774152 | tf_op jit(solution)/shard_map/ppermute | solution.py:1023
  304.9 33.5 %collective-permute-start.30 = (bf16[432,768]{1,0:T(8,128)(2,1)S(1)}, bf16[432,768]{1,0:T(8,128)(2,1)S(1)}, u32[]{:S(2)}, u32[]{:S(2)}) collective-permute-start(bf16[432,768]{1,0:T(8,128)(2,1)S(1)} %fusion.1), channel_id=1, source_target_pairs={{0,2},{1,3},{2,0},{3,1},{4,6},{5,7},{6,4},{7,5},{8,10},{9,11},{10,... | collective-permute-start | bytes 1990664 | tf_op jit(solution)/shard_map/ppermute | solution.py:1023
  338.6 13.5 %collective-permute-start.31 = (bf16[56,2304]{1,0:T(8,128)(2,1)S(1)}, bf16[56,2304]{1,0:T(8,128)(2,1)S(1)}, u32[]{:S(2)}, u32[]{:S(2)}) collective-permute-start(bf16[56,2304]{1,0:T(8,128)(2,1)S(1)} %fusion.9), channel_id=1, source_target_pairs={{0,2},{1,3},{2,0},{3,1},{4,6},{5,7},{6,4},{7,5},{8,10},{9,11},{10,... | collective-permute-start | bytes 774152 | tf_op jit(solution)/shard_map/ppermute | solution.py:1023
  352.3 20.4 %collective-permute-start.33 = (bf16[432,768]{1,0:T(8,128)(2,1)S(1)}, bf16[432,768]{1,0:T(8,128)(2,1)S(1)}, u32[]{:S(2)}, u32[]{:S(2)}) collective-permute-start(bf16[432,768]{1,0:T(8,128)(2,1)S(1)} %add_convert_fusion.1), channel_id=1, source_target_pairs={{0,1},{1,0},{2,3},{3,2},{4,5},{5,4},{6,7},{7,6},{8,9},{9,8},{10,11... | collective-permute-start | bytes 1990664 | tf_op jit(solution)/shard_map/ppermute | solution.py:1023
  (32 other events, 302.9 us)
Sparse Core Ops, SparseCore 0:
  57.5 62.3 all-gather.2
  175.6 95.0 reduce-scatter.1
